TPU v7x, 32 devices: a whole 2x2x4 slice. The times are simulated.
32 devices in a mesh: node: 8 (over z, core), local: 4 (over y, x).
Axes of the slice: x: 2, y: 2, z: 4, core: 2. Of those that a mesh axis runs over, the one named last changes fastest.
Arguments:
- images: float32 [256, 7, 7, 512], P(('node', 'local')), may hold values from -11 to 11, as said below
- targets: float32 [256, 7, 7, 512], P(('node', 'local')), may hold values from -6 to 6
- weight: float32 [3, 3, 512, 512], replicated, may hold values from -0.09375 to 0.09375
Outputs:
- combined: float32 [4608, 512], P('local', 'node')
Inputs may be any that keep to these rules, and one draw needn't show every extreme that they name: `images`: entries are real-valued, of order one.
All inputs are finite; a program needn't handle non-finite values.
Results may differ from a plain program's by a relative error of at most 0.00013.
Values sent between devices are 32-bit elements; how exact they have to be, the bound alone decides.
No kernel may reach another device: no remote copies, remote signals or barrier semaphores. Data moves between devices by JAX's collectives and lax.ppermute only.
A program may use at most 128 MiB of HBM per device.

v0:
```python
import jax
import jax.numpy as jnp
from jax import lax
from jax.experimental import pallas as pl
from jax.experimental.pallas import tpu as pltpu
from jax.sharding import PartitionSpec as P


epsilon = 1e-06
HALF = 64
BLK = 32


def partner(value, axis, distance):
    mask = 2**distance
    pairs = [(source, source ^ mask) for source in range(lax.axis_size(axis))]
    return lax.ppermute(value, axis, pairs)


def make_patches(images):
    side = images.shape[1]
    padded = jnp.pad(images, ((0, 0), (1, 1), (1, 1), (0, 0)))
    tap_views = []
    for row_shift in range(3):
        for col_shift in range(3):
            tap_views.append(padded[:, row_shift : row_shift + side, col_shift : col_shift + side, :])
    joined = jnp.concatenate(tap_views, axis=-1)
    return joined.reshape(-1, 9 * images.shape[3])


def adasum_pair(left_vec, right_vec, cross_sum, left_sq, right_sq):
    left_coef = 1.0 - cross_sum / (2.0 * (left_sq + epsilon))
    right_coef = 1.0 - cross_sum / (2.0 * (right_sq + epsilon))
    return left_coef * left_vec + right_coef * right_vec


def general_plan(images, targets, weight):
    channels = images.shape[3]
    flat_w = weight.reshape(9 * channels, channels)
    patches = make_patches(images)
    outputs = jnp.dot(patches, flat_w, precision=lax.Precision.HIGHEST, preferred_element_type=jnp.float32)
    residual = outputs - targets.reshape(-1, channels)
    row_scale = 1.0 / patches.shape[0]
    product = lax.dot_general(
        patches,
        residual,
        (((0,), (0,)), ((), ())),
        precision=lax.Precision.HIGHEST,
        preferred_element_type=jnp.float32,
    )
    my_rows = lax.psum_scatter(product * row_scale, "local", scatter_dimension=0, tiled=True)
    node_count = lax.axis_size("node")
    levels = node_count.bit_length() - 1
    row_count = my_rows.shape[0]
    col_width = channels // node_count
    node_id = lax.axis_index("node")
    piece_blocks = my_rows.reshape(row_count, node_count, col_width)
    for tree_level in range(levels):
        is_upper = jnp.bitwise_and(jnp.right_shift(node_id, tree_level), 1) == 1
        remaining = piece_blocks.shape[1]
        split_view = piece_blocks.reshape(row_count, remaining // 2, 2, col_width)
        lower_half = split_view[:, :, 0, :]
        upper_half = split_view[:, :, 1, :]
        kept_part = jnp.where(is_upper, upper_half, lower_half)
        sent_part = jnp.where(is_upper, lower_half, upper_half)
        received = partner(sent_part, "node", tree_level)
        first_part = jnp.where(is_upper, received, kept_part)
        second_part = jnp.where(is_upper, kept_part, received)
        totals = jnp.stack(
            [
                jnp.sum(first_part * second_part),
                jnp.sum(first_part * first_part),
                jnp.sum(second_part * second_part),
            ]
        )
        totals = lax.psum(totals, "local")
        for inner_bit in range(tree_level + 1):
            totals = totals + partner(totals, "node", inner_bit)
        piece_blocks = adasum_pair(first_part, second_part, totals[0], totals[1], totals[2])
    return piece_blocks.reshape(row_count, col_width)


def hop(value, mapping):
    z_count = lax.axis_size("node") // 2
    pairs = []
    for z in range(z_count):
        for c in range(2):
            for y in range(2):
                for x in range(2):
                    tz, tc, ty, tx = mapping(z, c, y, x)
                    pairs.append((((z * 2 + c) * 2 + y) * 2 + x, ((tz * 2 + tc) * 2 + ty) * 2 + tx))
    return lax.ppermute(value, ("node", "local"), pairs)


def split2(v):
    hi = v.astype(jnp.bfloat16)
    lo = (v - hi.astype(jnp.float32)).astype(jnp.bfloat16)
    return hi, lo


def mm(a, b):
    return jnp.dot(a, b, preferred_element_type=jnp.float32)


def low_lanes(shape):
    return lax.broadcasted_iota(jnp.int32, shape, len(shape) - 1) < HALF


def pair_pack(a, b):
    low = low_lanes(a.shape)
    axis = a.ndim - 1
    return (jnp.where(low, a, pltpu.roll(b, HALF, axis)), jnp.where(low, pltpu.roll(a, HALF, axis), b))


def lane_halves(v):
    evens, odds = [], []
    for k in range(v.shape[1] // 256):
        e, o = pair_pack(v[:, 256 * k : 256 * k + 128], v[:, 256 * k + 128 : 256 * k + 256])
        evens.append(e)
        odds.append(o)
    return jnp.concatenate(evens, axis=1), jnp.concatenate(odds, axis=1)


def split_kernel(s_ref, x_ref, own_ref, other_ref):
    even, odd = lane_halves(x_ref[...])
    up = s_ref[0] == 1
    own_ref[...] = jnp.where(up, odd, even)
    other_ref[...] = jnp.where(up, even, odd)


def residual_kernel(s_ref, x_ref, t_ref, w_ref, own_ref, other_ref, pad_ref, acc_ref):
    side = x_ref.shape[0]
    imgs, ch = x_ref.shape[2], x_ref.shape[3]
    rows = side * side * imgs
    tap = pl.program_id(0)

    @pl.when(tap == 0)
    def _():
        pad_ref[...] = jnp.zeros(pad_ref.shape, jnp.float32)
        pad_ref[1 : side + 1, 1 : side + 1] = x_ref[...]
        acc_ref[...] = -t_ref[...]

    shifted = pad_ref[pl.ds(tap // 3, side), pl.ds(tap % 3, side)].reshape(rows, ch)
    xh, xl = split2(shifted)
    wh, wl = split2(w_ref[0])
    acc_ref[...] += mm(xh, wh) + (mm(xh, wl) + mm(xl, wh))

    @pl.when(tap == pl.num_programs(0) - 1)
    def _():
        even, odd = lane_halves(acc_ref[...])
        up = s_ref[0] == 1
        own_ref[...] = jnp.where(up, odd, even)
        other_ref[...] = jnp.where(up, even, odd)


def gradient_kernel(
    scale, side, s_ref, x0, x1, x2, x3, r0, r1, r2, r3, keep_ref, send_ref, xt, rh, rl, g_ref
):
    xs, rs = (x0, x1, x2, x3), (r0, r1, r2, r3)
    rows, width = x0.shape
    strip = rows // side
    imgs = strip // side
    span = (side + 1) * 4 * imgs
    for ref in (rh, rl):
        for edge in (0, side + 1, side + 2):
            ref[:, edge] = jnp.zeros((side, 4 * imgs, width), jnp.bfloat16)
    for r in range(side):
        def gather(refs):
            parts = [ref[r * strip : (r + 1) * strip, :].reshape(side, imgs, width) for ref in refs]
            return jnp.concatenate(parts, axis=1)

        rows_x = gather(xs).reshape(4 * strip, width)
        rows_x = jnp.concatenate([rows_x, jnp.zeros((span - 4 * strip, width), jnp.float32)], axis=0)
        xh, xl = split2(rows_x.T)
        xt[r, :, 0:span] = xh
        xt[r, :, span : 2 * span] = xh
        xt[r, :, 2 * span : 3 * span] = xl
        h, lo = split2(gather(rs))
        rh[r, 1 : side + 1] = h
        rl[r, 1 : side + 1] = lo

    def column(j, carry):
        for i in range(3):
            total = None
            for r in range(side):
                p = r - i + 1
                if p < 0 or p >= side:
                    continue
                bh = rh[p, pl.ds(2 - j, side + 1)].reshape(span, width)
                bl = rl[p, pl.ds(2 - j, side + 1)].reshape(span, width)
                part = mm(xt[r], jnp.concatenate([bh, bl, bh], axis=0))
                total = part if total is None else total + part
            per = width // BLK
            g_ref[pl.ds((3 * i + j) * per, per)] = (total * scale).reshape(per, BLK, width)
        return carry

    lax.fori_loop(0, 3, column, 0)
    odd = s_ref[0] == 1
    per = g_ref.shape[0] // 8
    for quarter in range(4):
        for k in range(width // 128):
            slot = 4 * jnp.bitwise_xor(k, s_ref[1]) + 2 * jnp.bitwise_xor(quarter // 2, s_ref[2])
            slot = slot + jnp.bitwise_xor(quarter % 2, s_ref[3])
            for m in range(per):
                a = g_ref[2 * per * quarter + m, :, 128 * k : 128 * k + 128]
                b = g_ref[2 * per * quarter + per + m, :, 128 * k : 128 * k + 128]
                first, second = pair_pack(a, b)
                keep_ref[slot, m * BLK : (m + 1) * BLK, :] = jnp.where(odd, second, first)
                send_ref[slot, m * BLK : (m + 1) * BLK, :] = jnp.where(odd, first, second)


def column_sums(a, b):
    return jnp.sum((a * b).reshape(-1, a.shape[-1]), axis=0, keepdims=True)


def fetch(sources, slots, sems):
    copies = [pltpu.make_async_copy(src, dst, sems.at[i]) for i, (src, dst) in enumerate(zip(sources, slots))]
    for copy in copies:
        copy.start()
    return copies


def pair_dots_kernel(s_ref, keep_ref, received_ref, out_ref, buf, sems):
    core = s_ref[0]
    count = keep_ref.shape[0]
    sources = [ref.at[d] for d in range(count) for ref in (keep_ref, received_ref)]
    copies = fetch(sources, [buf.at[i] for i in range(2 * count)], sems)
    cross = mine = theirs = jnp.zeros((1, out_ref.shape[1]), jnp.float32)
    for d in range(count):
        copies[2 * d].wait()
        copies[2 * d + 1].wait()
        a, b = buf[2 * d], buf[2 * d + 1]
        cross += column_sums(a, b)
        mine += column_sums(a, a)
        theirs += column_sums(b, b)
    out_ref[...] = jnp.zeros(out_ref.shape, jnp.float32)
    out_ref[0:1] = cross
    out_ref[1:2] = jnp.where(core == 0, mine, theirs)
    out_ref[2:3] = jnp.where(core == 0, theirs, mine)


def pair_coefs(cross, left_sq, right_sq):
    return 1.0 - cross / (2.0 * (left_sq + epsilon)), 1.0 - cross / (2.0 * (right_sq + epsilon))


def pair_mix_kernel(s_ref, totals_ref, keep_ref, received_ref, *refs):
    core = s_ref[0]
    count = keep_ref.shape[0]
    out_refs, (buf, in_sems, out_sems) = refs[:count], refs[count:]
    order = list(range(count - 1, -1, -1))
    sources = [ref.at[d] for d in order for ref in (keep_ref, received_ref)]
    copies = fetch(sources, [buf.at[i] for i in range(2 * count)], in_sems)
    totals = jnp.sum(totals_ref[...], axis=1, keepdims=True)
    left, right = pair_coefs(totals[0:1], totals[1:2], totals[2:3])
    keep_coef = jnp.where(core == 0, left, right)
    received_coef = jnp.where(core == 0, right, left)
    stores = []
    for i, d in enumerate(order):
        copies[2 * i].wait()
        copies[2 * i + 1].wait()
        buf[2 * i] = keep_coef * buf[2 * i] + received_coef * buf[2 * i + 1]
        stores.append(pltpu.make_async_copy(buf.at[2 * i], out_refs[d], out_sems.at[i]))
        stores[-1].start()
    for store in stores:
        store.wait()


def gram_kernel(s_ref, *refs):
    upper, x = s_ref[0], s_ref[1]
    blocks, (gram_ref, buf, sems) = refs[:8], refs[8:]
    copies = fetch(blocks, [buf.at[slot_of(i)] for i in range(8)], sems)
    node = [2 * jnp.bitwise_xor(upper, d // 2) + jnp.bitwise_xor(x, d % 2) for d in range(4)]
    for i in (0, 1, 2, 3, 4, 5, 6, 7):
        copies[i].wait()
    for e in range(4):
        for d in range(e + 1):
            value = column_sums(buf[2 * d : 2 * d + 2], buf[2 * e : 2 * e + 2])
            gram_ref[pl.ds(4 * node[d] + node[e], 1)] = value
            gram_ref[pl.ds(4 * node[e] + node[d], 1)] = value


def slot_of(index):
    e, dy, dx = index // 4, index // 2 % 2, index % 2
    return 4 * e + 2 * dx + dy


def place_kernel(s_ref, gram_ref, *refs):
    upper, x, y = s_ref[0], s_ref[1], s_ref[2]
    blocks, (out_ref, parts, rows_ref, sems) = refs[:8], refs[8:]
    copies = fetch(blocks, [parts.at[slot_of(i)] for i in range(8)], sems)
    gram = jnp.sum(gram_ref[...], axis=1, keepdims=True)
    g = lambda a, b: gram[4 * a + b : 4 * a + b + 1]
    p = pair_coefs(g(0, 1), g(0, 0), g(1, 1)) + pair_coefs(g(2, 3), g(2, 2), g(3, 3))
    cross = p[0] * (p[2] * g(0, 2) + p[3] * g(0, 3)) + p[1] * (p[2] * g(1, 2) + p[3] * g(1, 3))
    near = p[0] * p[0] * g(0, 0) + 2.0 * p[0] * p[1] * g(0, 1) + p[1] * p[1] * g(1, 1)
    far = p[2] * p[2] * g(2, 2) + 2.0 * p[2] * p[3] * g(2, 3) + p[3] * p[3] * g(3, 3)
    near_coef, far_coef = pair_coefs(cross, near, far)
    absolute = (near_coef * p[0], near_coef * p[1], far_coef * p[2], far_coef * p[3])
    coefs = []
    for d in range(4):
        owner = 2 * jnp.bitwise_xor(upper, d // 2) + jnp.bitwise_xor(x, d % 2)
        coef = absolute[3]
        for a in range(3):
            coef = jnp.where(owner == a, absolute[a], coef)
        coefs.append(coef)
    for copy in copies:
        copy.wait()
    for dy in range(2):
        part = [parts[2 * d + dy] for d in range(4)]
        block = coefs[0] * part[0] + coefs[1] * part[1] + (coefs[2] * part[2] + coefs[3] * part[3])
        upper_half = pltpu.roll(block, HALF, 1)
        rows = jnp.concatenate([block[:, :HALF], upper_half[:, :HALF]], axis=0)
        rows = rows.reshape(rows_ref.shape[0], HALF, HALF)
        slot = jnp.bitwise_xor(y, dy)
        for k in range(rows_ref.shape[0]):
            rows_ref[k, slot] = rows[k]
    out_ref[...] = rows_ref[...].reshape(out_ref.shape[1], HALF).T


VM = pl.BlockSpec(memory_space=pltpu.VMEM)
HB = pl.BlockSpec(memory_space=pltpu.HBM)
SM = pl.BlockSpec(memory_space=pltpu.SMEM)


def f32(*shape):
    return jax.ShapeDtypeStruct(shape, jnp.float32)


def tile_plan(images, targets, weight):
    return tiles(images, targets, weight)


def tiles(images, targets, weight):
    imgs, side, _, channels = images.shape
    width = channels // 2
    rows = side * side * imgs
    node_id = lax.axis_index("node")
    local_id = lax.axis_index("local")
    z, c = node_id // 2, node_id % 2
    y, x = local_id // 2, local_id % 2

    def scalars(*values):
        return jnp.stack([jnp.asarray(v, jnp.int32) for v in values])

    xt = jnp.transpose(images, (1, 2, 0, 3))
    x_own, x_other = pl.pallas_call(
        split_kernel,
        out_shape=(f32(rows, width), f32(rows, width)),
        in_specs=[SM, VM],
        out_specs=(VM, VM),
        name="split_images",
    )(scalars(y), xt.reshape(rows, channels))
    x_y = hop(x_other, lambda z, c, y, x: (z, c, 1 - y, x))
    x_x = hop(x_own, lambda z, c, y, x: (z, c, y, 1 - x))
    x_d = hop(x_other, lambda z, c, y, x: (z, c, 1 - y, 1 - x))

    tt = jnp.transpose(targets, (1, 2, 0, 3)).reshape(rows, channels)
    taps = weight.shape[0] * weight.shape[1]
    whole = lambda *shape: pl.BlockSpec(shape, lambda t: (0,) * len(shape))
    r_own, r_other = pl.pallas_call(
        residual_kernel,
        grid=(taps,),
        out_shape=(f32(rows, width), f32(rows, width)),
        in_specs=[
            SM,
            whole(side, side, imgs, channels),
            whole(rows, channels),
            pl.BlockSpec((1, channels, channels), lambda t: (t, 0, 0)),
        ],
        out_specs=(whole(rows, width), whole(rows, width)),
        scratch_shapes=[
            pltpu.VMEM((side + 2, side + 2, imgs, channels), jnp.float32),
            pltpu.VMEM((rows, channels), jnp.float32),
        ],
        cost_estimate=pl.CostEstimate(
            flops=6 * rows * taps * channels * channels, bytes_accessed=4 * taps * channels * channels, transcendentals=0
        ),
        name="residual",
    )(scalars(x), xt, tt, weight.reshape(taps, channels, channels))
    r_x = hop(r_other, lambda z, c, y, x: (z, c, y, 1 - x))
    r_d = hop(r_other, lambda z, c, y, x: (z, c, 1 - y, 1 - x))
    r_y = hop(r_own, lambda z, c, y, x: (z, c, 1 - y, x))

    z_count = lax.axis_size("node") // 2
    part = taps * width // 8
    count = 2 * z_count
    place = scalars(z // 2, x, y)
    keep, send = pl.pallas_call(
        lambda *refs: gradient_kernel(1.0 / rows, side, *refs),
        out_shape=(f32(count, part, 128), f32(count, part, 128)),
        in_specs=[SM] + [VM] * 8,
        out_specs=(VM, VM),
        scratch_shapes=[
            pltpu.VMEM((side, width, 3 * (side + 1) * 4 * imgs), jnp.bfloat16),
            pltpu.VMEM((side, side + 3, 4 * imgs, width), jnp.bfloat16),
            pltpu.VMEM((side, side + 3, 4 * imgs, width), jnp.bfloat16),
            pltpu.VMEM((taps * width // BLK, BLK, width), jnp.float32),
        ],
        cost_estimate=pl.CostEstimate(
            flops=24 * rows * taps * width * width, bytes_accessed=4 * taps * width * width, transcendentals=0
        ),
        name="gradient",
    )(scalars(c, z // 2, y, z % 2), x_own, x_x, x_y, x_d, r_own, r_x, r_y, r_d)

    received = hop(send, lambda z, c, y, x: (z, 1 - c, y, x))
    totals = pl.pallas_call(
        pair_dots_kernel,
        out_shape=f32(8, 128),
        in_specs=[SM, HB, HB],
        out_specs=VM,
        scratch_shapes=[pltpu.VMEM((2 * count, part, 128), jnp.float32), pltpu.SemaphoreType.DMA((2 * count,))],
        name="pair_dots",
    )(scalars(c), keep, received)
    totals = plane_sum(totals)
    blocks = pl.pallas_call(
        pair_mix_kernel,
        out_shape=(f32(part, 128),) * count,
        in_specs=[SM, VM, HB, HB],
        out_specs=(HB,) * count,
        scratch_shapes=[
            pltpu.VMEM((2 * count, part, 128), jnp.float32),
            pltpu.SemaphoreType.DMA((2 * count,)),
            pltpu.SemaphoreType.DMA((count,)),
        ],
        name="pair_mix",
    )(scalars(c), totals, keep, received)

    moved = []
    for index in range(count):
        e, dy, dx = index // 4, index // 2 % 2, index % 2
        mapping = lambda z, c, y, x, e=e, dy=dy, dx=dx: (2 * (z // 2 ^ e) + c, x, y ^ dy, z % 2 ^ dx)
        moved.append(hop(blocks[index], mapping))
    gram = pl.pallas_call(
        gram_kernel,
        out_shape=f32(16, 128),
        in_specs=[SM] + [HB] * count,
        out_specs=VM,
        scratch_shapes=[pltpu.VMEM((count, part, 128), jnp.float32), pltpu.SemaphoreType.DMA((count,))],
        name="gram",
    )(place, *moved)
    along = [hop(gram, lambda z, c, y, x, d=d: (z ^ d, c, y, x)) for d in range(1, z_count)]
    gram = plane_sum((gram + along[0]) + (along[1] + along[2]))
    out = pl.pallas_call(
        place_kernel,
        out_shape=f32(HALF, 4 * part),
        in_specs=[SM, VM] + [HB] * count,
        out_specs=VM,
        scratch_shapes=[
            pltpu.VMEM((count, part, 128), jnp.float32),
            pltpu.VMEM((2 * part // HALF, 2, HALF, HALF), jnp.float32),
            pltpu.SemaphoreType.DMA((count,)),
        ],
        name="place",
    )(place, gram, *moved)
    return out.T


def plane_sum(value):
    value = value + hop(value, lambda z, c, y, x: (z, 1 - c, y, x))
    across = [hop(value, lambda z, c, y, x, d=d: (z, c, y ^ (d >> 1), x ^ (d & 1))) for d in (1, 2, 3)]
    return (value + across[0]) + (across[1] + across[2])


def fits(images, mesh):
    return (
        mesh.shape["local"] == 4
        and mesh.shape["node"] == 8
        and images.shape[3] == mesh.shape["node"] * HALF
        and images.shape[0] // mesh.size == 8
    )


def solution(mesh):
    def run(images, targets, weight):
        tiled = fits(images, mesh)
        step = jax.shard_map(
            tile_plan if tiled else general_plan,
            mesh=mesh,
            in_specs=(
                P(("node", "local"), None, None, None),
                P(("node", "local"), None, None, None),
                P(),
            ),
            out_specs=P("local", "node"),
            check_vma=False,
        )
        return step(images, targets, weight)

    return run
```

profile of v0, /device:TPU:0, one launch (start us, length us, event | category | flops | bytes accessed | tf_op | source)
XLA Modules:
  0.0 143.3 jit_solution(5882250254261539)
XLA Ops:
  0.0 12.1 %residual.1 = (f32[392,256]{1,0:T(8,128)}, f32[392,256]{1,0:T(8,128)}) custom-call(s32[1]{0:T(128)} %bitcast.1.s_ref, f32[7,7,8,512]{3,2,1,0:T(8,128)} %bitcast.13, f32[392,512]{1,0:T(8,128)} %bitcast.16, f32[9,512,512]{2,1,0:T(8,128)} %bitcast.15), custom_call_target="tpu_custom_call" | custom-call | flops 5549064192 | bytes 9437184 | tf_op jit(solution)/shard_map/residual/pallas_call | solution.py:360
  12.1 3.0 %collective-permute-start.4 = (f32[392,256]{1,0:T(8,128)}, f32[392,256]{1,0:T(8,128)S(1)}, u32[]{:S(2)}, u32[]{:S(2)}) collective-permute-start(f32[392,256]{1,0:T(8,128)} %get-tuple-element.21.refs_5_), channel_id=1, source_target_pairs={{0,2},{1,3},{2,0},{3,1},{4,6},{5,7},{6,4},{7,5},{8,10},{9,11},{10,... | collective-permute-start | bytes 1204232 | tf_op jit(solution)/shard_map/ppermute | solution.py:92
  15.1 1.4 collective-permute-start.5
  16.6 2.3 %split_images.1 = (f32[392,256]{1,0:T(8,128)}, f32[392,256]{1,0:T(8,128)}) custom-call(s32[1]{0:T(128)} %bitcast.2.s_ref, f32[392,512]{1,0:T(8,128)} %bitcast.14), custom_call_target="tpu_custom_call" | custom-call | tf_op jit(solution)/shard_map/split_images/pallas_call | solution.py:346
  18.9 2.0 %collective-permute-start = (f32[392,256]{1,0:T(8,128)}, f32[392,256]{1,0:T(8,128)S(1)}, u32[]{:S(2)}, u32[]{:S(2)}) collective-permute-start(f32[392,256]{1,0:T(8,128)} %get-tuple-element.19.refs_1_), channel_id=1, source_target_pairs={{0,1},{1,0},{2,3},{3,2},{4,5},{5,4},{6,7},{7,6},{8,9},{9,8},{10,11... | collective-permute-start | bytes 1204232 | tf_op jit(solution)/shard_map/ppermute | solution.py:92
  20.9 1.5 %collective-permute-start.2 = (f32[392,256]{1,0:T(8,128)}, f32[392,256]{1,0:T(8,128)S(1)}, u32[]{:S(2)}, u32[]{:S(2)}) collective-permute-start(f32[392,256]{1,0:T(8,128)} %get-tuple-element.20), channel_id=1, source_target_pairs={{0,3},{1,2},{2,1},{3,0},{4,7},{5,6},{6,5},{7,4},{8,11},{9,10},{10,... | collective-permute-start | bytes 1204232 | tf_op jit(solution)/shard_map/ppermute | solution.py:92
  22.4 10.8 %collective-permute-done.4.refs_7_ = f32[392,256]{1,0:T(8,128)S(1)} collective-permute-done((f32[392,256]{1,0:T(8,128)}, f32[392,256]{1,0:T(8,128)S(1)}, u32[]{:S(2)}, u32[]{:S(2)}) %collective-permute-start.4) | collective-permute-done | bytes 401440 | tf_op jit(solution)/shard_map/ppermute | solution.py:92
  33.2 1.7 %collective-permute-start.1 = (f32[392,256]{1,0:T(8,128)}, f32[392,256]{1,0:T(8,128)S(1)}, u32[]{:S(2)}, u32[]{:S(2)}) collective-permute-start(f32[392,256]{1,0:T(8,128)} %get-tuple-element.20), channel_id=1, source_target_pairs={{0,2},{1,3},{2,0},{3,1},{4,6},{5,7},{6,4},{7,5},{8,10},{9,11},{10,... | collective-permute-start | bytes 1204232 | tf_op jit(solution)/shard_map/ppermute | solution.py:92
  35.6 8.6 %collective-permute-done.refs_2_ = f32[392,256]{1,0:T(8,128)S(1)} collective-permute-done((f32[392,256]{1,0:T(8,128)}, f32[392,256]{1,0:T(8,128)S(1)}, u32[]{:S(2)}, u32[]{:S(2)}) %collective-permute-start) | collective-permute-done | bytes 401440 | tf_op jit(solution)/shard_map/ppermute | solution.py:92
  44.2 8.7 %collective-permute-done.2.refs_4_ = f32[392,256]{1,0:T(8,128)S(1)} collective-permute-done((f32[392,256]{1,0:T(8,128)}, f32[392,256]{1,0:T(8,128)S(1)}, u32[]{:S(2)}, u32[]{:S(2)}) %collective-permute-start.2) | collective-permute-done | bytes 401440 | tf_op jit(solution)/shard_map/ppermute | solution.py:92
  54.4 11.1 %gradient.1 = (f32[8,288,128]{2,1,0:T(8,128)}, f32[8,288,128]{2,1,0:T(8,128)}) custom-call(s32[4]{0:T(128)} %pad_add_fusion.1.refs_0_, f32[392,256]{1,0:T(8,128)} %get-tuple-element.19.refs_1_, f32[392,256]{1,0:T(8,128)} %copy-done.12, f32[392,256]{1,0:T(8,128)} %copy-done.14, f32[392,256]{1,0:T(8,128)} %copy-done.13, f32[392,256]{1,0:T(8,128)} %get-tuple-element.21.refs_5_, ...), custom_call_target="tpu_custom_call" | custom-call | flops 5549064192 | bytes 2359296 | tf_op jit(solution)/shard_map/gradient/pallas_call | solution.py:388
  65.5 3.1 %collective-permute-done.6.received_ref = f32[8,288,128]{2,1,0:T(8,128)S(1)} collective-permute-done((f32[8,288,128]{2,1,0:T(8,128)}, f32[8,288,128]{2,1,0:T(8,128)S(1)}, u32[]{:S(2)}, u32[]{:S(2)}) %collective-permute-start.6) | collective-permute-done | bytes 1179680 | tf_op jit(solution)/shard_map/ppermute | solution.py:92
  69.6 2.5 %pair_dots.1 = f32[8,128]{1,0:T(8,128)} custom-call(s32[1]{0:T(128)} %bitcast.3.s_ref, f32[8,288,128]{2,1,0:T(8,128)} %get-tuple-element.23.keep_ref, f32[8,288,128]{2,1,0:T(8,128)} %copy-done), custom_call_target="tpu_custom_call" | custom-call | tf_op jit(solution)/shard_map/pair_dots/pallas_call | solution.py:406
  72.3 1.2 collective-permute-done.7
  74.2 1.5 %collective-permute-start.10 = (f32[8,128]{1,0:T(8,128)S(1)}, f32[8,128]{1,0:T(8,128)S(1)}, u32[]{:S(2)}, u32[]{:S(2)}) collective-permute-start(f32[8,128]{1,0:T(8,128)S(1)} %add.49), channel_id=1, source_target_pairs={{0,3},{1,2},{2,1},{3,0},{4,7},{5,6},{6,5},{7,4},{8,11},{9,10},{10,... | collective-permute-start | bytes 12296 | tf_op jit(solution)/shard_map/ppermute | solution.py:92
  75.7 1.4 collective-permute-start.9
  79.3 1.4 collective-permute-done.8
  81.3 3.3 %pair_mix.1 = (f32[288,128]{1,0:T(8,128)}, f32[288,128]{1,0:T(8,128)}, f32[288,128]{1,0:T(8,128)}, f32[288,128]{1,0:T(8,128)}, f32[288,128]{1,0:T(8,128)}, /*ind...) custom-call(s32[1]{0:T(128)} %bitcast.3.s_ref, f32[8,128]{1,0:T(8,128)} %add_add_fusion.2.totals_ref, ...), custom_call_target="tpu_custom_call" | custom-call | tf_op jit(solution)/shard_map/pair_mix/pallas_call | solution.py:415
  84.6 1.6 %collective-permute-start.11 = (f32[288,128]{1,0:T(8,128)}, f32[288,128]{1,0:T(8,128)S(1)}, u32[]{:S(2)}, u32[]{:S(2)}) collective-permute-start(f32[288,128]{1,0:T(8,128)} %get-tuple-element.25), channel_id=1, source_target_pairs={{0,0},{1,4},{2,2},{3,6},{4,8},{5,12},{6,10},{7,14},{8,1},{9,5},{10... | collective-permute-start | bytes 442376 | tf_op jit(solution)/shard_map/ppermute | solution.py:92
  87.6 3.2 %collective-permute-start.14 = (f32[288,128]{1,0:T(8,128)}, f32[288,128]{1,0:T(8,128)S(1)}, u32[]{:S(2)}, u32[]{:S(2)}) collective-permute-start(f32[288,128]{1,0:T(8,128)} %get-tuple-element.28), channel_id=1, source_target_pairs={{0,3},{1,7},{2,1},{3,5},{4,11},{5,15},{6,9},{7,13},{8,2},{9,6},{10... | collective-permute-start | bytes 442376 | tf_op jit(solution)/shard_map/ppermute | solution.py:92
  90.9 2.6 %collective-permute-start.15 = (f32[288,128]{1,0:T(8,128)}, f32[288,128]{1,0:T(8,128)S(1)}, u32[]{:S(2)}, u32[]{:S(2)}) collective-permute-start(f32[288,128]{1,0:T(8,128)} %get-tuple-element.29), channel_id=1, source_target_pairs={{0,16},{1,20},{2,18},{3,22},{4,24},{5,28},{6,26},{7,30},{8,17},{9,... | collective-permute-start | bytes 442376 | tf_op jit(solution)/shard_map/ppermute | solution.py:92
  93.5 1.9 %collective-permute-start.16 = (f32[288,128]{1,0:T(8,128)}, f32[288,128]{1,0:T(8,128)S(1)}, u32[]{:S(2)}, u32[]{:S(2)}) collective-permute-start(f32[288,128]{1,0:T(8,128)} %get-tuple-element.30), channel_id=1, source_target_pairs={{0,17},{1,21},{2,19},{3,23},{4,25},{5,29},{6,27},{7,31},{8,16},{9,... | collective-permute-start | bytes 442376 | tf_op jit(solution)/shard_map/ppermute | solution.py:92
  95.4 2.4 %collective-permute-start.17 = (f32[288,128]{1,0:T(8,128)}, f32[288,128]{1,0:T(8,128)S(1)}, u32[]{:S(2)}, u32[]{:S(2)}) collective-permute-start(f32[288,128]{1,0:T(8,128)} %get-tuple-element.31), channel_id=1, source_target_pairs={{0,18},{1,22},{2,16},{3,20},{4,26},{5,30},{6,24},{7,28},{8,19},{9,... | collective-permute-start | bytes 442376 | tf_op jit(solution)/shard_map/ppermute | solution.py:92
  97.9 3.6 %collective-permute-start.18 = (f32[288,128]{1,0:T(8,128)}, f32[288,128]{1,0:T(8,128)S(1)}, u32[]{:S(2)}, u32[]{:S(2)}) collective-permute-start(f32[288,128]{1,0:T(8,128)} %get-tuple-element.32), channel_id=1, source_target_pairs={{0,19},{1,23},{2,17},{3,21},{4,27},{5,31},{6,25},{7,29},{8,18},{9,... | collective-permute-start | bytes 442376 | tf_op jit(solution)/shard_map/ppermute | solution.py:92
  102.0 5.9 %collective-permute-done.16.refs_5_ = f32[288,128]{1,0:T(8,128)S(1)} collective-permute-done((f32[288,128]{1,0:T(8,128)}, f32[288,128]{1,0:T(8,128)S(1)}, u32[]{:S(2)}, u32[]{:S(2)}) %collective-permute-start.16) | collective-permute-done | bytes 147488 | tf_op jit(solution)/shard_map/ppermute | solution.py:92
  108.0 9.8 %collective-permute-done.17.refs_6_ = f32[288,128]{1,0:T(8,128)S(1)} collective-permute-done((f32[288,128]{1,0:T(8,128)}, f32[288,128]{1,0:T(8,128)S(1)}, u32[]{:S(2)}, u32[]{:S(2)}) %collective-permute-start.17) | collective-permute-done | bytes 147488 | tf_op jit(solution)/shard_map/ppermute | solution.py:92
  119.0 2.9 %gram.1 = f32[16,128]{1,0:T(8,128)} custom-call(s32[3]{0:T(128)} %pad_add_fusion.s_ref, f32[288,128]{1,0:T(8,128)} %copy-done.1, f32[288,128]{1,0:T(8,128)} %copy-done.2, f32[288,128]{1,0:T(8,128)} %copy-done.3, f32[288,128]{1,0:T(8,128)} %copy-done.4, f32[288,128]{1,0:T(8,128)} %copy-done.5, f32[288,128]{1,0:T(8,128)} %copy-done.6, f32[288,128]{1,0:T(8,128)} %copy-done.7, ...), custom_call_target="tpu_custom_call" | custom-call | tf_op jit(solution)/shard_map/gram/pallas_call | solution.py:433
  122.0 5.8 %collective-permute-start.21 = (f32[16,128]{1,0:T(8,128)}, f32[16,128]{1,0:T(8,128)S(1)}, u32[]{:S(2)}, u32[]{:S(2)}) collective-permute-start(f32[16,128]{1,0:T(8,128)} %gram.1), channel_id=1, source_target_pairs={{0,24},{1,25},{2,26},{3,27},{4,28},{5,29},{6,30},{7,31},{8,16},{9,... | collective-permute-start | bytes 24584 | tf_op jit(solution)/shard_map/ppermute | solution.py:92
  129.6 2.9 %collective-permute-done.20 = f32[16,128]{1,0:T(8,128)S(1)} collective-permute-done((f32[16,128]{1,0:T(8,128)}, f32[16,128]{1,0:T(8,128)S(1)}, u32[]{:S(2)}, u32[]{:S(2)}) %collective-permute-start.20) | collective-permute-done | bytes 8224 | tf_op jit(solution)/shard_map/ppermute | solution.py:92
  134.4 1.4 collective-permute-start.24
  135.8 2.0 %collective-permute-start.23 = (f32[16,128]{1,0:T(8,128)S(1)}, f32[16,128]{1,0:T(8,128)S(1)}, u32[]{:S(2)}, u32[]{:S(2)}) collective-permute-start(f32[16,128]{1,0:T(8,128)S(1)} %add.56), channel_id=1, source_target_pairs={{0,1},{1,0},{2,3},{3,2},{4,5},{5,4},{6,7},{7,6},{8,9},{9,8},{10,11... | collective-permute-start | bytes 24584 | tf_op jit(solution)/shard_map/ppermute | solution.py:92
  140.1 3.2 %place.1 = f32[64,1152]{1,0:T(8,128)} custom-call(s32[3]{0:T(128)} %pad_add_fusion.s_ref, f32[16,128]{1,0:T(8,128)} %add_add_fusion.gram_ref, f32[288,128]{1,0:T(8,128)} %copy-done.1, f32[288,128]{1,0:T(8,128)} %copy-done.2, f32[288,128]{1,0:T(8,128)} %copy-done.3, f32[288,128]{1,0:T(8,128)} %copy-done.4, f32[288,128]{1,0:T(8,128)} %copy-done.5, ...), custom_call_target="tpu_custom_call" | custom-call | tf_op jit(solution)/shard_map/place/pallas_call | solution.py:443
  (64 shorter events, 16.2 us)
Async XLA Ops:
  12.1 21.1 %collective-permute-start.4 = (f32[392,256]{1,0:T(8,128)}, f32[392,256]{1,0:T(8,128)S(1)}, u32[]{:S(2)}, u32[]{:S(2)}) collective-permute-start(f32[392,256]{1,0:T(8,128)} %get-tuple-element.21.refs_5_), channel_id=1, source_target_pairs={{0,2},{1,3},{2,0},{3,1},{4,6},{5,7},{6,4},{7,5},{8,10},{9,11},{10,... | collective-permute-start | bytes 1204232 | tf_op jit(solution)/shard_map/ppermute | solution.py:92
  15.1 20.4 %collective-permute-start.5 = (f32[392,256]{1,0:T(8,128)}, f32[392,256]{1,0:T(8,128)S(1)}, u32[]{:S(2)}, u32[]{:S(2)}) collective-permute-start(f32[392,256]{1,0:T(8,128)} %get-tuple-element.22), channel_id=1, source_target_pairs={{0,3},{1,2},{2,1},{3,0},{4,7},{5,6},{6,5},{7,4},{8,11},{9,10},{10,... | collective-permute-start | bytes 1204232 | tf_op jit(solution)/shard_map/ppermute | solution.py:92
  16.6 19.0 %collective-permute-start.3 = (f32[392,256]{1,0:T(8,128)}, f32[392,256]{1,0:T(8,128)S(1)}, u32[]{:S(2)}, u32[]{:S(2)}) collective-permute-start(f32[392,256]{1,0:T(8,128)} %get-tuple-element.22), channel_id=1, source_target_pairs={{0,1},{1,0},{2,3},{3,2},{4,5},{5,4},{6,7},{7,6},{8,9},{9,8},{10,11... | collective-permute-start | bytes 1204232 | tf_op jit(solution)/shard_map/ppermute | solution.py:92
  18.9 25.2 %collective-permute-start = (f32[392,256]{1,0:T(8,128)}, f32[392,256]{1,0:T(8,128)S(1)}, u32[]{:S(2)}, u32[]{:S(2)}) collective-permute-start(f32[392,256]{1,0:T(8,128)} %get-tuple-element.19.refs_1_), channel_id=1, source_target_pairs={{0,1},{1,0},{2,3},{3,2},{4,5},{5,4},{6,7},{7,6},{8,9},{9,8},{10,11... | collective-permute-start | bytes 1204232 | tf_op jit(solution)/shard_map/ppermute | solution.py:92
  20.9 31.9 %collective-permute-start.2 = (f32[392,256]{1,0:T(8,128)}, f32[392,256]{1,0:T(8,128)S(1)}, u32[]{:S(2)}, u32[]{:S(2)}) collective-permute-start(f32[392,256]{1,0:T(8,128)} %get-tuple-element.20), channel_id=1, source_target_pairs={{0,3},{1,2},{2,1},{3,0},{4,7},{5,6},{6,5},{7,4},{8,11},{9,10},{10,... | collective-permute-start | bytes 1204232 | tf_op jit(solution)/shard_map/ppermute | solution.py:92
  33.2 19.6 %copy-start.9 = (f32[392,256]{1,0:T(8,128)}, f32[392,256]{1,0:T(8,128)S(1)}, u32[]{:S(2)}) copy-start(f32[392,256]{1,0:T(8,128)S(1)} %collective-permute-done.4.refs_7_) | copy-start | bytes 1204228
  33.2 19.6 %collective-permute-start.1 = (f32[392,256]{1,0:T(8,128)}, f32[392,256]{1,0:T(8,128)S(1)}, u32[]{:S(2)}, u32[]{:S(2)}) collective-permute-start(f32[392,256]{1,0:T(8,128)} %get-tuple-element.20), channel_id=1, source_target_pairs={{0,2},{1,3},{2,0},{3,1},{4,6},{5,7},{6,4},{7,5},{8,10},{9,11},{10,... | collective-permute-start | bytes 1204232 | tf_op jit(solution)/shard_map/ppermute | solution.py:92
  35.6 17.3 %copy-start.10 = (f32[392,256]{1,0:T(8,128)}, f32[392,256]{1,0:T(8,128)S(1)}, u32[]{:S(2)}) copy-start(f32[392,256]{1,0:T(8,128)S(1)} %collective-permute-done.5.refs_8_) | copy-start | bytes 1204228
  35.6 17.3 %copy-start.11 = (f32[392,256]{1,0:T(8,128)}, f32[392,256]{1,0:T(8,128)S(1)}, u32[]{:S(2)}) copy-start(f32[392,256]{1,0:T(8,128)S(1)} %collective-permute-done.3.refs_6_) | copy-start | bytes 1204228
  65.5 3.1 %collective-permute-start.6 = (f32[8,288,128]{2,1,0:T(8,128)}, f32[8,288,128]{2,1,0:T(8,128)S(1)}, u32[]{:S(2)}, u32[]{:S(2)}) collective-permute-start(f32[8,288,128]{2,1,0:T(8,128)} %get-tuple-element.24), channel_id=1, source_target_pairs={{0,4},{1,5},{2,6},{3,7},{4,0},{5,1},{6,2},{7,3},{8,12},{9,13},{10,... | collective-permute-start | bytes 3538952 | tf_op jit(solution)/shard_map/ppermute | solution.py:92
  72.1 1.4 %collective-permute-start.7 = (f32[8,128]{1,0:T(8,128)}, f32[8,128]{1,0:T(8,128)S(1)}, u32[]{:S(2)}, u32[]{:S(2)}) collective-permute-start(f32[8,128]{1,0:T(8,128)} %pair_dots.1), channel_id=1, source_target_pairs={{0,4},{1,5},{2,6},{3,7},{4,0},{5,1},{6,2},{7,3},{8,12},{9,13},{10,... | collective-permute-start | bytes 12296 | tf_op jit(solution)/shard_map/ppermute | solution.py:92
  74.2 4.5 %collective-permute-start.10 = (f32[8,128]{1,0:T(8,128)S(1)}, f32[8,128]{1,0:T(8,128)S(1)}, u32[]{:S(2)}, u32[]{:S(2)}) collective-permute-start(f32[8,128]{1,0:T(8,128)S(1)} %add.49), channel_id=1, source_target_pairs={{0,3},{1,2},{2,1},{3,0},{4,7},{5,6},{6,5},{7,4},{8,11},{9,10},{10,... | collective-permute-start | bytes 12296 | tf_op jit(solution)/shard_map/ppermute | solution.py:92
  75.7 3.6 %collective-permute-start.9 = (f32[8,128]{1,0:T(8,128)S(1)}, f32[8,128]{1,0:T(8,128)S(1)}, u32[]{:S(2)}, u32[]{:S(2)}) collective-permute-start(f32[8,128]{1,0:T(8,128)S(1)} %add.49), channel_id=1, source_target_pairs={{0,2},{1,3},{2,0},{3,1},{4,6},{5,7},{6,4},{7,5},{8,10},{9,11},{10,... | collective-permute-start | bytes 12296 | tf_op jit(solution)/shard_map/ppermute | solution.py:92
  77.1 3.6 %collective-permute-start.8 = (f32[8,128]{1,0:T(8,128)S(1)}, f32[8,128]{1,0:T(8,128)S(1)}, u32[]{:S(2)}, u32[]{:S(2)}) collective-permute-start(f32[8,128]{1,0:T(8,128)S(1)} %add.49), channel_id=1, source_target_pairs={{0,1},{1,0},{2,3},{3,2},{4,5},{5,4},{6,7},{7,6},{8,9},{9,8},{10,11... | collective-permute-start | bytes 12296 | tf_op jit(solution)/shard_map/ppermute | solution.py:92
  84.6 8.9 %collective-permute-start.11 = (f32[288,128]{1,0:T(8,128)}, f32[288,128]{1,0:T(8,128)S(1)}, u32[]{:S(2)}, u32[]{:S(2)}) collective-permute-start(f32[288,128]{1,0:T(8,128)} %get-tuple-element.25), channel_id=1, source_target_pairs={{0,0},{1,4},{2,2},{3,6},{4,8},{5,12},{6,10},{7,14},{8,1},{9,5},{10... | collective-permute-start | bytes 442376 | tf_op jit(solution)/shard_map/ppermute | solution.py:92
  86.2 9.2 %collective-permute-start.12 = (f32[288,128]{1,0:T(8,128)}, f32[288,128]{1,0:T(8,128)S(1)}, u32[]{:S(2)}, u32[]{:S(2)}) collective-permute-start(f32[288,128]{1,0:T(8,128)} %get-tuple-element.26), channel_id=1, source_target_pairs={{0,1},{1,5},{2,3},{3,7},{4,9},{5,13},{6,11},{7,15},{8,0},{9,4},{10... | collective-permute-start | bytes 442376 | tf_op jit(solution)/shard_map/ppermute | solution.py:92
  87.1 10.7 %collective-permute-start.13 = (f32[288,128]{1,0:T(8,128)}, f32[288,128]{1,0:T(8,128)S(1)}, u32[]{:S(2)}, u32[]{:S(2)}) collective-permute-start(f32[288,128]{1,0:T(8,128)} %get-tuple-element.27), channel_id=1, source_target_pairs={{0,2},{1,6},{2,0},{3,4},{4,10},{5,14},{6,8},{7,12},{8,3},{9,7},{10... | collective-permute-start | bytes 442376 | tf_op jit(solution)/shard_map/ppermute | solution.py:92
  87.6 14.4 %collective-permute-start.14 = (f32[288,128]{1,0:T(8,128)}, f32[288,128]{1,0:T(8,128)S(1)}, u32[]{:S(2)}, u32[]{:S(2)}) collective-permute-start(f32[288,128]{1,0:T(8,128)} %get-tuple-element.28), channel_id=1, source_target_pairs={{0,3},{1,7},{2,1},{3,5},{4,11},{5,15},{6,9},{7,13},{8,2},{9,6},{10... | collective-permute-start | bytes 442376 | tf_op jit(solution)/shard_map/ppermute | solution.py:92
  90.9 11.1 %collective-permute-start.15 = (f32[288,128]{1,0:T(8,128)}, f32[288,128]{1,0:T(8,128)S(1)}, u32[]{:S(2)}, u32[]{:S(2)}) collective-permute-start(f32[288,128]{1,0:T(8,128)} %get-tuple-element.29), channel_id=1, source_target_pairs={{0,16},{1,20},{2,18},{3,22},{4,24},{5,28},{6,26},{7,30},{8,17},{9,... | collective-permute-start | bytes 442376 | tf_op jit(solution)/shard_map/ppermute | solution.py:92
  93.5 24.3 %copy-start.1 = (f32[288,128]{1,0:T(8,128)}, f32[288,128]{1,0:T(8,128)S(1)}, u32[]{:S(2)}) copy-start(f32[288,128]{1,0:T(8,128)S(1)} %collective-permute-done.11.refs_0_) | copy-start | bytes 442372
  93.5 14.5 %collective-permute-start.16 = (f32[288,128]{1,0:T(8,128)}, f32[288,128]{1,0:T(8,128)S(1)}, u32[]{:S(2)}, u32[]{:S(2)}) collective-permute-start(f32[288,128]{1,0:T(8,128)} %get-tuple-element.30), channel_id=1, source_target_pairs={{0,17},{1,21},{2,19},{3,23},{4,25},{5,29},{6,27},{7,31},{8,16},{9,... | collective-permute-start | bytes 442376 | tf_op jit(solution)/shard_map/ppermute | solution.py:92
  95.4 22.3 %copy-start.2 = (f32[288,128]{1,0:T(8,128)}, f32[288,128]{1,0:T(8,128)S(1)}, u32[]{:S(2)}) copy-start(f32[288,128]{1,0:T(8,128)S(1)} %collective-permute-done.12.refs_1_) | copy-start | bytes 442372
  95.4 22.3 %collective-permute-start.17 = (f32[288,128]{1,0:T(8,128)}, f32[288,128]{1,0:T(8,128)S(1)}, u32[]{:S(2)}, u32[]{:S(2)}) collective-permute-start(f32[288,128]{1,0:T(8,128)} %get-tuple-element.31), channel_id=1, source_target_pairs={{0,18},{1,22},{2,16},{3,20},{4,26},{5,30},{6,24},{7,28},{8,19},{9,... | collective-permute-start | bytes 442376 | tf_op jit(solution)/shard_map/ppermute | solution.py:92
  97.8 19.9 %copy-start.3 = (f32[288,128]{1,0:T(8,128)}, f32[288,128]{1,0:T(8,128)S(1)}, u32[]{:S(2)}) copy-start(f32[288,128]{1,0:T(8,128)S(1)} %collective-permute-done.13.refs_2_) | copy-start | bytes 442372
  97.9 19.9 %collective-permute-start.18 = (f32[288,128]{1,0:T(8,128)}, f32[288,128]{1,0:T(8,128)S(1)}, u32[]{:S(2)}, u32[]{:S(2)}) collective-permute-start(f32[288,128]{1,0:T(8,128)} %get-tuple-element.32), channel_id=1, source_target_pairs={{0,19},{1,23},{2,17},{3,21},{4,27},{5,31},{6,25},{7,29},{8,18},{9,... | collective-permute-start | bytes 442376 | tf_op jit(solution)/shard_map/ppermute | solution.py:92
  122.0 7.6 %collective-permute-start.21 = (f32[16,128]{1,0:T(8,128)}, f32[16,128]{1,0:T(8,128)S(1)}, u32[]{:S(2)}, u32[]{:S(2)}) collective-permute-start(f32[16,128]{1,0:T(8,128)} %gram.1), channel_id=1, source_target_pairs={{0,24},{1,25},{2,26},{3,27},{4,28},{5,29},{6,30},{7,31},{8,16},{9,... | collective-permute-start | bytes 24584 | tf_op jit(solution)/shard_map/ppermute | solution.py:92
  127.7 4.8 %collective-permute-start.20 = (f32[16,128]{1,0:T(8,128)}, f32[16,128]{1,0:T(8,128)S(1)}, u32[]{:S(2)}, u32[]{:S(2)}) collective-permute-start(f32[16,128]{1,0:T(8,128)} %gram.1), channel_id=1, source_target_pairs={{0,16},{1,17},{2,18},{3,19},{4,20},{5,21},{6,22},{7,23},{8,24},{9,... | collective-permute-start | bytes 24584 | tf_op jit(solution)/shard_map/ppermute | solution.py:92
  127.7 4.8 %collective-permute-start.19 = (f32[16,128]{1,0:T(8,128)}, f32[16,128]{1,0:T(8,128)S(1)}, u32[]{:S(2)}, u32[]{:S(2)}) collective-permute-start(f32[16,128]{1,0:T(8,128)} %gram.1), channel_id=1, source_target_pairs={{0,8},{1,9},{2,10},{3,11},{4,12},{5,13},{6,14},{7,15},{8,0},{9,1},... | collective-permute-start | bytes 24584 | tf_op jit(solution)/shard_map/ppermute | solution.py:92
  133.2 1.2 collective-permute-start.22
  134.4 4.5 %collective-permute-start.25 = (f32[16,128]{1,0:T(8,128)S(1)}, f32[16,128]{1,0:T(8,128)S(1)}, u32[]{:S(2)}, u32[]{:S(2)}) collective-permute-start(f32[16,128]{1,0:T(8,128)S(1)} %add.56), channel_id=1, source_target_pairs={{0,3},{1,2},{2,1},{3,0},{4,7},{5,6},{6,5},{7,4},{8,11},{9,10},{10,... | collective-permute-start | bytes 24584 | tf_op jit(solution)/shard_map/ppermute | solution.py:92
  134.4 4.5 %collective-permute-start.24 = (f32[16,128]{1,0:T(8,128)S(1)}, f32[16,128]{1,0:T(8,128)S(1)}, u32[]{:S(2)}, u32[]{:S(2)}) collective-permute-start(f32[16,128]{1,0:T(8,128)S(1)} %add.56), channel_id=1, source_target_pairs={{0,2},{1,3},{2,0},{3,1},{4,6},{5,7},{6,4},{7,5},{8,10},{9,11},{10,... | collective-permute-start | bytes 24584 | tf_op jit(solution)/shard_map/ppermute | solution.py:92
  135.8 3.7 %collective-permute-start.23 = (f32[16,128]{1,0:T(8,128)S(1)}, f32[16,128]{1,0:T(8,128)S(1)}, u32[]{:S(2)}, u32[]{:S(2)}) collective-permute-start(f32[16,128]{1,0:T(8,128)S(1)} %add.56), channel_id=1, source_target_pairs={{0,1},{1,0},{2,3},{3,2},{4,5},{5,4},{6,7},{7,6},{8,9},{9,8},{10,11... | collective-permute-start | bytes 24584 | tf_op jit(solution)/shard_map/ppermute | solution.py:92
  (9 other events, 53.8 us)
where the time goes:
time: 144 us; the launch traced here: 143 us
  waiting for transfers between devices  58.1 us (40%)
  starting transfers between devices  40.1 us (28%)
  Pallas kernels  37.4 us (26%)
  local copies, waits for them, and re-layouts  3.78 us (3%)
  other arithmetic  3.78 us (3%)
    ppermute x26, waiting for transfers between devices, hop(): return lax.ppermute(value, ('node', 'local'), pairs)  58.1 us
    ppermute x26, starting transfers between devices, hop(): return lax.ppermute(value, ('node', 'local'), pairs)  40.1 us
    pallas_call x1, Pallas kernels, tiles(): pl.pallas_call(residual_kernel, grid=(taps,), out_shape=(f32(rows, width)...  12.1 us
    pallas_call x1, Pallas kernels, tiles(): pl.pallas_call(lambda *refs: gradient_kernel(1.0 / rows, side, *refs), ou...  11.1 us
    unnamed x30, local copies, waits for them, and re-layouts  3.78 us
    pallas_call x1, Pallas kernels, tiles(): pl.pallas_call(pair_mix_kernel, out_shape=(f32(part, 128),) * count, in_s...  3.25 us
    pallas_call x1, Pallas kernels, tiles(): pl.pallas_call(place_kernel, out_shape=f32(HALF, 4 * part), in_specs=[SM,...  3.22 us
    pallas_call x1, Pallas kernels, tiles(): pl.pallas_call(gram_kernel, out_shape=f32(16, 128), in_specs=[SM] + [HB]...  2.92 us
  transfers between devices with their start and end apart: 26, of which 15 were waited for; matrix products, arithmetic and copies ran while one was open for 1% of the time, Pallas kernels for 2%

commit v1 on v0

--- a/solution.py
+++ b/solution.py
@@ -9,6 +9,7 @@
 epsilon = 1e-06
 HALF = 64
 BLK = 32
+FULL = 65 * 2**20
 
 
 def partner(value, axis, distance):
@@ -121,11 +122,22 @@
     return jnp.concatenate(evens, axis=1), jnp.concatenate(odds, axis=1)
 
 
-def split_kernel(s_ref, x_ref, own_ref, other_ref):
-    even, odd = lane_halves(x_ref[...])
+def split_kernel(s_ref, x_ref, own_ref, other_ref, buf, halves, in_sems, out_sems):
+    strips, strip, _ = buf.shape
+    spans = [pl.ds(r * strip, strip) for r in range(strips)]
+    copies = fetch([x_ref.at[span] for span in spans], [buf.at[r] for r in range(strips)], in_sems)
     up = s_ref[0] == 1
-    own_ref[...] = jnp.where(up, odd, even)
-    other_ref[...] = jnp.where(up, even, odd)
+    stores = []
+    for r in range(strips):
+        copies[r].wait()
+        even, odd = lane_halves(buf[r])
+        halves[2 * r] = jnp.where(up, odd, even)
+        halves[2 * r + 1] = jnp.where(up, even, odd)
+        for k, ref in enumerate((own_ref, other_ref)):
+            stores.append(pltpu.make_async_copy(halves.at[2 * r + k], ref.at[spans[r]], out_sems.at[2 * r + k]))
+            stores[-1].start()
+    for store in stores:
+        store.wait()
 
 
 def residual_kernel(s_ref, x_ref, t_ref, w_ref, own_ref, other_ref, pad_ref, acc_ref):
@@ -153,45 +165,52 @@
         other_ref[...] = jnp.where(up, even, odd)
 
 
-def gradient_kernel(
-    scale, side, s_ref, x0, x1, x2, x3, r0, r1, r2, r3, keep_ref, send_ref, xt, rh, rl, g_ref
-):
-    xs, rs = (x0, x1, x2, x3), (r0, r1, r2, r3)
-    rows, width = x0.shape
+def gradient_kernel(scale, side, s_ref, *refs):
+    sources, (keep_ref, send_ref, buf, xt, rh, rl, g_ref, sems) = refs[:8], refs[8:]
+    copies = fetch(sources, [buf.at[i] for i in range(8)], sems)
+    _, rows, width = buf.shape
     strip = rows // side
     imgs = strip // side
     span = (side + 1) * 4 * imgs
     for ref in (rh, rl):
         for edge in (0, side + 1, side + 2):
             ref[:, edge] = jnp.zeros((side, 4 * imgs, width), jnp.bfloat16)
+
+    def gather(base, r):
+        parts = [buf[base + i, r * strip : (r + 1) * strip, :].reshape(side, imgs, width) for i in range(4)]
+        return jnp.concatenate(parts, axis=1)
+
+    for copy in copies[:4]:
+        copy.wait()
     for r in range(side):
-        def gather(refs):
-            parts = [ref[r * strip : (r + 1) * strip, :].reshape(side, imgs, width) for ref in refs]
-            return jnp.concatenate(parts, axis=1)
-
-        rows_x = gather(xs).reshape(4 * strip, width)
+        rows_x = gather(0, r).reshape(4 * strip, width)
         rows_x = jnp.concatenate([rows_x, jnp.zeros((span - 4 * strip, width), jnp.float32)], axis=0)
         xh, xl = split2(rows_x.T)
         xt[r, :, 0:span] = xh
         xt[r, :, span : 2 * span] = xh
         xt[r, :, 2 * span : 3 * span] = xl
-        h, lo = split2(gather(rs))
+    for copy in copies[4:]:
+        copy.wait()
+    for r in range(side):
+        h, lo = split2(gather(4, r))
         rh[r, 1 : side + 1] = h
         rl[r, 1 : side + 1] = lo
 
     def column(j, carry):
+        totals = [None] * 3
+        for p in range(side):
+            first, last = max(p - 1, 0), min(p + 1, side - 1)
+            bh = rh[p, pl.ds(2 - j, side + 1)].reshape(span, width)
+            bl = rl[p, pl.ds(2 - j, side + 1)].reshape(span, width)
+            left = xt[first : last + 1].reshape((last + 1 - first) * width, 3 * span)
+            product = mm(left, jnp.concatenate([bh, bl, bh], axis=0))
+            for r in range(first, last + 1):
+                i = r - p + 1
+                part = product[(r - first) * width : (r - first + 1) * width]
+                totals[i] = part if totals[i] is None else totals[i] + part
+        per = width // BLK
         for i in range(3):
-            total = None
-            for r in range(side):
-                p = r - i + 1
-                if p < 0 or p >= side:
-                    continue
-                bh = rh[p, pl.ds(2 - j, side + 1)].reshape(span, width)
-                bl = rl[p, pl.ds(2 - j, side + 1)].reshape(span, width)
-                part = mm(xt[r], jnp.concatenate([bh, bl, bh], axis=0))
-                total = part if total is None else total + part
-            per = width // BLK
-            g_ref[pl.ds((3 * i + j) * per, per)] = (total * scale).reshape(per, BLK, width)
+            g_ref[pl.ds((3 * i + j) * per, per)] = (totals[i] * scale).reshape(per, BLK, width)
         return carry
 
     lax.fori_loop(0, 3, column, 0)
@@ -239,18 +258,23 @@
     out_ref[2:3] = jnp.where(core == 0, theirs, mine)
 
 
+def sum_four(refs):
+    return (refs[0][...] + refs[1][...]) + (refs[2][...] + refs[3][...])
+
+
 def pair_coefs(cross, left_sq, right_sq):
     return 1.0 - cross / (2.0 * (left_sq + epsilon)), 1.0 - cross / (2.0 * (right_sq + epsilon))
 
 
-def pair_mix_kernel(s_ref, totals_ref, keep_ref, received_ref, *refs):
+def pair_mix_kernel(s_ref, t0, t1, t2, t3, keep_ref, received_ref, *refs):
+    totals_refs = (t0, t1, t2, t3)
     core = s_ref[0]
     count = keep_ref.shape[0]
     out_refs, (buf, in_sems, out_sems) = refs[:count], refs[count:]
     order = list(range(count - 1, -1, -1))
     sources = [ref.at[d] for d in order for ref in (keep_ref, received_ref)]
     copies = fetch(sources, [buf.at[i] for i in range(2 * count)], in_sems)
-    totals = jnp.sum(totals_ref[...], axis=1, keepdims=True)
+    totals = jnp.sum(sum_four(totals_refs), axis=1, keepdims=True)
     left, right = pair_coefs(totals[0:1], totals[1:2], totals[2:3])
     keep_coef = jnp.where(core == 0, left, right)
     received_coef = jnp.where(core == 0, right, left)
@@ -284,11 +308,11 @@
     return 4 * e + 2 * dx + dy
 
 
-def place_kernel(s_ref, gram_ref, *refs):
+def place_kernel(s_ref, g0, g1, g2, g3, *refs):
     upper, x, y = s_ref[0], s_ref[1], s_ref[2]
     blocks, (out_ref, parts, rows_ref, sems) = refs[:8], refs[8:]
     copies = fetch(blocks, [parts.at[slot_of(i)] for i in range(8)], sems)
-    gram = jnp.sum(gram_ref[...], axis=1, keepdims=True)
+    gram = jnp.sum(sum_four((g0, g1, g2, g3)), axis=1, keepdims=True)
     g = lambda a, b: gram[4 * a + b : 4 * a + b + 1]
     p = pair_coefs(g(0, 1), g(0, 0), g(1, 1)) + pair_coefs(g(2, 3), g(2, 2), g(3, 3))
     cross = p[0] * (p[2] * g(0, 2) + p[3] * g(0, 3)) + p[1] * (p[2] * g(1, 2) + p[3] * g(1, 3))
@@ -346,8 +370,14 @@
     x_own, x_other = pl.pallas_call(
         split_kernel,
         out_shape=(f32(rows, width), f32(rows, width)),
-        in_specs=[SM, VM],
-        out_specs=(VM, VM),
+        in_specs=[SM, HB],
+        out_specs=(HB, HB),
+        scratch_shapes=[
+            pltpu.VMEM((side, rows // side, channels), jnp.float32),
+            pltpu.VMEM((2 * side, rows // side, width), jnp.float32),
+            pltpu.SemaphoreType.DMA((side,)),
+            pltpu.SemaphoreType.DMA((2 * side,)),
+        ],
         name="split_images",
     )(scalars(y), xt.reshape(rows, channels))
     x_y = hop(x_other, lambda z, c, y, x: (z, c, 1 - y, x))
@@ -388,17 +418,20 @@
     keep, send = pl.pallas_call(
         lambda *refs: gradient_kernel(1.0 / rows, side, *refs),
         out_shape=(f32(count, part, 128), f32(count, part, 128)),
-        in_specs=[SM] + [VM] * 8,
+        in_specs=[SM] + [HB] * 8,
         out_specs=(VM, VM),
         scratch_shapes=[
+            pltpu.VMEM((8, rows, width), jnp.float32),
             pltpu.VMEM((side, width, 3 * (side + 1) * 4 * imgs), jnp.bfloat16),
             pltpu.VMEM((side, side + 3, 4 * imgs, width), jnp.bfloat16),
             pltpu.VMEM((side, side + 3, 4 * imgs, width), jnp.bfloat16),
             pltpu.VMEM((taps * width // BLK, BLK, width), jnp.float32),
+            pltpu.SemaphoreType.DMA((8,)),
         ],
         cost_estimate=pl.CostEstimate(
             flops=24 * rows * taps * width * width, bytes_accessed=4 * taps * width * width, transcendentals=0
         ),
+        compiler_params=pltpu.CompilerParams(vmem_limit_bytes=FULL),
         name="gradient",
     )(scalars(c, z // 2, y, z % 2), x_own, x_x, x_y, x_d, r_own, r_x, r_y, r_d)
 
@@ -409,21 +442,23 @@
         in_specs=[SM, HB, HB],
         out_specs=VM,
         scratch_shapes=[pltpu.VMEM((2 * count, part, 128), jnp.float32), pltpu.SemaphoreType.DMA((2 * count,))],
+        compiler_params=pltpu.CompilerParams(vmem_limit_bytes=FULL),
         name="pair_dots",
     )(scalars(c), keep, received)
     totals = plane_sum(totals)
     blocks = pl.pallas_call(
         pair_mix_kernel,
         out_shape=(f32(part, 128),) * count,
-        in_specs=[SM, VM, HB, HB],
+        in_specs=[SM] + [VM] * 4 + [HB, HB],
         out_specs=(HB,) * count,
         scratch_shapes=[
             pltpu.VMEM((2 * count, part, 128), jnp.float32),
             pltpu.SemaphoreType.DMA((2 * count,)),
             pltpu.SemaphoreType.DMA((count,)),
         ],
+        compiler_params=pltpu.CompilerParams(vmem_limit_bytes=FULL),
         name="pair_mix",
-    )(scalars(c), totals, keep, received)
+    )(scalars(c), *totals, keep, received)
 
     moved = []
     for index in range(count):
@@ -436,6 +471,7 @@
         in_specs=[SM] + [HB] * count,
         out_specs=VM,
         scratch_shapes=[pltpu.VMEM((count, part, 128), jnp.float32), pltpu.SemaphoreType.DMA((count,))],
+        compiler_params=pltpu.CompilerParams(vmem_limit_bytes=FULL),
         name="gram",
     )(place, *moved)
     along = [hop(gram, lambda z, c, y, x, d=d: (z ^ d, c, y, x)) for d in range(1, z_count)]
@@ -443,22 +479,23 @@
     out = pl.pallas_call(
         place_kernel,
         out_shape=f32(HALF, 4 * part),
-        in_specs=[SM, VM] + [HB] * count,
+        in_specs=[SM] + [VM] * 4 + [HB] * count,
         out_specs=VM,
         scratch_shapes=[
             pltpu.VMEM((count, part, 128), jnp.float32),
             pltpu.VMEM((2 * part // HALF, 2, HALF, HALF), jnp.float32),
             pltpu.SemaphoreType.DMA((count,)),
         ],
+        compiler_params=pltpu.CompilerParams(vmem_limit_bytes=FULL),
         name="place",
-    )(place, gram, *moved)
+    )(place, *gram, *moved)
     return out.T
 
 
 def plane_sum(value):
     value = value + hop(value, lambda z, c, y, x: (z, 1 - c, y, x))
     across = [hop(value, lambda z, c, y, x, d=d: (z, c, y ^ (d >> 1), x ^ (d & 1))) for d in (1, 2, 3)]
-    return (value + across[0]) + (across[1] + across[2])
+    return [value] + across
 
 
 def fits(images, mesh):

time: 144 us -> 142 us (0.986)
  local copies, waits for them, and re-layouts: 3.78 us -> 1.75 us
    unnamed x30 -> x12, local copies, waits for them, and re-layouts: 3.78 us -> 1.75 us
  transfers between devices with their start and end apart: 26 -> 26, of which waited for: 15 -> 14; matrix products, arithmetic and copies ran while one was open for 1% -> 1% of each run, Pallas kernels for 2% -> 2%
where the time goes in v1:
time: 142 us; the launch traced here: 141 us
  waiting for transfers between devices  57.9 us (41%)
  starting transfers between devices  41.2 us (29%)
  Pallas kernels  37.8 us (27%)
  other arithmetic  2.63 us (2%)
  local copies, waits for them, and re-layouts  1.75 us (1%)
    ppermute x26, waiting for transfers between devices, hop(): return lax.ppermute(value, ('node', 'local'), pairs)  57.9 us
    ppermute x26, starting transfers between devices, hop(): return lax.ppermute(value, ('node', 'local'), pairs)  41.2 us
    pallas_call x1, Pallas kernels, tiles(): pl.pallas_call(residual_kernel, grid=(taps,), out_shape=(f32(rows, width)...  12.1 us
    pallas_call x1, Pallas kernels, tiles(): pl.pallas_call(lambda *refs: gradient_kernel(1.0 / rows, side, *refs), ou...  11.2 us
    pallas_call x1, Pallas kernels, tiles(): pl.pallas_call(place_kernel, out_shape=f32(HALF, 4 * part), in_specs=[SM]...  3.32 us
    pallas_call x1, Pallas kernels, tiles(): pl.pallas_call(pair_mix_kernel, out_shape=(f32(part, 128),) * count, in_s...  3.28 us
    pallas_call x1, Pallas kernels, tiles(): pl.pallas_call(gram_kernel, out_shape=f32(16, 128), in_specs=[SM] + [HB]...  2.92 us
  transfers between devices with their start and end apart: 26, of which 14 were waited for; matrix products, arithmetic and copies ran while one was open for 1% of the time, Pallas kernels for 2%

profile of v1, /device:TPU:0, one launch (start us, length us, event | category | flops | bytes accessed | tf_op | source)
XLA Modules:
  0.0 141.3 jit_solution(16307632521076206119)
XLA Ops:
  0.0 12.1 %residual.1 = (f32[392,256]{1,0:T(8,128)}, f32[392,256]{1,0:T(8,128)}) custom-call(s32[1]{0:T(128)} %bitcast.1.s_ref, f32[7,7,8,512]{3,2,1,0:T(8,128)} %bitcast.13, f32[392,512]{1,0:T(8,128)} %bitcast.16, f32[9,512,512]{2,1,0:T(8,128)} %bitcast.15), custom_call_target="tpu_custom_call" | custom-call | flops 5549064192 | bytes 9437184 | tf_op jit(solution)/shard_map/residual/pallas_call | solution.py:390
  12.1 3.0 %collective-permute-start.4 = (f32[392,256]{1,0:T(8,128)}, f32[392,256]{1,0:T(8,128)}, u32[]{:S(2)}, u32[]{:S(2)}) collective-permute-start(f32[392,256]{1,0:T(8,128)} %get-tuple-element.21.refs_5_), channel_id=1, source_target_pairs={{0,2},{1,3},{2,0},{3,1},{4,6},{5,7},{6,4},{7,5},{8,10},{9,11},{10,... | collective-permute-start | bytes 1204232 | tf_op jit(solution)/shard_map/ppermute | solution.py:93
  15.1 1.4 %collective-permute-start.5 = (f32[392,256]{1,0:T(8,128)}, f32[392,256]{1,0:T(8,128)}, u32[]{:S(2)}, u32[]{:S(2)}) collective-permute-start(f32[392,256]{1,0:T(8,128)} %get-tuple-element.22), channel_id=1, source_target_pairs={{0,3},{1,2},{2,1},{3,0},{4,7},{5,6},{6,5},{7,4},{8,11},{9,10},{10,... | collective-permute-start | bytes 1204232 | tf_op jit(solution)/shard_map/ppermute | solution.py:93
  16.6 2.4 %split_images.1 = (f32[392,256]{1,0:T(8,128)}, f32[392,256]{1,0:T(8,128)}) custom-call(s32[1]{0:T(128)} %bitcast.2.s_ref, f32[392,512]{1,0:T(8,128)} %bitcast.14), custom_call_target="tpu_custom_call" | custom-call | tf_op jit(solution)/shard_map/split_images/pallas_call | solution.py:370
  19.1 2.0 %collective-permute-start = (f32[392,256]{1,0:T(8,128)}, f32[392,256]{1,0:T(8,128)}, u32[]{:S(2)}, u32[]{:S(2)}) collective-permute-start(f32[392,256]{1,0:T(8,128)} %get-tuple-element.19.refs_1_), channel_id=1, source_target_pairs={{0,1},{1,0},{2,3},{3,2},{4,5},{5,4},{6,7},{7,6},{8,9},{9,8},{10,11... | collective-permute-start | bytes 1204232 | tf_op jit(solution)/shard_map/ppermute | solution.py:93
  21.1 1.5 %collective-permute-start.2 = (f32[392,256]{1,0:T(8,128)}, f32[392,256]{1,0:T(8,128)}, u32[]{:S(2)}, u32[]{:S(2)}) collective-permute-start(f32[392,256]{1,0:T(8,128)} %get-tuple-element.20), channel_id=1, source_target_pairs={{0,3},{1,2},{2,1},{3,0},{4,7},{5,6},{6,5},{7,4},{8,11},{9,10},{10,... | collective-permute-start | bytes 1204232 | tf_op jit(solution)/shard_map/ppermute | solution.py:93
  22.6 10.7 %collective-permute-done.4.refs_7_ = f32[392,256]{1,0:T(8,128)} collective-permute-done((f32[392,256]{1,0:T(8,128)}, f32[392,256]{1,0:T(8,128)}, u32[]{:S(2)}, u32[]{:S(2)}) %collective-permute-start.4) | collective-permute-done | bytes 401440 | tf_op jit(solution)/shard_map/ppermute | solution.py:93
  33.3 1.7 %collective-permute-start.1 = (f32[392,256]{1,0:T(8,128)}, f32[392,256]{1,0:T(8,128)}, u32[]{:S(2)}, u32[]{:S(2)}) collective-permute-start(f32[392,256]{1,0:T(8,128)} %get-tuple-element.20), channel_id=1, source_target_pairs={{0,2},{1,3},{2,0},{3,1},{4,6},{5,7},{6,4},{7,5},{8,10},{9,11},{10,... | collective-permute-start | bytes 1204232 | tf_op jit(solution)/shard_map/ppermute | solution.py:93
  35.7 8.6 %collective-permute-done.refs_2_ = f32[392,256]{1,0:T(8,128)} collective-permute-done((f32[392,256]{1,0:T(8,128)}, f32[392,256]{1,0:T(8,128)}, u32[]{:S(2)}, u32[]{:S(2)}) %collective-permute-start) | collective-permute-done | bytes 401440 | tf_op jit(solution)/shard_map/ppermute | solution.py:93
  44.3 8.7 %collective-permute-done.2.refs_4_ = f32[392,256]{1,0:T(8,128)} collective-permute-done((f32[392,256]{1,0:T(8,128)}, f32[392,256]{1,0:T(8,128)}, u32[]{:S(2)}, u32[]{:S(2)}) %collective-permute-start.2) | collective-permute-done | bytes 401440 | tf_op jit(solution)/shard_map/ppermute | solution.py:93
  52.9 11.2 %gradient.1 = (f32[8,288,128]{2,1,0:T(8,128)}, f32[8,288,128]{2,1,0:T(8,128)}) custom-call(s32[4]{0:T(128)} %pad_add_fusion.1.refs_0_, f32[392,256]{1,0:T(8,128)} %get-tuple-element.19.refs_1_, f32[392,256]{1,0:T(8,128)} %collective-permute-done.refs_2_, f32[392,256]{1,0:T(8,128)} %collective-permute-done.1.refs_3_, ...), custom_call_target="tpu_custom_call" | custom-call | flops 5549064192 | bytes 2359296 | tf_op jit(solution)/shard_map/gradient/pallas_call | solution.py:418
  64.3 3.2 %collective-permute-done.6.received_ref = f32[8,288,128]{2,1,0:T(8,128)} collective-permute-done((f32[8,288,128]{2,1,0:T(8,128)}, f32[8,288,128]{2,1,0:T(8,128)}, u32[]{:S(2)}, u32[]{:S(2)}) %collective-permute-start.6) | collective-permute-done | bytes 1179680 | tf_op jit(solution)/shard_map/ppermute | solution.py:93
  67.5 2.5 %pair_dots.1 = f32[8,128]{1,0:T(8,128)} custom-call(s32[1]{0:T(128)} %bitcast.3.s_ref, f32[8,288,128]{2,1,0:T(8,128)} %get-tuple-element.23.keep_ref, f32[8,288,128]{2,1,0:T(8,128)} %collective-permute-done.6.received_ref), custom_call_target="tpu_custom_call" | custom-call | tf_op jit(solution)/shard_map/pair_dots/pallas_call | solution.py:439
  70.1 1.2 collective-permute-done.7
  72.1 2.1 %collective-permute-start.10 = (f32[8,128]{1,0:T(8,128)S(1)}, f32[8,128]{1,0:T(8,128)S(1)}, u32[]{:S(2)}, u32[]{:S(2)}) collective-permute-start(f32[8,128]{1,0:T(8,128)S(1)} %add.31.t0), channel_id=1, source_target_pairs={{0,3},{1,2},{2,1},{3,0},{4,7},{5,6},{6,5},{7,4},{8,11},{9,10},{10,... | collective-permute-start | bytes 12296 | tf_op jit(solution)/shard_map/ppermute | solution.py:93
  76.6 1.2 collective-permute-done.9.t2
  78.7 3.3 %pair_mix.1 = (f32[288,128]{1,0:T(8,128)}, f32[288,128]{1,0:T(8,128)}, f32[288,128]{1,0:T(8,128)}, f32[288,128]{1,0:T(8,128)}, f32[288,128]{1,0:T(8,128)}, /*ind...) custom-call(s32[1]{0:T(128)} %bitcast.3.s_ref, f32[8,128]{1,0:T(8,128)} %copy-done.1, ...), custom_call_target="tpu_custom_call" | custom-call | tf_op jit(solution)/shard_map/pair_mix/pallas_call | solution.py:449
  82.0 2.8 %collective-permute-start.11 = (f32[288,128]{1,0:T(8,128)}, f32[288,128]{1,0:T(8,128)}, u32[]{:S(2)}, u32[]{:S(2)}) collective-permute-start(f32[288,128]{1,0:T(8,128)} %get-tuple-element.25), channel_id=1, source_target_pairs={{0,0},{1,4},{2,2},{3,6},{4,8},{5,12},{6,10},{7,14},{8,1},{9,5},{10... | collective-permute-start | bytes 442376 | tf_op jit(solution)/shard_map/ppermute | solution.py:93
  84.9 1.2 collective-permute-start.13
  86.1 2.2 %collective-permute-start.14 = (f32[288,128]{1,0:T(8,128)}, f32[288,128]{1,0:T(8,128)}, u32[]{:S(2)}, u32[]{:S(2)}) collective-permute-start(f32[288,128]{1,0:T(8,128)} %get-tuple-element.28), channel_id=1, source_target_pairs={{0,3},{1,7},{2,1},{3,5},{4,11},{5,15},{6,9},{7,13},{8,2},{9,6},{10... | collective-permute-start | bytes 442376 | tf_op jit(solution)/shard_map/ppermute | solution.py:93
  88.3 2.6 %collective-permute-start.15 = (f32[288,128]{1,0:T(8,128)}, f32[288,128]{1,0:T(8,128)}, u32[]{:S(2)}, u32[]{:S(2)}) collective-permute-start(f32[288,128]{1,0:T(8,128)} %get-tuple-element.29), channel_id=1, source_target_pairs={{0,16},{1,20},{2,18},{3,22},{4,24},{5,28},{6,26},{7,30},{8,17},{9,... | collective-permute-start | bytes 442376 | tf_op jit(solution)/shard_map/ppermute | solution.py:93
  90.9 2.1 %collective-permute-start.16 = (f32[288,128]{1,0:T(8,128)}, f32[288,128]{1,0:T(8,128)}, u32[]{:S(2)}, u32[]{:S(2)}) collective-permute-start(f32[288,128]{1,0:T(8,128)} %get-tuple-element.30), channel_id=1, source_target_pairs={{0,17},{1,21},{2,19},{3,23},{4,25},{5,29},{6,27},{7,31},{8,16},{9,... | collective-permute-start | bytes 442376 | tf_op jit(solution)/shard_map/ppermute | solution.py:93
  93.0 2.3 %collective-permute-start.17 = (f32[288,128]{1,0:T(8,128)}, f32[288,128]{1,0:T(8,128)}, u32[]{:S(2)}, u32[]{:S(2)}) collective-permute-start(f32[288,128]{1,0:T(8,128)} %get-tuple-element.31), channel_id=1, source_target_pairs={{0,18},{1,22},{2,16},{3,20},{4,26},{5,30},{6,24},{7,28},{8,19},{9,... | collective-permute-start | bytes 442376 | tf_op jit(solution)/shard_map/ppermute | solution.py:93
  95.3 3.5 %collective-permute-start.18 = (f32[288,128]{1,0:T(8,128)}, f32[288,128]{1,0:T(8,128)}, u32[]{:S(2)}, u32[]{:S(2)}) collective-permute-start(f32[288,128]{1,0:T(8,128)} %get-tuple-element.32), channel_id=1, source_target_pairs={{0,19},{1,23},{2,17},{3,21},{4,27},{5,31},{6,25},{7,29},{8,18},{9,... | collective-permute-start | bytes 442376 | tf_op jit(solution)/shard_map/ppermute | solution.py:93
  99.3 5.5 %collective-permute-done.16.refs_5_ = f32[288,128]{1,0:T(8,128)} collective-permute-done((f32[288,128]{1,0:T(8,128)}, f32[288,128]{1,0:T(8,128)}, u32[]{:S(2)}, u32[]{:S(2)}) %collective-permute-start.16) | collective-permute-done | bytes 147488 | tf_op jit(solution)/shard_map/ppermute | solution.py:93
  104.8 11.1 %collective-permute-done.17.refs_6_ = f32[288,128]{1,0:T(8,128)} collective-permute-done((f32[288,128]{1,0:T(8,128)}, f32[288,128]{1,0:T(8,128)}, u32[]{:S(2)}, u32[]{:S(2)}) %collective-permute-start.17) | collective-permute-done | bytes 147488 | tf_op jit(solution)/shard_map/ppermute | solution.py:93
  115.9 2.9 %gram.1 = f32[16,128]{1,0:T(8,128)} custom-call(s32[3]{0:T(128)} %pad_add_fusion.s_ref, f32[288,128]{1,0:T(8,128)} %collective-permute-done.11.refs_0_, f32[288,128]{1,0:T(8,128)} %collective-permute-done.12.refs_1_, f32[288,128]{1,0:T(8,128)} %collective-permute-done.13.refs_2_, f32[288,128]{1,0:T(8,128)} %collective-permute-done.14.refs_3_, ...), custom_call_target="tpu_custom_call" | custom-call | tf_op jit(solution)/shard_map/gram/pallas_call | solution.py:468
  118.8 6.9 %collective-permute-start.21 = (f32[16,128]{1,0:T(8,128)}, f32[16,128]{1,0:T(8,128)S(1)}, u32[]{:S(2)}, u32[]{:S(2)}) collective-permute-start(f32[16,128]{1,0:T(8,128)} %gram.1), channel_id=1, source_target_pairs={{0,24},{1,25},{2,26},{3,27},{4,28},{5,29},{6,30},{7,31},{8,16},{9,... | collective-permute-start | bytes 24584 | tf_op jit(solution)/shard_map/ppermute | solution.py:93
  126.3 1.2 collective-permute-done.21
  127.5 2.9 %collective-permute-done.20 = f32[16,128]{1,0:T(8,128)S(1)} collective-permute-done((f32[16,128]{1,0:T(8,128)}, f32[16,128]{1,0:T(8,128)S(1)}, u32[]{:S(2)}, u32[]{:S(2)}) %collective-permute-start.20) | collective-permute-done | bytes 8224 | tf_op jit(solution)/shard_map/ppermute | solution.py:93
  133.2 2.6 %collective-permute-start.23 = (f32[16,128]{1,0:T(8,128)S(1)}, f32[16,128]{1,0:T(8,128)}, u32[]{:S(2)}, u32[]{:S(2)}) collective-permute-start(f32[16,128]{1,0:T(8,128)S(1)} %add.35.g0), channel_id=1, source_target_pairs={{0,1},{1,0},{2,3},{3,2},{4,5},{5,4},{6,7},{7,6},{8,9},{9,8},{10,11... | collective-permute-start | bytes 24584 | tf_op jit(solution)/shard_map/ppermute | solution.py:93
  138.0 3.3 %place.1 = f32[64,1152]{1,0:T(8,128)} custom-call(s32[3]{0:T(128)} %pad_add_fusion.s_ref, f32[16,128]{1,0:T(8,128)} %copy-done, f32[16,128]{1,0:T(8,128)} %collective-permute-done.23.g1, f32[16,128]{1,0:T(8,128)} %copy-done.3, f32[16,128]{1,0:T(8,128)} %copy-done.2, f32[288,128]{1,0:T(8,128)} %collective-permute-done.11.refs_0_, ...), custom_call_target="tpu_custom_call" | custom-call | tf_op jit(solution)/shard_map/place/pallas_call | solution.py:479
  (44 shorter events, 11.2 us)
Async XLA Ops:
  12.1 21.2 %collective-permute-start.4 = (f32[392,256]{1,0:T(8,128)}, f32[392,256]{1,0:T(8,128)}, u32[]{:S(2)}, u32[]{:S(2)}) collective-permute-start(f32[392,256]{1,0:T(8,128)} %get-tuple-element.21.refs_5_), channel_id=1, source_target_pairs={{0,2},{1,3},{2,0},{3,1},{4,6},{5,7},{6,4},{7,5},{8,10},{9,11},{10,... | collective-permute-start | bytes 1204232 | tf_op jit(solution)/shard_map/ppermute | solution.py:93
  15.1 20.6 %collective-permute-start.5 = (f32[392,256]{1,0:T(8,128)}, f32[392,256]{1,0:T(8,128)}, u32[]{:S(2)}, u32[]{:S(2)}) collective-permute-start(f32[392,256]{1,0:T(8,128)} %get-tuple-element.22), channel_id=1, source_target_pairs={{0,3},{1,2},{2,1},{3,0},{4,7},{5,6},{6,5},{7,4},{8,11},{9,10},{10,... | collective-permute-start | bytes 1204232 | tf_op jit(solution)/shard_map/ppermute | solution.py:93
  16.6 19.2 %collective-permute-start.3 = (f32[392,256]{1,0:T(8,128)}, f32[392,256]{1,0:T(8,128)}, u32[]{:S(2)}, u32[]{:S(2)}) collective-permute-start(f32[392,256]{1,0:T(8,128)} %get-tuple-element.22), channel_id=1, source_target_pairs={{0,1},{1,0},{2,3},{3,2},{4,5},{5,4},{6,7},{7,6},{8,9},{9,8},{10,11... | collective-permute-start | bytes 1204232 | tf_op jit(solution)/shard_map/ppermute | solution.py:93
  19.1 25.2 %collective-permute-start = (f32[392,256]{1,0:T(8,128)}, f32[392,256]{1,0:T(8,128)}, u32[]{:S(2)}, u32[]{:S(2)}) collective-permute-start(f32[392,256]{1,0:T(8,128)} %get-tuple-element.19.refs_1_), channel_id=1, source_target_pairs={{0,1},{1,0},{2,3},{3,2},{4,5},{5,4},{6,7},{7,6},{8,9},{9,8},{10,11... | collective-permute-start | bytes 1204232 | tf_op jit(solution)/shard_map/ppermute | solution.py:93
  21.1 31.8 %collective-permute-start.2 = (f32[392,256]{1,0:T(8,128)}, f32[392,256]{1,0:T(8,128)}, u32[]{:S(2)}, u32[]{:S(2)}) collective-permute-start(f32[392,256]{1,0:T(8,128)} %get-tuple-element.20), channel_id=1, source_target_pairs={{0,3},{1,2},{2,1},{3,0},{4,7},{5,6},{6,5},{7,4},{8,11},{9,10},{10,... | collective-permute-start | bytes 1204232 | tf_op jit(solution)/shard_map/ppermute | solution.py:93
  33.3 19.6 %collective-permute-start.1 = (f32[392,256]{1,0:T(8,128)}, f32[392,256]{1,0:T(8,128)}, u32[]{:S(2)}, u32[]{:S(2)}) collective-permute-start(f32[392,256]{1,0:T(8,128)} %get-tuple-element.20), channel_id=1, source_target_pairs={{0,2},{1,3},{2,0},{3,1},{4,6},{5,7},{6,4},{7,5},{8,10},{9,11},{10,... | collective-permute-start | bytes 1204232 | tf_op jit(solution)/shard_map/ppermute | solution.py:93
  64.2 3.3 %collective-permute-start.6 = (f32[8,288,128]{2,1,0:T(8,128)}, f32[8,288,128]{2,1,0:T(8,128)}, u32[]{:S(2)}, u32[]{:S(2)}) collective-permute-start(f32[8,288,128]{2,1,0:T(8,128)} %get-tuple-element.24), channel_id=1, source_target_pairs={{0,4},{1,5},{2,6},{3,7},{4,0},{5,1},{6,2},{7,3},{8,12},{9,13},{10,... | collective-permute-start | bytes 3538952 | tf_op jit(solution)/shard_map/ppermute | solution.py:93
  69.9 1.4 %collective-permute-start.7 = (f32[8,128]{1,0:T(8,128)}, f32[8,128]{1,0:T(8,128)S(1)}, u32[]{:S(2)}, u32[]{:S(2)}) collective-permute-start(f32[8,128]{1,0:T(8,128)} %pair_dots.1), channel_id=1, source_target_pairs={{0,4},{1,5},{2,6},{3,7},{4,0},{5,1},{6,2},{7,3},{8,12},{9,13},{10,... | collective-permute-start | bytes 12296 | tf_op jit(solution)/shard_map/ppermute | solution.py:93
  72.1 3.0 %copy-start.1 = (f32[8,128]{1,0:T(8,128)}, f32[8,128]{1,0:T(8,128)S(1)}, u32[]{:S(2)}) copy-start(f32[8,128]{1,0:T(8,128)S(1)} %add.31.t0) | copy-start | bytes 12292
  72.1 4.5 %collective-permute-start.10 = (f32[8,128]{1,0:T(8,128)S(1)}, f32[8,128]{1,0:T(8,128)S(1)}, u32[]{:S(2)}, u32[]{:S(2)}) collective-permute-start(f32[8,128]{1,0:T(8,128)S(1)} %add.31.t0), channel_id=1, source_target_pairs={{0,3},{1,2},{2,1},{3,0},{4,7},{5,6},{6,5},{7,4},{8,11},{9,10},{10,... | collective-permute-start | bytes 12296 | tf_op jit(solution)/shard_map/ppermute | solution.py:93
  74.2 3.6 %collective-permute-start.9 = (f32[8,128]{1,0:T(8,128)S(1)}, f32[8,128]{1,0:T(8,128)S(1)}, u32[]{:S(2)}, u32[]{:S(2)}) collective-permute-start(f32[8,128]{1,0:T(8,128)S(1)} %add.31.t0), channel_id=1, source_target_pairs={{0,2},{1,3},{2,0},{3,1},{4,6},{5,7},{6,4},{7,5},{8,10},{9,11},{10,... | collective-permute-start | bytes 12296 | tf_op jit(solution)/shard_map/ppermute | solution.py:93
  75.0 3.7 %collective-permute-start.8 = (f32[8,128]{1,0:T(8,128)S(1)}, f32[8,128]{1,0:T(8,128)}, u32[]{:S(2)}, u32[]{:S(2)}) collective-permute-start(f32[8,128]{1,0:T(8,128)S(1)} %add.31.t0), channel_id=1, source_target_pairs={{0,1},{1,0},{2,3},{3,2},{4,5},{5,4},{6,7},{7,6},{8,9},{9,8},{10,11... | collective-permute-start | bytes 12296 | tf_op jit(solution)/shard_map/ppermute | solution.py:93
  76.6 1.2 copy-start.4
  77.8 0.6 copy-start.5
  82.0 8.9 %collective-permute-start.11 = (f32[288,128]{1,0:T(8,128)}, f32[288,128]{1,0:T(8,128)}, u32[]{:S(2)}, u32[]{:S(2)}) collective-permute-start(f32[288,128]{1,0:T(8,128)} %get-tuple-element.25), channel_id=1, source_target_pairs={{0,0},{1,4},{2,2},{3,6},{4,8},{5,12},{6,10},{7,14},{8,1},{9,5},{10... | collective-permute-start | bytes 442376 | tf_op jit(solution)/shard_map/ppermute | solution.py:93
  84.9 8.1 %collective-permute-start.12 = (f32[288,128]{1,0:T(8,128)}, f32[288,128]{1,0:T(8,128)}, u32[]{:S(2)}, u32[]{:S(2)}) collective-permute-start(f32[288,128]{1,0:T(8,128)} %get-tuple-element.26), channel_id=1, source_target_pairs={{0,1},{1,5},{2,3},{3,7},{4,9},{5,13},{6,11},{7,15},{8,0},{9,4},{10... | collective-permute-start | bytes 442376 | tf_op jit(solution)/shard_map/ppermute | solution.py:93
  84.9 10.4 %collective-permute-start.13 = (f32[288,128]{1,0:T(8,128)}, f32[288,128]{1,0:T(8,128)}, u32[]{:S(2)}, u32[]{:S(2)}) collective-permute-start(f32[288,128]{1,0:T(8,128)} %get-tuple-element.27), channel_id=1, source_target_pairs={{0,2},{1,6},{2,0},{3,4},{4,10},{5,14},{6,8},{7,12},{8,3},{9,7},{10... | collective-permute-start | bytes 442376 | tf_op jit(solution)/shard_map/ppermute | solution.py:93
  86.1 13.2 %collective-permute-start.14 = (f32[288,128]{1,0:T(8,128)}, f32[288,128]{1,0:T(8,128)}, u32[]{:S(2)}, u32[]{:S(2)}) collective-permute-start(f32[288,128]{1,0:T(8,128)} %get-tuple-element.28), channel_id=1, source_target_pairs={{0,3},{1,7},{2,1},{3,5},{4,11},{5,15},{6,9},{7,13},{8,2},{9,6},{10... | collective-permute-start | bytes 442376 | tf_op jit(solution)/shard_map/ppermute | solution.py:93
  88.3 11.0 %collective-permute-start.15 = (f32[288,128]{1,0:T(8,128)}, f32[288,128]{1,0:T(8,128)}, u32[]{:S(2)}, u32[]{:S(2)}) collective-permute-start(f32[288,128]{1,0:T(8,128)} %get-tuple-element.29), channel_id=1, source_target_pairs={{0,16},{1,20},{2,18},{3,22},{4,24},{5,28},{6,26},{7,30},{8,17},{9,... | collective-permute-start | bytes 442376 | tf_op jit(solution)/shard_map/ppermute | solution.py:93
  90.9 13.9 %collective-permute-start.16 = (f32[288,128]{1,0:T(8,128)}, f32[288,128]{1,0:T(8,128)}, u32[]{:S(2)}, u32[]{:S(2)}) collective-permute-start(f32[288,128]{1,0:T(8,128)} %get-tuple-element.30), channel_id=1, source_target_pairs={{0,17},{1,21},{2,19},{3,23},{4,25},{5,29},{6,27},{7,31},{8,16},{9,... | collective-permute-start | bytes 442376 | tf_op jit(solution)/shard_map/ppermute | solution.py:93
  93.0 22.9 %collective-permute-start.17 = (f32[288,128]{1,0:T(8,128)}, f32[288,128]{1,0:T(8,128)}, u32[]{:S(2)}, u32[]{:S(2)}) collective-permute-start(f32[288,128]{1,0:T(8,128)} %get-tuple-element.31), channel_id=1, source_target_pairs={{0,18},{1,22},{2,16},{3,20},{4,26},{5,30},{6,24},{7,28},{8,19},{9,... | collective-permute-start | bytes 442376 | tf_op jit(solution)/shard_map/ppermute | solution.py:93
  95.3 20.6 %collective-permute-start.18 = (f32[288,128]{1,0:T(8,128)}, f32[288,128]{1,0:T(8,128)}, u32[]{:S(2)}, u32[]{:S(2)}) collective-permute-start(f32[288,128]{1,0:T(8,128)} %get-tuple-element.32), channel_id=1, source_target_pairs={{0,19},{1,23},{2,17},{3,21},{4,27},{5,31},{6,25},{7,29},{8,18},{9,... | collective-permute-start | bytes 442376 | tf_op jit(solution)/shard_map/ppermute | solution.py:93
  118.8 8.7 %collective-permute-start.21 = (f32[16,128]{1,0:T(8,128)}, f32[16,128]{1,0:T(8,128)S(1)}, u32[]{:S(2)}, u32[]{:S(2)}) collective-permute-start(f32[16,128]{1,0:T(8,128)} %gram.1), channel_id=1, source_target_pairs={{0,24},{1,25},{2,26},{3,27},{4,28},{5,29},{6,30},{7,31},{8,16},{9,... | collective-permute-start | bytes 24584 | tf_op jit(solution)/shard_map/ppermute | solution.py:93
  125.6 4.8 %collective-permute-start.20 = (f32[16,128]{1,0:T(8,128)}, f32[16,128]{1,0:T(8,128)S(1)}, u32[]{:S(2)}, u32[]{:S(2)}) collective-permute-start(f32[16,128]{1,0:T(8,128)} %gram.1), channel_id=1, source_target_pairs={{0,16},{1,17},{2,18},{3,19},{4,20},{5,21},{6,22},{7,23},{8,24},{9,... | collective-permute-start | bytes 24584 | tf_op jit(solution)/shard_map/ppermute | solution.py:93
  125.6 4.8 %collective-permute-start.19 = (f32[16,128]{1,0:T(8,128)}, f32[16,128]{1,0:T(8,128)S(1)}, u32[]{:S(2)}, u32[]{:S(2)}) collective-permute-start(f32[16,128]{1,0:T(8,128)} %gram.1), channel_id=1, source_target_pairs={{0,8},{1,9},{2,10},{3,11},{4,12},{5,13},{6,14},{7,15},{8,0},{9,1},... | collective-permute-start | bytes 24584 | tf_op jit(solution)/shard_map/ppermute | solution.py:93
  131.1 1.2 collective-permute-start.22
  132.3 0.9 copy-start
  132.3 4.5 %collective-permute-start.25 = (f32[16,128]{1,0:T(8,128)S(1)}, f32[16,128]{1,0:T(8,128)S(1)}, u32[]{:S(2)}, u32[]{:S(2)}) collective-permute-start(f32[16,128]{1,0:T(8,128)S(1)} %add.35.g0), channel_id=1, source_target_pairs={{0,3},{1,2},{2,1},{3,0},{4,7},{5,6},{6,5},{7,4},{8,11},{9,10},{10,... | collective-permute-start | bytes 24584 | tf_op jit(solution)/shard_map/ppermute | solution.py:93
  132.3 4.5 %collective-permute-start.24 = (f32[16,128]{1,0:T(8,128)S(1)}, f32[16,128]{1,0:T(8,128)S(1)}, u32[]{:S(2)}, u32[]{:S(2)}) collective-permute-start(f32[16,128]{1,0:T(8,128)S(1)} %add.35.g0), channel_id=1, source_target_pairs={{0,2},{1,3},{2,0},{3,1},{4,6},{5,7},{6,4},{7,5},{8,10},{9,11},{10,... | collective-permute-start | bytes 24584 | tf_op jit(solution)/shard_map/ppermute | solution.py:93
  133.2 4.8 %collective-permute-start.23 = (f32[16,128]{1,0:T(8,128)S(1)}, f32[16,128]{1,0:T(8,128)}, u32[]{:S(2)}, u32[]{:S(2)}) collective-permute-start(f32[16,128]{1,0:T(8,128)S(1)} %add.35.g0), channel_id=1, source_target_pairs={{0,1},{1,0},{2,3},{3,2},{4,5},{5,4},{6,7},{7,6},{8,9},{9,8},{10,11... | collective-permute-start | bytes 24584 | tf_op jit(solution)/shard_map/ppermute | solution.py:93
  136.8 0.6 copy-start.2
  137.4 0.6 copy-start.3

commit v2 on v1

--- a/solution.py
+++ b/solution.py
@@ -9,7 +9,9 @@
 epsilon = 1e-06
 HALF = 64
 BLK = 32
-FULL = 65 * 2**20
+AHEAD = 2
+SHARED = 24 * 2**20
+ALONE = 65 * 2**20
 
 
 def partner(value, axis, distance):
@@ -140,92 +142,107 @@
         store.wait()
 
 
-def residual_kernel(s_ref, x_ref, t_ref, w_ref, own_ref, other_ref, pad_ref, acc_ref):
-    side = x_ref.shape[0]
-    imgs, ch = x_ref.shape[2], x_ref.shape[3]
-    rows = side * side * imgs
-    tap = pl.program_id(0)
-
-    @pl.when(tap == 0)
-    def _():
-        pad_ref[...] = jnp.zeros(pad_ref.shape, jnp.float32)
-        pad_ref[1 : side + 1, 1 : side + 1] = x_ref[...]
-        acc_ref[...] = -t_ref[...]
-
-    shifted = pad_ref[pl.ds(tap // 3, side), pl.ds(tap % 3, side)].reshape(rows, ch)
-    xh, xl = split2(shifted)
-    wh, wl = split2(w_ref[0])
-    acc_ref[...] += mm(xh, wh) + (mm(xh, wl) + mm(xl, wh))
-
-    @pl.when(tap == pl.num_programs(0) - 1)
-    def _():
-        even, odd = lane_halves(acc_ref[...])
-        up = s_ref[0] == 1
-        own_ref[...] = jnp.where(up, odd, even)
-        other_ref[...] = jnp.where(up, even, odd)
-
-
-def gradient_kernel(scale, side, s_ref, *refs):
-    sources, (keep_ref, send_ref, buf, xt, rh, rl, g_ref, sems) = refs[:8], refs[8:]
-    copies = fetch(sources, [buf.at[i] for i in range(8)], sems)
-    _, rows, width = buf.shape
-    strip = rows // side
-    imgs = strip // side
-    span = (side + 1) * 4 * imgs
+def residual_kernel(s_ref, x_ref, t_ref, w_ref, own_far, other_far, own_near, other_near, *scratch):
+    x_buf, t_buf, w_buf, left_ref, acc_ref, sems, w_sems = scratch
+    side = acc_ref.shape[0] - 2
+    imgs, cols = acc_ref.shape[2:]
+    taps = w_buf.shape[0]
+    (x_copy,) = fetch([x_ref], [x_buf], sems)
+    fetch([w_ref.at[tap] for tap in range(AHEAD)], [w_buf.at[tap] for tap in range(AHEAD)], w_sems)
+    acc_ref[...] = jnp.zeros(acc_ref.shape, jnp.float32)
+    x_copy.wait()
+    xh, xl = split2(x_buf[...])
+    left_ref[...] = jnp.concatenate([xh, xh, xl], axis=1)
+    t_copy = pltpu.make_async_copy(t_ref, t_buf, sems.at[1])
+    t_copy.start()
+
+    def add_tap(tap, carry):
+        pltpu.make_async_copy(w_ref.at[tap], w_buf.at[tap], w_sems.at[tap]).wait()
+
+        @pl.when(tap + AHEAD < taps)
+        def _():
+            later = tap + AHEAD
+            pltpu.make_async_copy(w_ref.at[later], w_buf.at[later], w_sems.at[later]).start()
+
+        wh, wl = split2(w_buf[tap])
+        product = mm(left_ref[...], jnp.concatenate([wh, wl, wh], axis=0))
+        at = (pl.ds(2 - tap // 3, side), pl.ds(2 - tap % 3, side))
+        acc_ref[at] += product.reshape(side, side, imgs, cols)
+        return carry
+
+    lax.fori_loop(0, taps, add_tap, 0)
+    t_copy.wait()
+    total = acc_ref[1 : side + 1, 1 : side + 1].reshape(t_buf.shape) - t_buf[...]
+    even, odd = lane_halves(total)
+    up, high = s_ref[0] == 1, s_ref[1] == 1
+    own, other = jnp.where(up, odd, even), jnp.where(up, even, odd)
+    for value, near, far in ((own, own_near, own_far), (other, other_near, other_far)):
+        near[...] = jnp.where(high, value[:, 128:], value[:, :128])
+        far[...] = jnp.where(high, value[:, :128], value[:, 128:])
+
+
+def prepare_kernel(side, *refs):
+    sources, (out_ref, buf, sems) = refs[:4], refs[4:]
+    copies = fetch(sources, [buf.at[i] for i in range(4)], sems)
+    _, _, width = buf.shape
+    span = out_ref.shape[2] // 2
+    for copy in copies:
+        copy.wait()
+    for r in range(side):
+        strip = gather(buf, r, side)
+        strip = strip.reshape(-1, width)
+        strip = jnp.concatenate([strip, jnp.zeros((span - strip.shape[0], width), jnp.float32)], axis=0)
+        xh, xl = split2(strip.T)
+        out_ref[r, :, :span] = xh
+        out_ref[r, :, span:] = xl
+
+
+def gather(buf, r, side):
+    strip = buf.shape[1] // side
+    parts = [buf[i, r * strip : (r + 1) * strip, :].reshape(side, strip // side, -1) for i in range(4)]
+    return jnp.concatenate(parts, axis=1)
+
+
+def gradient_kernel(scale, side, s_ref, xt_ref, *refs):
+    sources, (keep_ref, send_ref, buf, rh, rl, g_ref, sems) = refs[:4], refs[4:]
+    xt = xt_ref
+    copies = fetch(sources, [buf.at[i] for i in range(4)], sems)
+    width = buf.shape[2]
+    span = xt.shape[2] // 2
     for ref in (rh, rl):
         for edge in (0, side + 1, side + 2):
-            ref[:, edge] = jnp.zeros((side, 4 * imgs, width), jnp.bfloat16)
-
-    def gather(base, r):
-        parts = [buf[base + i, r * strip : (r + 1) * strip, :].reshape(side, imgs, width) for i in range(4)]
-        return jnp.concatenate(parts, axis=1)
-
-    for copy in copies[:4]:
+            ref[:, edge] = jnp.zeros((side,) + ref.shape[2:], jnp.bfloat16)
+    for copy in copies:
         copy.wait()
     for r in range(side):
-        rows_x = gather(0, r).reshape(4 * strip, width)
-        rows_x = jnp.concatenate([rows_x, jnp.zeros((span - 4 * strip, width), jnp.float32)], axis=0)
-        xh, xl = split2(rows_x.T)
-        xt[r, :, 0:span] = xh
-        xt[r, :, span : 2 * span] = xh
-        xt[r, :, 2 * span : 3 * span] = xl
-    for copy in copies[4:]:
-        copy.wait()
-    for r in range(side):
-        h, lo = split2(gather(4, r))
+        h, lo = split2(gather(buf, r, side))
         rh[r, 1 : side + 1] = h
         rl[r, 1 : side + 1] = lo
-
-    def column(j, carry):
-        totals = [None] * 3
-        for p in range(side):
-            first, last = max(p - 1, 0), min(p + 1, side - 1)
-            bh = rh[p, pl.ds(2 - j, side + 1)].reshape(span, width)
-            bl = rl[p, pl.ds(2 - j, side + 1)].reshape(span, width)
-            left = xt[first : last + 1].reshape((last + 1 - first) * width, 3 * span)
-            product = mm(left, jnp.concatenate([bh, bl, bh], axis=0))
-            for r in range(first, last + 1):
-                i = r - p + 1
-                part = product[(r - first) * width : (r - first + 1) * width]
-                totals[i] = part if totals[i] is None else totals[i] + part
-        per = width // BLK
-        for i in range(3):
-            g_ref[pl.ds((3 * i + j) * per, per)] = (totals[i] * scale).reshape(per, BLK, width)
-        return carry
-
-    lax.fori_loop(0, 3, column, 0)
+    totals = [None] * 9
+    for r in range(side):
+        taps = [(i, j) for i in range(3) for j in range(3) if 0 <= r - i + 1 < side]
+
+        def strips(ref):
+            return [ref[r - i + 1, 2 - j : 2 - j + side + 1].reshape(span, width) for i, j in taps]
+
+        bh, bl = jnp.concatenate(strips(rh), axis=1), jnp.concatenate(strips(rl), axis=1)
+        xh, xl = xt[r, :, :span], xt[r, :, span:]
+        product = mm(jnp.concatenate([xh, xh, xl], axis=1), jnp.concatenate([bh, bl, bh], axis=0))
+        for n, (i, j) in enumerate(taps):
+            piece = product[:, n * width : (n + 1) * width]
+            tap = 3 * i + j
+            totals[tap] = piece if totals[tap] is None else totals[tap] + piece
+    blocks = g_ref.shape[0] // 9
+    for tap in range(9):
+        g_ref[tap * blocks : (tap + 1) * blocks] = (totals[tap] * scale).reshape(blocks, BLK, width)
     odd = s_ref[0] == 1
     per = g_ref.shape[0] // 8
     for quarter in range(4):
-        for k in range(width // 128):
-            slot = 4 * jnp.bitwise_xor(k, s_ref[1]) + 2 * jnp.bitwise_xor(quarter // 2, s_ref[2])
-            slot = slot + jnp.bitwise_xor(quarter % 2, s_ref[3])
-            for m in range(per):
-                a = g_ref[2 * per * quarter + m, :, 128 * k : 128 * k + 128]
-                b = g_ref[2 * per * quarter + per + m, :, 128 * k : 128 * k + 128]
-                first, second = pair_pack(a, b)
-                keep_ref[slot, m * BLK : (m + 1) * BLK, :] = jnp.where(odd, second, first)
-                send_ref[slot, m * BLK : (m + 1) * BLK, :] = jnp.where(odd, first, second)
+        slot = 2 * jnp.bitwise_xor(quarter // 2, s_ref[1]) + jnp.bitwise_xor(quarter % 2, s_ref[2])
+        for m in range(per):
+            first, second = pair_pack(g_ref[2 * per * quarter + m], g_ref[2 * per * quarter + per + m])
+            keep_ref[slot, m * BLK : (m + 1) * BLK, :] = jnp.where(odd, second, first)
+            send_ref[slot, m * BLK : (m + 1) * BLK, :] = jnp.where(odd, first, second)
 
 
 def column_sums(a, b):
@@ -239,7 +256,8 @@
     return copies
 
 
-def pair_dots_kernel(s_ref, keep_ref, received_ref, out_ref, buf, sems):
+def pair_dots_kernel(s_ref, keep_ref, received_ref, *refs):
+    out_ref, buf, sems = refs[-3:]
     core = s_ref[0]
     count = keep_ref.shape[0]
     sources = [ref.at[d] for d in range(count) for ref in (keep_ref, received_ref)]
@@ -252,14 +270,14 @@
         cross += column_sums(a, b)
         mine += column_sums(a, a)
         theirs += column_sums(b, b)
+    left, right = jnp.where(core == 0, mine, theirs), jnp.where(core == 0, theirs, mine)
+    if len(refs) > 3:
+        before = refs[0]
+        cross, left, right = cross + before[0:1], left + before[1:2], right + before[2:3]
     out_ref[...] = jnp.zeros(out_ref.shape, jnp.float32)
     out_ref[0:1] = cross
-    out_ref[1:2] = jnp.where(core == 0, mine, theirs)
-    out_ref[2:3] = jnp.where(core == 0, theirs, mine)
-
-
-def sum_four(refs):
-    return (refs[0][...] + refs[1][...]) + (refs[2][...] + refs[3][...])
+    out_ref[1:2] = left
+    out_ref[2:3] = right
 
 
 def pair_coefs(cross, left_sq, right_sq):
@@ -267,21 +285,22 @@
 
 
 def pair_mix_kernel(s_ref, t0, t1, t2, t3, keep_ref, received_ref, *refs):
-    totals_refs = (t0, t1, t2, t3)
     core = s_ref[0]
     count = keep_ref.shape[0]
-    out_refs, (buf, in_sems, out_sems) = refs[:count], refs[count:]
+    out_refs, (buf, sums, in_sems, out_sems) = refs[:count], refs[count:]
     order = list(range(count - 1, -1, -1))
-    sources = [ref.at[d] for d in order for ref in (keep_ref, received_ref)]
-    copies = fetch(sources, [buf.at[i] for i in range(2 * count)], in_sems)
-    totals = jnp.sum(sum_four(totals_refs), axis=1, keepdims=True)
+    slots = [sums.at[i] for i in range(4)] + [buf.at[i] for i in range(2 * count)]
+    copies = fetch([t0, t1, t2, t3] + [ref.at[d] for d in order for ref in (keep_ref, received_ref)], slots, in_sems)
+    for copy in copies[:4]:
+        copy.wait()
+    totals = jnp.sum((sums[0] + sums[1]) + (sums[2] + sums[3]), axis=1, keepdims=True)
     left, right = pair_coefs(totals[0:1], totals[1:2], totals[2:3])
     keep_coef = jnp.where(core == 0, left, right)
     received_coef = jnp.where(core == 0, right, left)
     stores = []
     for i, d in enumerate(order):
-        copies[2 * i].wait()
-        copies[2 * i + 1].wait()
+        copies[4 + 2 * i].wait()
+        copies[5 + 2 * i].wait()
         buf[2 * i] = keep_coef * buf[2 * i] + received_coef * buf[2 * i + 1]
         stores.append(pltpu.make_async_copy(buf.at[2 * i], out_refs[d], out_sems.at[i]))
         stores[-1].start()
@@ -308,11 +327,14 @@
     return 4 * e + 2 * dx + dy
 
 
-def place_kernel(s_ref, g0, g1, g2, g3, *refs):
+def place_kernel(s_ref, *refs):
     upper, x, y = s_ref[0], s_ref[1], s_ref[2]
-    blocks, (out_ref, parts, rows_ref, sems) = refs[:8], refs[8:]
-    copies = fetch(blocks, [parts.at[slot_of(i)] for i in range(8)], sems)
-    gram = jnp.sum(sum_four((g0, g1, g2, g3)), axis=1, keepdims=True)
+    sources, (out_ref, parts, sums, rows_ref, sems) = refs[:12], refs[12:]
+    slots = [sums.at[i] for i in range(4)] + [parts.at[slot_of(i)] for i in range(8)]
+    copies = fetch(sources, slots, sems)
+    for copy in copies[:4]:
+        copy.wait()
+    gram = jnp.sum((sums[0] + sums[1]) + (sums[2] + sums[3]), axis=1, keepdims=True)
     g = lambda a, b: gram[4 * a + b : 4 * a + b + 1]
     p = pair_coefs(g(0, 1), g(0, 0), g(1, 1)) + pair_coefs(g(2, 3), g(2, 2), g(3, 3))
     cross = p[0] * (p[2] * g(0, 2) + p[3] * g(0, 3)) + p[1] * (p[2] * g(1, 2) + p[3] * g(1, 3))
@@ -327,7 +349,7 @@
         for a in range(3):
             coef = jnp.where(owner == a, absolute[a], coef)
         coefs.append(coef)
-    for copy in copies:
+    for copy in copies[4:]:
         copy.wait()
     for dy in range(2):
         part = [parts[2 * d + dy] for d in range(4)]
@@ -378,6 +400,7 @@
             pltpu.SemaphoreType.DMA((side,)),
             pltpu.SemaphoreType.DMA((2 * side,)),
         ],
+        compiler_params=pltpu.CompilerParams(vmem_limit_bytes=ALONE),
         name="split_images",
     )(scalars(y), xt.reshape(rows, channels))
     x_y = hop(x_other, lambda z, c, y, x: (z, c, 1 - y, x))
@@ -386,79 +409,101 @@
 
     tt = jnp.transpose(targets, (1, 2, 0, 3)).reshape(rows, channels)
     taps = weight.shape[0] * weight.shape[1]
-    whole = lambda *shape: pl.BlockSpec(shape, lambda t: (0,) * len(shape))
-    r_own, r_other = pl.pallas_call(
+    own_far, other_far, own_near, other_near = pl.pallas_call(
         residual_kernel,
-        grid=(taps,),
-        out_shape=(f32(rows, width), f32(rows, width)),
-        in_specs=[
-            SM,
-            whole(side, side, imgs, channels),
-            whole(rows, channels),
-            pl.BlockSpec((1, channels, channels), lambda t: (t, 0, 0)),
-        ],
-        out_specs=(whole(rows, width), whole(rows, width)),
+        out_shape=(f32(rows, 128),) * 4,
+        in_specs=[SM] + [HB] * 3,
+        out_specs=(VM,) * 4,
         scratch_shapes=[
+            pltpu.VMEM((rows, channels), jnp.float32),
+            pltpu.VMEM((rows, channels), jnp.float32),
+            pltpu.VMEM((taps, channels, channels), jnp.float32),
+            pltpu.VMEM((rows, 3 * channels), jnp.bfloat16),
             pltpu.VMEM((side + 2, side + 2, imgs, channels), jnp.float32),
-            pltpu.VMEM((rows, channels), jnp.float32),
+            pltpu.SemaphoreType.DMA((2,)),
+            pltpu.SemaphoreType.DMA((taps,)),
         ],
         cost_estimate=pl.CostEstimate(
             flops=6 * rows * taps * channels * channels, bytes_accessed=4 * taps * channels * channels, transcendentals=0
         ),
+        compiler_params=pltpu.CompilerParams(vmem_limit_bytes=ALONE),
         name="residual",
-    )(scalars(x), xt, tt, weight.reshape(taps, channels, channels))
-    r_x = hop(r_other, lambda z, c, y, x: (z, c, y, 1 - x))
-    r_d = hop(r_other, lambda z, c, y, x: (z, c, 1 - y, 1 - x))
-    r_y = hop(r_own, lambda z, c, y, x: (z, c, 1 - y, x))
+    )(scalars(x, z // 2), xt.reshape(rows, channels), tt, weight.reshape(taps, channels, channels))
+    far = exchange(own_far, other_far)
+    near = exchange(own_near, other_near)
+
+    span = (side + 1) * 4 * imgs
+    xt_shape = (side, width, 2 * span)
+    images_t = pl.pallas_call(
+        lambda *refs: prepare_kernel(side, *refs),
+        out_shape=jax.ShapeDtypeStruct(xt_shape, jnp.bfloat16),
+        in_specs=[HB] * 4,
+        out_specs=VM,
+        scratch_shapes=[pltpu.VMEM((4, rows, width), jnp.float32), pltpu.SemaphoreType.DMA((4,))],
+        compiler_params=pltpu.CompilerParams(vmem_limit_bytes=SHARED),
+        name="prepare",
+    )(x_own, x_x, x_y, x_d)
 
     z_count = lax.axis_size("node") // 2
     part = taps * width // 8
     count = 2 * z_count
+    half = count // 2
     place = scalars(z // 2, x, y)
-    keep, send = pl.pallas_call(
-        lambda *refs: gradient_kernel(1.0 / rows, side, *refs),
-        out_shape=(f32(count, part, 128), f32(count, part, 128)),
-        in_specs=[SM] + [HB] * 8,
-        out_specs=(VM, VM),
-        scratch_shapes=[
-            pltpu.VMEM((8, rows, width), jnp.float32),
-            pltpu.VMEM((side, width, 3 * (side + 1) * 4 * imgs), jnp.bfloat16),
-            pltpu.VMEM((side, side + 3, 4 * imgs, width), jnp.bfloat16),
-            pltpu.VMEM((side, side + 3, 4 * imgs, width), jnp.bfloat16),
-            pltpu.VMEM((taps * width // BLK, BLK, width), jnp.float32),
-            pltpu.SemaphoreType.DMA((8,)),
-        ],
-        cost_estimate=pl.CostEstimate(
-            flops=24 * rows * taps * width * width, bytes_accessed=4 * taps * width * width, transcendentals=0
-        ),
-        compiler_params=pltpu.CompilerParams(vmem_limit_bytes=FULL),
-        name="gradient",
-    )(scalars(c, z // 2, y, z % 2), x_own, x_x, x_y, x_d, r_own, r_x, r_y, r_d)
-
-    received = hop(send, lambda z, c, y, x: (z, 1 - c, y, x))
-    totals = pl.pallas_call(
-        pair_dots_kernel,
-        out_shape=f32(8, 128),
-        in_specs=[SM, HB, HB],
-        out_specs=VM,
-        scratch_shapes=[pltpu.VMEM((2 * count, part, 128), jnp.float32), pltpu.SemaphoreType.DMA((2 * count,))],
-        compiler_params=pltpu.CompilerParams(vmem_limit_bytes=FULL),
-        name="pair_dots",
-    )(scalars(c), keep, received)
-    totals = plane_sum(totals)
-    blocks = pl.pallas_call(
-        pair_mix_kernel,
-        out_shape=(f32(part, 128),) * count,
-        in_specs=[SM] + [VM] * 4 + [HB, HB],
-        out_specs=(HB,) * count,
-        scratch_shapes=[
-            pltpu.VMEM((2 * count, part, 128), jnp.float32),
-            pltpu.SemaphoreType.DMA((2 * count,)),
-            pltpu.SemaphoreType.DMA((count,)),
-        ],
-        compiler_params=pltpu.CompilerParams(vmem_limit_bytes=FULL),
-        name="pair_mix",
-    )(scalars(c), *totals, keep, received)
+
+    def gradient(pieces):
+        return pl.pallas_call(
+            lambda *refs: gradient_kernel(1.0 / rows, side, *refs),
+            out_shape=(f32(half, part, 128), f32(half, part, 128)),
+            in_specs=[SM, VM] + [HB] * 4,
+            out_specs=(VM, VM),
+            scratch_shapes=[
+                pltpu.VMEM((4, rows, 128), jnp.float32),
+                pltpu.VMEM((side, side + 3, 4 * imgs, 128), jnp.bfloat16),
+                pltpu.VMEM((side, side + 3, 4 * imgs, 128), jnp.bfloat16),
+                pltpu.VMEM((taps * width // BLK, BLK, 128), jnp.float32),
+                pltpu.SemaphoreType.DMA((4,)),
+            ],
+            cost_estimate=pl.CostEstimate(
+                flops=24 * rows * taps * width * 128, bytes_accessed=4 * taps * width * 128, transcendentals=0
+            ),
+            compiler_params=pltpu.CompilerParams(vmem_limit_bytes=SHARED),
+        )(scalars(c, y, z % 2), images_t, *pieces)
+
+    def dots(keep, received, before):
+        return pl.pallas_call(
+            pair_dots_kernel,
+            out_shape=f32(8, 128),
+            in_specs=[SM, HB, HB] + [VM] * len(before),
+            out_specs=VM,
+            scratch_shapes=[pltpu.VMEM((2 * half, part, 128), jnp.float32), pltpu.SemaphoreType.DMA((2 * half,))],
+            compiler_params=pltpu.CompilerParams(vmem_limit_bytes=SHARED),
+        )(scalars(c), keep, received, *before)
+
+    across = lambda z, c, y, x: (z, 1 - c, y, x)
+    keep_far, send_far = gradient(far)
+    received_far = hop(send_far, across)
+    keep_near, send_near = gradient(near)
+    received_near = hop(send_near, across)
+    totals = dots(keep_far, received_far, ())
+    totals = plane_sum(dots(keep_near, received_near, (totals,)))
+
+    def mix(keep, received):
+        return pl.pallas_call(
+            pair_mix_kernel,
+            out_shape=(f32(part, 128),) * half,
+            in_specs=[SM] + [HB] * 6,
+            out_specs=(HB,) * half,
+            scratch_shapes=[
+                pltpu.VMEM((2 * half, part, 128), jnp.float32),
+                pltpu.VMEM((4, 8, 128), jnp.float32),
+                pltpu.SemaphoreType.DMA((4 + 2 * half,)),
+                pltpu.SemaphoreType.DMA((half,)),
+            ],
+            compiler_params=pltpu.CompilerParams(vmem_limit_bytes=SHARED),
+        )(scalars(c), *totals, keep, received)
+
+    mixed_far = mix(keep_far, received_far)
+    blocks = tuple(mix(keep_near, received_near)) + tuple(mixed_far)
 
     moved = []
     for index in range(count):
@@ -471,7 +516,7 @@
         in_specs=[SM] + [HB] * count,
         out_specs=VM,
         scratch_shapes=[pltpu.VMEM((count, part, 128), jnp.float32), pltpu.SemaphoreType.DMA((count,))],
-        compiler_params=pltpu.CompilerParams(vmem_limit_bytes=FULL),
+        compiler_params=pltpu.CompilerParams(vmem_limit_bytes=SHARED),
         name="gram",
     )(place, *moved)
     along = [hop(gram, lambda z, c, y, x, d=d: (z ^ d, c, y, x)) for d in range(1, z_count)]
@@ -479,17 +524,25 @@
     out = pl.pallas_call(
         place_kernel,
         out_shape=f32(HALF, 4 * part),
-        in_specs=[SM] + [VM] * 4 + [HB] * count,
+        in_specs=[SM] + [HB] * (4 + count),
         out_specs=VM,
         scratch_shapes=[
             pltpu.VMEM((count, part, 128), jnp.float32),
+            pltpu.VMEM((4, 16, 128), jnp.float32),
             pltpu.VMEM((2 * part // HALF, 2, HALF, HALF), jnp.float32),
-            pltpu.SemaphoreType.DMA((count,)),
+            pltpu.SemaphoreType.DMA((4 + count,)),
         ],
-        compiler_params=pltpu.CompilerParams(vmem_limit_bytes=FULL),
+        compiler_params=pltpu.CompilerParams(vmem_limit_bytes=SHARED),
         name="place",
     )(place, *gram, *moved)
     return out.T
+
+
+def exchange(own, other):
+    along_x = hop(other, lambda z, c, y, x: (z, c, y, 1 - x))
+    across = hop(other, lambda z, c, y, x: (z, c, 1 - y, 1 - x))
+    along_y = hop(own, lambda z, c, y, x: (z, c, 1 - y, x))
+    return own, along_x, along_y, across
 
 
 def plane_sum(value):

time: 142 us -> 123 us (0.87)
  waiting for transfers between devices: 57.9 us -> 36 us
  Pallas kernels: 37.8 us -> 40.5 us
  starting transfers between devices: 41.2 us -> 43.1 us
  other arithmetic: 2.63 us -> 0.76 us
    ppermute x26 -> x30, waiting for transfers between devices: 57.9 us -> 36 us  [hop(): return lax.ppermute(value, ('node', 'local'), pairs)]
    pallas_call x4 -> x8, Pallas kernels: 29.1 us -> 32.2 us  [the longest x1 10.8 us: tiles(): pl.pallas_call(residual_kernel, out_shape=(f32(rows, 128),) * 4, in_specs...]
    ppermute x26 -> x30, starting transfers between devices: 41.2 us -> 43.1 us  [hop(): return lax.ppermute(value, ('node', 'local'), pairs)]
  transfers between devices with their start and end apart: 26 -> 30, of which waited for: 14 -> 14; matrix products, arithmetic and copies ran while one was open for 1% -> 1% of each run, Pallas kernels for 2% -> 23%
where the time goes in v2:
time: 123 us
  starting transfers between devices  43.1 us (35%)
  Pallas kernels  40.5 us (33%)
  waiting for transfers between devices  36 us (29%)
  local copies, waits for them, and re-layouts  1.93 us (2%)
    ppermute x30, starting transfers between devices, hop(): return lax.ppermute(value, ('node', 'local'), pairs)  43.1 us
    ppermute x30, waiting for transfers between devices, hop(): return lax.ppermute(value, ('node', 'local'), pairs)  36 us
    pallas_call x1, Pallas kernels, tiles(): pl.pallas_call(residual_kernel, out_shape=(f32(rows, 128),) * 4, in_specs...  10.8 us
    pallas_call x2, Pallas kernels, gradient(): pl.pallas_call(lambda *refs: gradient_kernel(1.0 / rows, side, *refs), ou...  10.5 us
    pallas_call x2, Pallas kernels, mix(): pl.pallas_call(pair_mix_kernel, out_shape=(f32(part, 128),) * half, in_sp...  5.28 us
    pallas_call x2, Pallas kernels, dots(): pl.pallas_call(pair_dots_kernel, out_shape=f32(8, 128), in_specs=[SM, HB,...  3.62 us
    pallas_call x1, Pallas kernels, tiles(): pl.pallas_call(place_kernel, out_shape=f32(HALF, 4 * part), in_specs=[SM]...  3.44 us
  transfers between devices with their start and end apart: 30, of which 14 were waited for; matrix products, arithmetic and copies ran while one was open for 1% of the time, Pallas kernels for 23%

profile of v2, /device:TPU:0, one launch (start us, length us, event | category | flops | bytes accessed | tf_op | source)
XLA Modules:
  0.0 122.5 jit_solution(13029646873640658781)
XLA Ops:
  0.0 2.4 %split_images.1 = (f32[392,256]{1,0:T(8,128)}, f32[392,256]{1,0:T(8,128)}) custom-call(s32[1]{0:T(128)} %bitcast.2.s_ref, f32[392,512]{1,0:T(8,128)} %bitcast.13), custom_call_target="tpu_custom_call" | custom-call | tf_op jit(solution)/shard_map/split_images/pallas_call | solution.py:392
  2.5 3.1 %collective-permute-start.1 = (f32[392,256]{1,0:T(8,128)}, f32[392,256]{1,0:T(8,128)}, u32[]{:S(2)}, u32[]{:S(2)}) collective-permute-start(f32[392,256]{1,0:T(8,128)} %get-tuple-element.24), channel_id=1, source_target_pairs={{0,2},{1,3},{2,0},{3,1},{4,6},{5,7},{6,4},{7,5},{8,10},{9,11},{10,... | collective-permute-start | bytes 1204232 | tf_op jit(solution)/shard_map/ppermute | solution.py:95
  5.5 1.4 %collective-permute-start.2 = (f32[392,256]{1,0:T(8,128)}, f32[392,256]{1,0:T(8,128)}, u32[]{:S(2)}, u32[]{:S(2)}) collective-permute-start(f32[392,256]{1,0:T(8,128)} %get-tuple-element.24), channel_id=1, source_target_pairs={{0,3},{1,2},{2,1},{3,0},{4,7},{5,6},{6,5},{7,4},{8,11},{9,10},{10,... | collective-permute-start | bytes 1204232 | tf_op jit(solution)/shard_map/ppermute | solution.py:95
  7.7 10.8 %residual.1 = (f32[392,128]{1,0:T(8,128)}, f32[392,128]{1,0:T(8,128)}, f32[392,128]{1,0:T(8,128)}, f32[392,128]{1,0:T(8,128)}) custom-call(s32[2]{0:T(128)} %pad_add_fusion.2.s_ref, f32[392,512]{1,0:T(8,128)} %bitcast.14, f32[392,512]{1,0:T(8,128)} %bitcast.16, f32[9,512,512]{2,1,0:T(8,128)} %bitcast.15), custom_call_target="tpu_custom_call" | custom-call | flops 5549064192 | bytes 9437184 | tf_op jit(solution)/shard_map/residual/pallas_call | solution.py:412
  18.5 2.0 %collective-permute-start.7 = (f32[392,128]{1,0:T(8,128)}, f32[392,128]{1,0:T(8,128)S(1)}, u32[]{:S(2)}, u32[]{:S(2)}) collective-permute-start(f32[392,128]{1,0:T(8,128)} %get-tuple-element.30), channel_id=1, source_target_pairs={{0,1},{1,0},{2,3},{3,2},{4,5},{5,4},{6,7},{7,6},{8,9},{9,8},{10,11... | collective-permute-start | bytes 602120 | tf_op jit(solution)/shard_map/ppermute | solution.py:95
  20.4 1.5 %collective-permute-start.8 = (f32[392,128]{1,0:T(8,128)}, f32[392,128]{1,0:T(8,128)S(1)}, u32[]{:S(2)}, u32[]{:S(2)}) collective-permute-start(f32[392,128]{1,0:T(8,128)} %get-tuple-element.29.refs_2_), channel_id=1, source_target_pairs={{0,2},{1,3},{2,0},{3,1},{4,6},{5,7},{6,4},{7,5},{8,10},{9,11},{10,... | collective-permute-start | bytes 602120 | tf_op jit(solution)/shard_map/ppermute | solution.py:95
  22.0 4.2 %collective-permute-done.refs_1_ = f32[392,256]{1,0:T(8,128)} collective-permute-done((f32[392,256]{1,0:T(8,128)}, f32[392,256]{1,0:T(8,128)}, u32[]{:S(2)}, u32[]{:S(2)}) %collective-permute-start) | collective-permute-done | bytes 401440 | tf_op jit(solution)/shard_map/ppermute | solution.py:95
  26.1 2.9 %collective-permute-start.9 = (f32[392,128]{1,0:T(8,128)}, f32[392,128]{1,0:T(8,128)S(1)}, u32[]{:S(2)}, u32[]{:S(2)}) collective-permute-start(f32[392,128]{1,0:T(8,128)} %get-tuple-element.30), channel_id=1, source_target_pairs={{0,3},{1,2},{2,1},{3,0},{4,7},{5,6},{6,5},{7,4},{8,11},{9,10},{10,... | collective-permute-start | bytes 602120 | tf_op jit(solution)/shard_map/ppermute | solution.py:95
  29.6 1.4 %collective-permute-start.5 = (f32[392,128]{1,0:T(8,128)}, f32[392,128]{1,0:T(8,128)S(1)}, u32[]{:S(2)}, u32[]{:S(2)}) collective-permute-start(f32[392,128]{1,0:T(8,128)} %get-tuple-element.26), channel_id=1, source_target_pairs={{0,3},{1,2},{2,1},{3,0},{4,7},{5,6},{6,5},{7,4},{8,11},{9,10},{10,... | collective-permute-start | bytes 602120 | tf_op jit(solution)/shard_map/ppermute | solution.py:95
  32.0 2.0 %prepare.1.refs_1_ = bf16[7,256,512]{2,1,0:T(8,128)(2,1)S(1)} custom-call(f32[392,256]{1,0:T(8,128)S(1)} %copy-done, f32[392,256]{1,0:T(8,128)} %collective-permute-done.refs_1_, f32[392,256]{1,0:T(8,128)} %collective-permute-done.1.refs_2_, f32[392,256]{1,0:T(8,128)} %collective-permute-done.2.refs_3_), custom_call_target="tpu_custom_call" | custom-call | tf_op jit(solution)/shard_map/prepare/pallas_call | solution.py:437
  34.1 1.6 %collective-permute-start.4 = (f32[392,128]{1,0:T(8,128)}, f32[392,128]{1,0:T(8,128)S(1)}, u32[]{:S(2)}, u32[]{:S(2)}) collective-permute-start(f32[392,128]{1,0:T(8,128)} %get-tuple-element.25.refs_2_), channel_id=1, source_target_pairs={{0,2},{1,3},{2,0},{3,1},{4,6},{5,7},{6,4},{7,5},{8,10},{9,11},{10,... | collective-permute-start | bytes 602120 | tf_op jit(solution)/shard_map/ppermute | solution.py:95
  36.9 5.3 %shard_map.38 = (f32[4,288,128]{2,1,0:T(8,128)S(1)}, f32[4,288,128]{2,1,0:T(8,128)S(1)}) custom-call(s32[3]{0:T(128)S(1)} %pad_add_fusion.1.refs_0_, bf16[7,256,512]{2,1,0:T(8,128)(2,1)S(1)} %prepare.1.refs_1_, f32[392,128]{1,0:T(8,128)S(1)} %copy-done.2, f32[392,128]{1,0:T(8,128)S(1)} %collective-permute-done.7.refs_3_, ...), custom_call_target="tpu_custom_call" | custom-call | flops 2774532096 | bytes 1179648 | tf_op jit(solution)/shard_map/pallas_call | solution.py:454
  42.3 1.9 %collective-permute-done.4.refs_4_ = f32[392,128]{1,0:T(8,128)S(1)} collective-permute-done((f32[392,128]{1,0:T(8,128)}, f32[392,128]{1,0:T(8,128)S(1)}, u32[]{:S(2)}, u32[]{:S(2)}) %collective-permute-start.4) | collective-permute-done | bytes 200736 | tf_op jit(solution)/shard_map/ppermute | solution.py:95
  44.2 5.3 %shard_map.37 = (f32[4,288,128]{2,1,0:T(8,128)S(1)}, f32[4,288,128]{2,1,0:T(8,128)S(1)}) custom-call(s32[3]{0:T(128)S(1)} %pad_add_fusion.1.refs_0_, bf16[7,256,512]{2,1,0:T(8,128)(2,1)S(1)} %prepare.1.refs_1_, f32[392,128]{1,0:T(8,128)S(1)} %copy-done.1, f32[392,128]{1,0:T(8,128)S(1)} %collective-permute-done.3.refs_3_, ...), custom_call_target="tpu_custom_call" | custom-call | flops 2774532096 | bytes 1179648 | tf_op jit(solution)/shard_map/pallas_call | solution.py:454
  49.5 1.8 %shard_map.39.refs_0_ = f32[8,128]{1,0:T(8,128)S(1)} custom-call(s32[1]{0:T(128)} %bitcast.3.s_ref, f32[4,288,128]{2,1,0:T(8,128)S(1)} %get-tuple-element.31.keep_ref, f32[4,288,128]{2,1,0:T(8,128)S(1)} %collective-permute-done.10.received_ref), custom_call_target="tpu_custom_call" | custom-call | tf_op jit(solution)/shard_map/pallas_call | solution.py:473
  51.5 1.8 %shard_map.40 = f32[8,128]{1,0:T(8,128)S(1)} custom-call(s32[1]{0:T(128)} %bitcast.3.s_ref, f32[4,288,128]{2,1,0:T(8,128)S(1)} %get-tuple-element.27.keep_ref, f32[4,288,128]{2,1,0:T(8,128)S(1)} %collective-permute-done.6.received_ref, f32[8,128]{1,0:T(8,128)S(1)} %shard_map.39.refs_0_), custom_call_target="tpu_custom_call" | custom-call | tf_op jit(solution)/shard_map/pallas_call | solution.py:473
  56.4 1.7 %collective-permute-start.14 = (f32[8,128]{1,0:T(8,128)S(1)}, f32[8,128]{1,0:T(8,128)S(1)}, u32[]{:S(2)}, u32[]{:S(2)}) collective-permute-start(f32[8,128]{1,0:T(8,128)S(1)} %add.32.t0), channel_id=1, source_target_pairs={{0,3},{1,2},{2,1},{3,0},{4,7},{5,6},{6,5},{7,4},{8,11},{9,10},{10,... | collective-permute-start | bytes 12296 | tf_op jit(solution)/shard_map/ppermute | solution.py:95
  58.7 2.1 %collective-permute-done.14.t3 = f32[8,128]{1,0:T(8,128)S(1)} collective-permute-done((f32[8,128]{1,0:T(8,128)S(1)}, f32[8,128]{1,0:T(8,128)S(1)}, u32[]{:S(2)}, u32[]{:S(2)}) %collective-permute-start.14) | collective-permute-done | bytes 4128 | tf_op jit(solution)/shard_map/ppermute | solution.py:95
  60.9 2.6 %shard_map.41 = (f32[288,128]{1,0:T(8,128)S(1)}, f32[288,128]{1,0:T(8,128)S(1)}, f32[288,128]{1,0:T(8,128)S(1)}, f32[288,128]{1,0:T(8,128)S(1)}) custom-call(s32[1]{0:T(128)} %bitcast.3.s_ref, f32[8,128]{1,0:T(8,128)S(1)} %add.32.t0, f32[8,128]{1,0:T(8,128)S(1)} %collective-permute-done.12.t1, f32[8,128]{1,0:T(8,128)S(1)} %collective-permute-done.13.t2, ...), custom_call_target="tpu_custom_call" | custom-call | tf_op jit(solution)/shard_map/pallas_call | solution.py:491
  64.2 2.2 %collective-permute-start.16 = (f32[288,128]{1,0:T(8,128)S(1)}, f32[288,128]{1,0:T(8,128)S(1)}, u32[]{:S(2)}, u32[]{:S(2)}) collective-permute-start(f32[288,128]{1,0:T(8,128)S(1)} %get-tuple-element.34), channel_id=1, source_target_pairs={{0,1},{1,5},{2,3},{3,7},{4,9},{5,13},{6,11},{7,15},{8,0},{9,4},{10... | collective-permute-start | bytes 442376 | tf_op jit(solution)/shard_map/ppermute | solution.py:95
  67.8 2.4 %collective-permute-start.18 = (f32[288,128]{1,0:T(8,128)S(1)}, f32[288,128]{1,0:T(8,128)S(1)}, u32[]{:S(2)}, u32[]{:S(2)}) collective-permute-start(f32[288,128]{1,0:T(8,128)S(1)} %get-tuple-element.36), channel_id=1, source_target_pairs={{0,3},{1,7},{2,1},{3,5},{4,11},{5,15},{6,9},{7,13},{8,2},{9,6},{10... | collective-permute-start | bytes 442376 | tf_op jit(solution)/shard_map/ppermute | solution.py:95
  70.2 2.6 %shard_map.42 = (f32[288,128]{1,0:T(8,128)S(1)}, f32[288,128]{1,0:T(8,128)S(1)}, f32[288,128]{1,0:T(8,128)S(1)}, f32[288,128]{1,0:T(8,128)S(1)}) custom-call(s32[1]{0:T(128)} %bitcast.3.s_ref, f32[8,128]{1,0:T(8,128)S(1)} %add.32.t0, f32[8,128]{1,0:T(8,128)S(1)} %collective-permute-done.12.t1, f32[8,128]{1,0:T(8,128)S(1)} %collective-permute-done.13.t2, ...), custom_call_target="tpu_custom_call" | custom-call | tf_op jit(solution)/shard_map/pallas_call | solution.py:491
  72.8 2.6 %collective-permute-start.19 = (f32[288,128]{1,0:T(8,128)S(1)}, f32[288,128]{1,0:T(8,128)S(1)}, u32[]{:S(2)}, u32[]{:S(2)}) collective-permute-start(f32[288,128]{1,0:T(8,128)S(1)} %get-tuple-element.37), channel_id=1, source_target_pairs={{0,16},{1,20},{2,18},{3,22},{4,24},{5,28},{6,26},{7,30},{8,17},{9,... | collective-permute-start | bytes 442376 | tf_op jit(solution)/shard_map/ppermute | solution.py:95
  76.4 3.1 %collective-permute-start.21 = (f32[288,128]{1,0:T(8,128)S(1)}, f32[288,128]{1,0:T(8,128)S(1)}, u32[]{:S(2)}, u32[]{:S(2)}) collective-permute-start(f32[288,128]{1,0:T(8,128)S(1)} %get-tuple-element.39), channel_id=1, source_target_pairs={{0,18},{1,22},{2,16},{3,20},{4,26},{5,30},{6,24},{7,28},{8,19},{9,... | collective-permute-start | bytes 442376 | tf_op jit(solution)/shard_map/ppermute | solution.py:95
  80.9 12.2 %collective-permute-done.19.refs_4_.refs_8_ = f32[288,128]{1,0:T(8,128)S(1)} collective-permute-done((f32[288,128]{1,0:T(8,128)S(1)}, f32[288,128]{1,0:T(8,128)S(1)}, u32[]{:S(2)}, u32[]{:S(2)}) %collective-permute-start.19) | collective-permute-done | bytes 147488 | tf_op jit(solution)/shard_map/ppermute | solution.py:95
  93.1 7.0 %collective-permute-done.21.refs_6_.refs_10_ = f32[288,128]{1,0:T(8,128)S(1)} collective-permute-done((f32[288,128]{1,0:T(8,128)S(1)}, f32[288,128]{1,0:T(8,128)S(1)}, u32[]{:S(2)}, u32[]{:S(2)}) %collective-permute-start.21) | collective-permute-done | bytes 147488 | tf_op jit(solution)/shard_map/ppermute | solution.py:95
  100.2 2.4 %gram.1 = f32[16,128]{1,0:T(8,128)S(1)} custom-call(s32[3]{0:T(128)S(1)} %pad_add_fusion.s_ref, f32[288,128]{1,0:T(8,128)S(1)} %collective-permute-done.15.refs_0_.refs_4_, f32[288,128]{1,0:T(8,128)S(1)} %collective-permute-done.16.refs_1_.refs_5_, f32[288,128]{1,0:T(8,128)S(1)} %collective-permute-done.17.refs_2_.refs_6_, ...), custom_call_target="tpu_custom_call" | custom-call | tf_op jit(solution)/shard_map/gram/pallas_call | solution.py:513
  102.6 4.5 %collective-permute-start.24 = (f32[16,128]{1,0:T(8,128)S(1)}, f32[16,128]{1,0:T(8,128)S(1)}, u32[]{:S(2)}, u32[]{:S(2)}) collective-permute-start(f32[16,128]{1,0:T(8,128)S(1)} %gram.1), channel_id=1, source_target_pairs={{0,16},{1,17},{2,18},{3,19},{4,20},{5,21},{6,22},{7,23},{8,24},{9,... | collective-permute-start | bytes 24584 | tf_op jit(solution)/shard_map/ppermute | solution.py:95
  108.9 3.6 %collective-permute-done.25 = f32[16,128]{1,0:T(8,128)S(1)} collective-permute-done((f32[16,128]{1,0:T(8,128)S(1)}, f32[16,128]{1,0:T(8,128)S(1)}, u32[]{:S(2)}, u32[]{:S(2)}) %collective-permute-start.25) | collective-permute-done | bytes 8224 | tf_op jit(solution)/shard_map/ppermute | solution.py:95
  114.5 2.7 %collective-permute-start.29 = (f32[16,128]{1,0:T(8,128)S(1)}, f32[16,128]{1,0:T(8,128)S(1)}, u32[]{:S(2)}, u32[]{:S(2)}) collective-permute-start(f32[16,128]{1,0:T(8,128)S(1)} %add.36.refs_0_), channel_id=1, source_target_pairs={{0,3},{1,2},{2,1},{3,0},{4,7},{5,6},{6,5},{7,4},{8,11},{9,10},{10,... | collective-permute-start | bytes 24584 | tf_op jit(solution)/shard_map/ppermute | solution.py:95
  117.4 1.7 %collective-permute-done.29.refs_3_ = f32[16,128]{1,0:T(8,128)S(1)} collective-permute-done((f32[16,128]{1,0:T(8,128)S(1)}, f32[16,128]{1,0:T(8,128)S(1)}, u32[]{:S(2)}, u32[]{:S(2)}) %collective-permute-start.29) | collective-permute-done | bytes 8224 | tf_op jit(solution)/shard_map/ppermute | solution.py:95
  119.1 3.4 %place.1 = f32[64,1152]{1,0:T(8,128)} custom-call(s32[3]{0:T(128)S(1)} %pad_add_fusion.s_ref, f32[16,128]{1,0:T(8,128)S(1)} %add.36.refs_0_, f32[16,128]{1,0:T(8,128)S(1)} %collective-permute-done.27.refs_1_, f32[16,128]{1,0:T(8,128)S(1)} %collective-permute-done.28.refs_2_, f32[16,128]{1,0:T(8,128)S(1)} %collective-permute-done.29.refs_3_, ...), custom_call_target="tpu_custom_call" | custom-call | tf_op jit(solution)/shard_map/place/pallas_call | solution.py:524
  (51 shorter events, 16.1 us)
Async XLA Ops:
  2.5 26.6 %collective-permute-start.1 = (f32[392,256]{1,0:T(8,128)}, f32[392,256]{1,0:T(8,128)}, u32[]{:S(2)}, u32[]{:S(2)}) collective-permute-start(f32[392,256]{1,0:T(8,128)} %get-tuple-element.24), channel_id=1, source_target_pairs={{0,2},{1,3},{2,0},{3,1},{4,6},{5,7},{6,4},{7,5},{8,10},{9,11},{10,... | collective-permute-start | bytes 1204232 | tf_op jit(solution)/shard_map/ppermute | solution.py:95
  5.5 24.1 %collective-permute-start.2 = (f32[392,256]{1,0:T(8,128)}, f32[392,256]{1,0:T(8,128)}, u32[]{:S(2)}, u32[]{:S(2)}) collective-permute-start(f32[392,256]{1,0:T(8,128)} %get-tuple-element.24), channel_id=1, source_target_pairs={{0,3},{1,2},{2,1},{3,0},{4,7},{5,6},{6,5},{7,4},{8,11},{9,10},{10,... | collective-permute-start | bytes 1204232 | tf_op jit(solution)/shard_map/ppermute | solution.py:95
  7.0 19.2 %collective-permute-start = (f32[392,256]{1,0:T(8,128)}, f32[392,256]{1,0:T(8,128)}, u32[]{:S(2)}, u32[]{:S(2)}) collective-permute-start(f32[392,256]{1,0:T(8,128)} %get-tuple-element.23.refs_0_), channel_id=1, source_target_pairs={{0,1},{1,0},{2,3},{3,2},{4,5},{5,4},{6,7},{7,6},{8,9},{9,8},{10,11... | collective-permute-start | bytes 1204232 | tf_op jit(solution)/shard_map/ppermute | solution.py:95
  18.5 15.6 %collective-permute-start.7 = (f32[392,128]{1,0:T(8,128)}, f32[392,128]{1,0:T(8,128)S(1)}, u32[]{:S(2)}, u32[]{:S(2)}) collective-permute-start(f32[392,128]{1,0:T(8,128)} %get-tuple-element.30), channel_id=1, source_target_pairs={{0,1},{1,0},{2,3},{3,2},{4,5},{5,4},{6,7},{7,6},{8,9},{9,8},{10,11... | collective-permute-start | bytes 602120 | tf_op jit(solution)/shard_map/ppermute | solution.py:95
  20.4 15.2 %collective-permute-start.8 = (f32[392,128]{1,0:T(8,128)}, f32[392,128]{1,0:T(8,128)S(1)}, u32[]{:S(2)}, u32[]{:S(2)}) collective-permute-start(f32[392,128]{1,0:T(8,128)} %get-tuple-element.29.refs_2_), channel_id=1, source_target_pairs={{0,2},{1,3},{2,0},{3,1},{4,6},{5,7},{6,4},{7,5},{8,10},{9,11},{10,... | collective-permute-start | bytes 602120 | tf_op jit(solution)/shard_map/ppermute | solution.py:95
  26.1 9.9 %collective-permute-start.9 = (f32[392,128]{1,0:T(8,128)}, f32[392,128]{1,0:T(8,128)S(1)}, u32[]{:S(2)}, u32[]{:S(2)}) collective-permute-start(f32[392,128]{1,0:T(8,128)} %get-tuple-element.30), channel_id=1, source_target_pairs={{0,3},{1,2},{2,1},{3,0},{4,7},{5,6},{6,5},{7,4},{8,11},{9,10},{10,... | collective-permute-start | bytes 602120 | tf_op jit(solution)/shard_map/ppermute | solution.py:95
  29.1 13.2 %collective-permute-start.3 = (f32[392,128]{1,0:T(8,128)}, f32[392,128]{1,0:T(8,128)S(1)}, u32[]{:S(2)}, u32[]{:S(2)}) collective-permute-start(f32[392,128]{1,0:T(8,128)} %get-tuple-element.26), channel_id=1, source_target_pairs={{0,1},{1,0},{2,3},{3,2},{4,5},{5,4},{6,7},{7,6},{8,9},{9,8},{10,11... | collective-permute-start | bytes 602120 | tf_op jit(solution)/shard_map/ppermute | solution.py:95
  29.6 14.6 %collective-permute-start.5 = (f32[392,128]{1,0:T(8,128)}, f32[392,128]{1,0:T(8,128)S(1)}, u32[]{:S(2)}, u32[]{:S(2)}) collective-permute-start(f32[392,128]{1,0:T(8,128)} %get-tuple-element.26), channel_id=1, source_target_pairs={{0,3},{1,2},{2,1},{3,0},{4,7},{5,6},{6,5},{7,4},{8,11},{9,10},{10,... | collective-permute-start | bytes 602120 | tf_op jit(solution)/shard_map/ppermute | solution.py:95
  31.0 1.0 copy-start
  32.0 12.1 %copy-start.1 = (f32[392,128]{1,0:T(8,128)S(1)}, f32[392,128]{1,0:T(8,128)}, u32[]{:S(2)}) copy-start(f32[392,128]{1,0:T(8,128)} %get-tuple-element.25.refs_2_) | copy-start | bytes 602116
  34.1 10.1 %collective-permute-start.4 = (f32[392,128]{1,0:T(8,128)}, f32[392,128]{1,0:T(8,128)S(1)}, u32[]{:S(2)}, u32[]{:S(2)}) collective-permute-start(f32[392,128]{1,0:T(8,128)} %get-tuple-element.25.refs_2_), channel_id=1, source_target_pairs={{0,2},{1,3},{2,0},{3,1},{4,6},{5,7},{6,4},{7,5},{8,10},{9,11},{10,... | collective-permute-start | bytes 602120 | tf_op jit(solution)/shard_map/ppermute | solution.py:95
  42.2 7.4 %collective-permute-start.10 = (f32[4,288,128]{2,1,0:T(8,128)S(1)}, f32[4,288,128]{2,1,0:T(8,128)S(1)}, u32[]{:S(2)}, u32[]{:S(2)}) collective-permute-start(f32[4,288,128]{2,1,0:T(8,128)S(1)} %get-tuple-element.32), channel_id=1, source_target_pairs={{0,4},{1,5},{2,6},{3,7},{4,0},{5,1},{6,2},{7,3},{8,12},{9,13},{10,... | collective-permute-start | bytes 1769480 | tf_op jit(solution)/shard_map/ppermute | solution.py:95
  49.5 2.1 %collective-permute-start.6 = (f32[4,288,128]{2,1,0:T(8,128)S(1)}, f32[4,288,128]{2,1,0:T(8,128)S(1)}, u32[]{:S(2)}, u32[]{:S(2)}) collective-permute-start(f32[4,288,128]{2,1,0:T(8,128)S(1)} %get-tuple-element.28), channel_id=1, source_target_pairs={{0,4},{1,5},{2,6},{3,7},{4,0},{5,1},{6,2},{7,3},{8,12},{9,13},{10,... | collective-permute-start | bytes 1769480 | tf_op jit(solution)/shard_map/ppermute | solution.py:95
  53.3 1.3 %collective-permute-start.11 = (f32[8,128]{1,0:T(8,128)S(1)}, f32[8,128]{1,0:T(8,128)S(1)}, u32[]{:S(2)}, u32[]{:S(2)}) collective-permute-start(f32[8,128]{1,0:T(8,128)S(1)} %shard_map.40), channel_id=1, source_target_pairs={{0,4},{1,5},{2,6},{3,7},{4,0},{5,1},{6,2},{7,3},{8,12},{9,13},{10,... | collective-permute-start | bytes 12296 | tf_op jit(solution)/shard_map/ppermute | solution.py:95
  54.6 3.6 %collective-permute-start.12 = (f32[8,128]{1,0:T(8,128)S(1)}, f32[8,128]{1,0:T(8,128)S(1)}, u32[]{:S(2)}, u32[]{:S(2)}) collective-permute-start(f32[8,128]{1,0:T(8,128)S(1)} %add.32.t0), channel_id=1, source_target_pairs={{0,1},{1,0},{2,3},{3,2},{4,5},{5,4},{6,7},{7,6},{8,9},{9,8},{10,11... | collective-permute-start | bytes 12296 | tf_op jit(solution)/shard_map/ppermute | solution.py:95
  55.1 3.6 %collective-permute-start.13 = (f32[8,128]{1,0:T(8,128)S(1)}, f32[8,128]{1,0:T(8,128)S(1)}, u32[]{:S(2)}, u32[]{:S(2)}) collective-permute-start(f32[8,128]{1,0:T(8,128)S(1)} %add.32.t0), channel_id=1, source_target_pairs={{0,2},{1,3},{2,0},{3,1},{4,6},{5,7},{6,4},{7,5},{8,10},{9,11},{10,... | collective-permute-start | bytes 12296 | tf_op jit(solution)/shard_map/ppermute | solution.py:95
  56.4 4.5 %collective-permute-start.14 = (f32[8,128]{1,0:T(8,128)S(1)}, f32[8,128]{1,0:T(8,128)S(1)}, u32[]{:S(2)}, u32[]{:S(2)}) collective-permute-start(f32[8,128]{1,0:T(8,128)S(1)} %add.32.t0), channel_id=1, source_target_pairs={{0,3},{1,2},{2,1},{3,0},{4,7},{5,6},{6,5},{7,4},{8,11},{9,10},{10,... | collective-permute-start | bytes 12296 | tf_op jit(solution)/shard_map/ppermute | solution.py:95
  63.5 12.0 %collective-permute-start.15 = (f32[288,128]{1,0:T(8,128)S(1)}, f32[288,128]{1,0:T(8,128)S(1)}, u32[]{:S(2)}, u32[]{:S(2)}) collective-permute-start(f32[288,128]{1,0:T(8,128)S(1)} %get-tuple-element.33), channel_id=1, source_target_pairs={{0,0},{1,4},{2,2},{3,6},{4,8},{5,12},{6,10},{7,14},{8,1},{9,5},{10... | collective-permute-start | bytes 442376 | tf_op jit(solution)/shard_map/ppermute | solution.py:95
  64.2 12.2 %collective-permute-start.16 = (f32[288,128]{1,0:T(8,128)S(1)}, f32[288,128]{1,0:T(8,128)S(1)}, u32[]{:S(2)}, u32[]{:S(2)}) collective-permute-start(f32[288,128]{1,0:T(8,128)S(1)} %get-tuple-element.34), channel_id=1, source_target_pairs={{0,1},{1,5},{2,3},{3,7},{4,9},{5,13},{6,11},{7,15},{8,0},{9,4},{10... | collective-permute-start | bytes 442376 | tf_op jit(solution)/shard_map/ppermute | solution.py:95
  66.4 13.1 %collective-permute-start.17 = (f32[288,128]{1,0:T(8,128)S(1)}, f32[288,128]{1,0:T(8,128)S(1)}, u32[]{:S(2)}, u32[]{:S(2)}) collective-permute-start(f32[288,128]{1,0:T(8,128)S(1)} %get-tuple-element.35), channel_id=1, source_target_pairs={{0,2},{1,6},{2,0},{3,4},{4,10},{5,14},{6,8},{7,12},{8,3},{9,7},{10... | collective-permute-start | bytes 442376 | tf_op jit(solution)/shard_map/ppermute | solution.py:95
  67.8 13.2 %collective-permute-start.18 = (f32[288,128]{1,0:T(8,128)S(1)}, f32[288,128]{1,0:T(8,128)S(1)}, u32[]{:S(2)}, u32[]{:S(2)}) collective-permute-start(f32[288,128]{1,0:T(8,128)S(1)} %get-tuple-element.36), channel_id=1, source_target_pairs={{0,3},{1,7},{2,1},{3,5},{4,11},{5,15},{6,9},{7,13},{8,2},{9,6},{10... | collective-permute-start | bytes 442376 | tf_op jit(solution)/shard_map/ppermute | solution.py:95
  72.8 20.3 %collective-permute-start.19 = (f32[288,128]{1,0:T(8,128)S(1)}, f32[288,128]{1,0:T(8,128)S(1)}, u32[]{:S(2)}, u32[]{:S(2)}) collective-permute-start(f32[288,128]{1,0:T(8,128)S(1)} %get-tuple-element.37), channel_id=1, source_target_pairs={{0,16},{1,20},{2,18},{3,22},{4,24},{5,28},{6,26},{7,30},{8,17},{9,... | collective-permute-start | bytes 442376 | tf_op jit(solution)/shard_map/ppermute | solution.py:95
  75.5 17.7 %collective-permute-start.20 = (f32[288,128]{1,0:T(8,128)S(1)}, f32[288,128]{1,0:T(8,128)S(1)}, u32[]{:S(2)}, u32[]{:S(2)}) collective-permute-start(f32[288,128]{1,0:T(8,128)S(1)} %get-tuple-element.38), channel_id=1, source_target_pairs={{0,17},{1,21},{2,19},{3,23},{4,25},{5,29},{6,27},{7,31},{8,16},{9,... | collective-permute-start | bytes 442376 | tf_op jit(solution)/shard_map/ppermute | solution.py:95
  76.4 23.8 %collective-permute-start.21 = (f32[288,128]{1,0:T(8,128)S(1)}, f32[288,128]{1,0:T(8,128)S(1)}, u32[]{:S(2)}, u32[]{:S(2)}) collective-permute-start(f32[288,128]{1,0:T(8,128)S(1)} %get-tuple-element.39), channel_id=1, source_target_pairs={{0,18},{1,22},{2,16},{3,20},{4,26},{5,30},{6,24},{7,28},{8,19},{9,... | collective-permute-start | bytes 442376 | tf_op jit(solution)/shard_map/ppermute | solution.py:95
  79.5 20.7 %collective-permute-start.22 = (f32[288,128]{1,0:T(8,128)S(1)}, f32[288,128]{1,0:T(8,128)S(1)}, u32[]{:S(2)}, u32[]{:S(2)}) collective-permute-start(f32[288,128]{1,0:T(8,128)S(1)} %get-tuple-element.40), channel_id=1, source_target_pairs={{0,19},{1,23},{2,17},{3,21},{4,27},{5,31},{6,25},{7,29},{8,18},{9,... | collective-permute-start | bytes 442376 | tf_op jit(solution)/shard_map/ppermute | solution.py:95
  102.6 6.3 %collective-permute-start.24 = (f32[16,128]{1,0:T(8,128)S(1)}, f32[16,128]{1,0:T(8,128)S(1)}, u32[]{:S(2)}, u32[]{:S(2)}) collective-permute-start(f32[16,128]{1,0:T(8,128)S(1)} %gram.1), channel_id=1, source_target_pairs={{0,16},{1,17},{2,18},{3,19},{4,20},{5,21},{6,22},{7,23},{8,24},{9,... | collective-permute-start | bytes 24584 | tf_op jit(solution)/shard_map/ppermute | solution.py:95
  107.0 5.4 %collective-permute-start.25 = (f32[16,128]{1,0:T(8,128)S(1)}, f32[16,128]{1,0:T(8,128)S(1)}, u32[]{:S(2)}, u32[]{:S(2)}) collective-permute-start(f32[16,128]{1,0:T(8,128)S(1)} %gram.1), channel_id=1, source_target_pairs={{0,24},{1,25},{2,26},{3,27},{4,28},{5,29},{6,30},{7,31},{8,16},{9,... | collective-permute-start | bytes 24584 | tf_op jit(solution)/shard_map/ppermute | solution.py:95
  108.4 4.1 %collective-permute-start.23 = (f32[16,128]{1,0:T(8,128)S(1)}, f32[16,128]{1,0:T(8,128)S(1)}, u32[]{:S(2)}, u32[]{:S(2)}) collective-permute-start(f32[16,128]{1,0:T(8,128)S(1)} %gram.1), channel_id=1, source_target_pairs={{0,8},{1,9},{2,10},{3,11},{4,12},{5,13},{6,14},{7,15},{8,0},{9,1},... | collective-permute-start | bytes 24584 | tf_op jit(solution)/shard_map/ppermute | solution.py:95
  112.5 1.2 %collective-permute-start.26 = (f32[16,128]{1,0:T(8,128)S(1)}, f32[16,128]{1,0:T(8,128)S(1)}, u32[]{:S(2)}, u32[]{:S(2)}) collective-permute-start(f32[16,128]{1,0:T(8,128)S(1)} %add_add_fusion), channel_id=1, source_target_pairs={{0,4},{1,5},{2,6},{3,7},{4,0},{5,1},{6,2},{7,3},{8,12},{9,13},{10,... | collective-permute-start | bytes 24584 | tf_op jit(solution)/shard_map/ppermute | solution.py:95
  113.7 3.7 %collective-permute-start.27 = (f32[16,128]{1,0:T(8,128)S(1)}, f32[16,128]{1,0:T(8,128)S(1)}, u32[]{:S(2)}, u32[]{:S(2)}) collective-permute-start(f32[16,128]{1,0:T(8,128)S(1)} %add.36.refs_0_), channel_id=1, source_target_pairs={{0,1},{1,0},{2,3},{3,2},{4,5},{5,4},{6,7},{7,6},{8,9},{9,8},{10,11... | collective-permute-start | bytes 24584 | tf_op jit(solution)/shard_map/ppermute | solution.py:95
  113.8 3.7 %collective-permute-start.28 = (f32[16,128]{1,0:T(8,128)S(1)}, f32[16,128]{1,0:T(8,128)S(1)}, u32[]{:S(2)}, u32[]{:S(2)}) collective-permute-start(f32[16,128]{1,0:T(8,128)S(1)} %add.36.refs_0_), channel_id=1, source_target_pairs={{0,2},{1,3},{2,0},{3,1},{4,6},{5,7},{6,4},{7,5},{8,10},{9,11},{10,... | collective-permute-start | bytes 24584 | tf_op jit(solution)/shard_map/ppermute | solution.py:95
  114.5 4.5 %collective-permute-start.29 = (f32[16,128]{1,0:T(8,128)S(1)}, f32[16,128]{1,0:T(8,128)S(1)}, u32[]{:S(2)}, u32[]{:S(2)}) collective-permute-start(f32[16,128]{1,0:T(8,128)S(1)} %add.36.refs_0_), channel_id=1, source_target_pairs={{0,3},{1,2},{2,1},{3,0},{4,7},{5,6},{6,5},{7,4},{8,11},{9,10},{10,... | collective-permute-start | bytes 24584 | tf_op jit(solution)/shard_map/ppermute | solution.py:95
  (1 other events, 0.9 us)

commit v3 on v2

--- a/solution.py
+++ b/solution.py
@@ -189,7 +189,7 @@
     for copy in copies:
         copy.wait()
     for r in range(side):
-        strip = gather(buf, r, side)
+        strip = gather([buf.at[i] for i in range(4)], r, side)
         strip = strip.reshape(-1, width)
         strip = jnp.concatenate([strip, jnp.zeros((span - strip.shape[0], width), jnp.float32)], axis=0)
         xh, xl = split2(strip.T)
@@ -197,25 +197,22 @@
         out_ref[r, :, span:] = xl
 
 
-def gather(buf, r, side):
-    strip = buf.shape[1] // side
-    parts = [buf[i, r * strip : (r + 1) * strip, :].reshape(side, strip // side, -1) for i in range(4)]
+def gather(refs, r, side):
+    strip = refs[0].shape[0] // side
+    parts = [ref[r * strip : (r + 1) * strip, :].reshape(side, strip // side, -1) for ref in refs]
     return jnp.concatenate(parts, axis=1)
 
 
 def gradient_kernel(scale, side, s_ref, xt_ref, *refs):
-    sources, (keep_ref, send_ref, buf, rh, rl, g_ref, sems) = refs[:4], refs[4:]
+    sources, (keep_ref, send_ref, rh, rl, g_ref) = refs[:4], refs[4:]
     xt = xt_ref
-    copies = fetch(sources, [buf.at[i] for i in range(4)], sems)
-    width = buf.shape[2]
+    width = sources[0].shape[1]
     span = xt.shape[2] // 2
     for ref in (rh, rl):
         for edge in (0, side + 1, side + 2):
             ref[:, edge] = jnp.zeros((side,) + ref.shape[2:], jnp.bfloat16)
-    for copy in copies:
-        copy.wait()
     for r in range(side):
-        h, lo = split2(gather(buf, r, side))
+        h, lo = split2(gather(sources, r, side))
         rh[r, 1 : side + 1] = h
         rl[r, 1 : side + 1] = lo
     totals = [None] * 9
@@ -257,21 +254,16 @@
 
 
 def pair_dots_kernel(s_ref, keep_ref, received_ref, *refs):
-    out_ref, buf, sems = refs[-3:]
     core = s_ref[0]
-    count = keep_ref.shape[0]
-    sources = [ref.at[d] for d in range(count) for ref in (keep_ref, received_ref)]
-    copies = fetch(sources, [buf.at[i] for i in range(2 * count)], sems)
+    out_ref = refs[-1]
     cross = mine = theirs = jnp.zeros((1, out_ref.shape[1]), jnp.float32)
-    for d in range(count):
-        copies[2 * d].wait()
-        copies[2 * d + 1].wait()
-        a, b = buf[2 * d], buf[2 * d + 1]
+    for d in range(keep_ref.shape[0]):
+        a, b = keep_ref[d], received_ref[d]
         cross += column_sums(a, b)
         mine += column_sums(a, a)
         theirs += column_sums(b, b)
     left, right = jnp.where(core == 0, mine, theirs), jnp.where(core == 0, theirs, mine)
-    if len(refs) > 3:
+    if len(refs) > 1:
         before = refs[0]
         cross, left, right = cross + before[0:1], left + before[1:2], right + before[2:3]
     out_ref[...] = jnp.zeros(out_ref.shape, jnp.float32)
@@ -284,57 +276,39 @@
     return 1.0 - cross / (2.0 * (left_sq + epsilon)), 1.0 - cross / (2.0 * (right_sq + epsilon))
 
 
-def pair_mix_kernel(s_ref, t0, t1, t2, t3, keep_ref, received_ref, *refs):
+def sum_four(refs):
+    return (refs[0][...] + refs[1][...]) + (refs[2][...] + refs[3][...])
+
+
+def pair_mix_kernel(s_ref, t0, t1, t2, t3, keep_ref, received_ref, *out_refs):
     core = s_ref[0]
-    count = keep_ref.shape[0]
-    out_refs, (buf, sums, in_sems, out_sems) = refs[:count], refs[count:]
-    order = list(range(count - 1, -1, -1))
-    slots = [sums.at[i] for i in range(4)] + [buf.at[i] for i in range(2 * count)]
-    copies = fetch([t0, t1, t2, t3] + [ref.at[d] for d in order for ref in (keep_ref, received_ref)], slots, in_sems)
-    for copy in copies[:4]:
-        copy.wait()
-    totals = jnp.sum((sums[0] + sums[1]) + (sums[2] + sums[3]), axis=1, keepdims=True)
+    totals = jnp.sum(sum_four((t0, t1, t2, t3)), axis=1, keepdims=True)
     left, right = pair_coefs(totals[0:1], totals[1:2], totals[2:3])
     keep_coef = jnp.where(core == 0, left, right)
     received_coef = jnp.where(core == 0, right, left)
-    stores = []
-    for i, d in enumerate(order):
-        copies[4 + 2 * i].wait()
-        copies[5 + 2 * i].wait()
-        buf[2 * i] = keep_coef * buf[2 * i] + received_coef * buf[2 * i + 1]
-        stores.append(pltpu.make_async_copy(buf.at[2 * i], out_refs[d], out_sems.at[i]))
-        stores[-1].start()
-    for store in stores:
-        store.wait()
+    for d, out in enumerate(out_refs):
+        out[...] = keep_coef * keep_ref[d] + received_coef * received_ref[d]
 
 
 def gram_kernel(s_ref, *refs):
     upper, x = s_ref[0], s_ref[1]
-    blocks, (gram_ref, buf, sems) = refs[:8], refs[8:]
-    copies = fetch(blocks, [buf.at[slot_of(i)] for i in range(8)], sems)
+    blocks, gram_ref = refs[:8], refs[8]
     node = [2 * jnp.bitwise_xor(upper, d // 2) + jnp.bitwise_xor(x, d % 2) for d in range(4)]
-    for i in (0, 1, 2, 3, 4, 5, 6, 7):
-        copies[i].wait()
     for e in range(4):
         for d in range(e + 1):
-            value = column_sums(buf[2 * d : 2 * d + 2], buf[2 * e : 2 * e + 2])
+            value = sum(column_sums(blocks[slot_of(d, dy)][...], blocks[slot_of(e, dy)][...]) for dy in range(2))
             gram_ref[pl.ds(4 * node[d] + node[e], 1)] = value
             gram_ref[pl.ds(4 * node[e] + node[d], 1)] = value
 
 
-def slot_of(index):
-    e, dy, dx = index // 4, index // 2 % 2, index % 2
-    return 4 * e + 2 * dx + dy
+def slot_of(d, dy):
+    return 4 * (d // 2) + 2 * dy + d % 2
 
 
 def place_kernel(s_ref, *refs):
     upper, x, y = s_ref[0], s_ref[1], s_ref[2]
-    sources, (out_ref, parts, sums, rows_ref, sems) = refs[:12], refs[12:]
-    slots = [sums.at[i] for i in range(4)] + [parts.at[slot_of(i)] for i in range(8)]
-    copies = fetch(sources, slots, sems)
-    for copy in copies[:4]:
-        copy.wait()
-    gram = jnp.sum((sums[0] + sums[1]) + (sums[2] + sums[3]), axis=1, keepdims=True)
+    blocks, (out_ref, rows_ref) = refs[4:12], refs[12:]
+    gram = jnp.sum(sum_four(refs[:4]), axis=1, keepdims=True)
     g = lambda a, b: gram[4 * a + b : 4 * a + b + 1]
     p = pair_coefs(g(0, 1), g(0, 0), g(1, 1)) + pair_coefs(g(2, 3), g(2, 2), g(3, 3))
     cross = p[0] * (p[2] * g(0, 2) + p[3] * g(0, 3)) + p[1] * (p[2] * g(1, 2) + p[3] * g(1, 3))
@@ -349,10 +323,8 @@
         for a in range(3):
             coef = jnp.where(owner == a, absolute[a], coef)
         coefs.append(coef)
-    for copy in copies[4:]:
-        copy.wait()
     for dy in range(2):
-        part = [parts[2 * d + dy] for d in range(4)]
+        part = [blocks[slot_of(d, dy)][...] for d in range(4)]
         block = coefs[0] * part[0] + coefs[1] * part[1] + (coefs[2] * part[2] + coefs[3] * part[3])
         upper_half = pltpu.roll(block, HALF, 1)
         rows = jnp.concatenate([block[:, :HALF], upper_half[:, :HALF]], axis=0)
@@ -454,14 +426,12 @@
         return pl.pallas_call(
             lambda *refs: gradient_kernel(1.0 / rows, side, *refs),
             out_shape=(f32(half, part, 128), f32(half, part, 128)),
-            in_specs=[SM, VM] + [HB] * 4,
+            in_specs=[SM] + [VM] * 5,
             out_specs=(VM, VM),
             scratch_shapes=[
-                pltpu.VMEM((4, rows, 128), jnp.float32),
                 pltpu.VMEM((side, side + 3, 4 * imgs, 128), jnp.bfloat16),
                 pltpu.VMEM((side, side + 3, 4 * imgs, 128), jnp.bfloat16),
                 pltpu.VMEM((taps * width // BLK, BLK, 128), jnp.float32),
-                pltpu.SemaphoreType.DMA((4,)),
             ],
             cost_estimate=pl.CostEstimate(
                 flops=24 * rows * taps * width * 128, bytes_accessed=4 * taps * width * 128, transcendentals=0
@@ -473,9 +443,8 @@
         return pl.pallas_call(
             pair_dots_kernel,
             out_shape=f32(8, 128),
-            in_specs=[SM, HB, HB] + [VM] * len(before),
+            in_specs=[SM, VM, VM] + [VM] * len(before),
             out_specs=VM,
-            scratch_shapes=[pltpu.VMEM((2 * half, part, 128), jnp.float32), pltpu.SemaphoreType.DMA((2 * half,))],
             compiler_params=pltpu.CompilerParams(vmem_limit_bytes=SHARED),
         )(scalars(c), keep, received, *before)
 
@@ -491,14 +460,8 @@
         return pl.pallas_call(
             pair_mix_kernel,
             out_shape=(f32(part, 128),) * half,
-            in_specs=[SM] + [HB] * 6,
-            out_specs=(HB,) * half,
-            scratch_shapes=[
-                pltpu.VMEM((2 * half, part, 128), jnp.float32),
-                pltpu.VMEM((4, 8, 128), jnp.float32),
-                pltpu.SemaphoreType.DMA((4 + 2 * half,)),
-                pltpu.SemaphoreType.DMA((half,)),
-            ],
+            in_specs=[SM] + [VM] * 6,
+            out_specs=(VM,) * half,
             compiler_params=pltpu.CompilerParams(vmem_limit_bytes=SHARED),
         )(scalars(c), *totals, keep, received)
 
@@ -513,9 +476,8 @@
     gram = pl.pallas_call(
         gram_kernel,
         out_shape=f32(16, 128),
-        in_specs=[SM] + [HB] * count,
+        in_specs=[SM] + [VM] * count,
         out_specs=VM,
-        scratch_shapes=[pltpu.VMEM((count, part, 128), jnp.float32), pltpu.SemaphoreType.DMA((count,))],
         compiler_params=pltpu.CompilerParams(vmem_limit_bytes=SHARED),
         name="gram",
     )(place, *moved)
@@ -524,14 +486,9 @@
     out = pl.pallas_call(
         place_kernel,
         out_shape=f32(HALF, 4 * part),
-        in_specs=[SM] + [HB] * (4 + count),
+        in_specs=[SM] + [VM] * (4 + count),
         out_specs=VM,
-        scratch_shapes=[
-            pltpu.VMEM((count, part, 128), jnp.float32),
-            pltpu.VMEM((4, 16, 128), jnp.float32),
-            pltpu.VMEM((2 * part // HALF, 2, HALF, HALF), jnp.float32),
-            pltpu.SemaphoreType.DMA((4 + count,)),
-        ],
+        scratch_shapes=[pltpu.VMEM((2 * part // HALF, 2, HALF, HALF), jnp.float32)],
         compiler_params=pltpu.CompilerParams(vmem_limit_bytes=SHARED),
         name="place",
     )(place, *gram, *moved)

time: 123 us -> 112 us (0.911)
  Pallas kernels: 40.5 us -> 27 us
  starting transfers between devices: 43.1 us -> 44.7 us
  waiting for transfers between devices: 36 us -> 37.4 us
    pallas_call x2, Pallas kernels: 5.28 us -> 0.42 us  [mix(): pl.pallas_call(pair_mix_kernel, out_shape=(f32(part, 128),) * half, in_sp...]
    pallas_call x3, Pallas kernels: 6.02 us -> 1.18 us  [the longest x1 0.78 us: tiles(): pl.pallas_call(gram_kernel, out_shape=f32(16, 128), in_specs=[SM] + [VM]...]
    pallas_call x2, Pallas kernels: 10.5 us -> 8.34 us  [gradient(): pl.pallas_call(lambda *refs: gradient_kernel(1.0 / rows, side, *refs), ou...]
    pallas_call x1, Pallas kernels: 3.44 us -> 1.77 us  [tiles(): pl.pallas_call(place_kernel, out_shape=f32(HALF, 4 * part), in_specs=[SM]...]
    ppermute x30, starting transfers between devices: 43.1 us -> 44.7 us  [hop(): return lax.ppermute(value, ('node', 'local'), pairs)]
    ppermute x30, waiting for transfers between devices: 36 us -> 37.4 us  [hop(): return lax.ppermute(value, ('node', 'local'), pairs)]
  transfers between devices with their start and end apart: 30 -> 30, of which waited for: 14 -> 14; matrix products, arithmetic and copies ran while one was open for 1% -> 1% of each run, Pallas kernels for 23% -> 19%
where the time goes in v3:
time: 112 us
  starting transfers between devices  44.7 us (40%)
  waiting for transfers between devices  37.4 us (33%)
  Pallas kernels  27 us (24%)
  local copies, waits for them, and re-layouts  1.93 us (2%)
    ppermute x30, starting transfers between devices, hop(): return lax.ppermute(value, ('node', 'local'), pairs)  44.7 us
    ppermute x30, waiting for transfers between devices, hop(): return lax.ppermute(value, ('node', 'local'), pairs)  37.4 us
    pallas_call x1, Pallas kernels, tiles(): pl.pallas_call(residual_kernel, out_shape=(f32(rows, 128),) * 4, in_specs...  10.8 us
    pallas_call x2, Pallas kernels, gradient(): pl.pallas_call(lambda *refs: gradient_kernel(1.0 / rows, side, *refs), ou...  8.34 us
    pallas_call x1, Pallas kernels, tiles(): pl.pallas_call(split_kernel, out_shape=(f32(rows, width), f32(rows, width...  2.45 us
  transfers between devices with their start and end apart: 30, of which 14 were waited for; matrix products, arithmetic and copies ran while one was open for 1% of the time, Pallas kernels for 19%

profile of v3, /device:TPU:0, one launch (start us, length us, event | category | flops | bytes accessed | tf_op | source)
XLA Modules:
  0.0 111.8 jit_solution(95318279570013570)
XLA Ops:
  0.0 2.4 %split_images.1 = (f32[392,256]{1,0:T(8,128)}, f32[392,256]{1,0:T(8,128)}) custom-call(s32[1]{0:T(128)} %bitcast.2.s_ref, f32[392,512]{1,0:T(8,128)} %bitcast.13), custom_call_target="tpu_custom_call" | custom-call | tf_op jit(solution)/shard_map/split_images/pallas_call | solution.py:364
  2.5 3.1 %collective-permute-start.1 = (f32[392,256]{1,0:T(8,128)}, f32[392,256]{1,0:T(8,128)}, u32[]{:S(2)}, u32[]{:S(2)}) collective-permute-start(f32[392,256]{1,0:T(8,128)} %get-tuple-element.24), channel_id=1, source_target_pairs={{0,2},{1,3},{2,0},{3,1},{4,6},{5,7},{6,4},{7,5},{8,10},{9,11},{10,... | collective-permute-start | bytes 1204232 | tf_op jit(solution)/shard_map/ppermute | solution.py:95
  5.5 1.4 %collective-permute-start.2 = (f32[392,256]{1,0:T(8,128)}, f32[392,256]{1,0:T(8,128)}, u32[]{:S(2)}, u32[]{:S(2)}) collective-permute-start(f32[392,256]{1,0:T(8,128)} %get-tuple-element.24), channel_id=1, source_target_pairs={{0,3},{1,2},{2,1},{3,0},{4,7},{5,6},{6,5},{7,4},{8,11},{9,10},{10,... | collective-permute-start | bytes 1204232 | tf_op jit(solution)/shard_map/ppermute | solution.py:95
  7.7 10.8 %residual.1 = (f32[392,128]{1,0:T(8,128)}, f32[392,128]{1,0:T(8,128)}, f32[392,128]{1,0:T(8,128)}, f32[392,128]{1,0:T(8,128)}) custom-call(s32[2]{0:T(128)} %pad_add_fusion.2.s_ref, f32[392,512]{1,0:T(8,128)} %bitcast.14, f32[392,512]{1,0:T(8,128)} %bitcast.16, f32[9,512,512]{2,1,0:T(8,128)} %bitcast.15), custom_call_target="tpu_custom_call" | custom-call | flops 5549064192 | bytes 9437184 | tf_op jit(solution)/shard_map/residual/pallas_call | solution.py:384
  18.5 2.0 %collective-permute-start.7 = (f32[392,128]{1,0:T(8,128)}, f32[392,128]{1,0:T(8,128)S(1)}, u32[]{:S(2)}, u32[]{:S(2)}) collective-permute-start(f32[392,128]{1,0:T(8,128)} %get-tuple-element.30), channel_id=1, source_target_pairs={{0,1},{1,0},{2,3},{3,2},{4,5},{5,4},{6,7},{7,6},{8,9},{9,8},{10,11... | collective-permute-start | bytes 602120 | tf_op jit(solution)/shard_map/ppermute | solution.py:95
  20.4 1.5 %collective-permute-start.8 = (f32[392,128]{1,0:T(8,128)}, f32[392,128]{1,0:T(8,128)S(1)}, u32[]{:S(2)}, u32[]{:S(2)}) collective-permute-start(f32[392,128]{1,0:T(8,128)} %get-tuple-element.29.refs_2_), channel_id=1, source_target_pairs={{0,2},{1,3},{2,0},{3,1},{4,6},{5,7},{6,4},{7,5},{8,10},{9,11},{10,... | collective-permute-start | bytes 602120 | tf_op jit(solution)/shard_map/ppermute | solution.py:95
  22.0 4.2 %collective-permute-done.refs_1_ = f32[392,256]{1,0:T(8,128)} collective-permute-done((f32[392,256]{1,0:T(8,128)}, f32[392,256]{1,0:T(8,128)}, u32[]{:S(2)}, u32[]{:S(2)}) %collective-permute-start) | collective-permute-done | bytes 401440 | tf_op jit(solution)/shard_map/ppermute | solution.py:95
  26.1 2.9 %collective-permute-start.9 = (f32[392,128]{1,0:T(8,128)}, f32[392,128]{1,0:T(8,128)S(1)}, u32[]{:S(2)}, u32[]{:S(2)}) collective-permute-start(f32[392,128]{1,0:T(8,128)} %get-tuple-element.30), channel_id=1, source_target_pairs={{0,3},{1,2},{2,1},{3,0},{4,7},{5,6},{6,5},{7,4},{8,11},{9,10},{10,... | collective-permute-start | bytes 602120 | tf_op jit(solution)/shard_map/ppermute | solution.py:95
  29.6 1.4 %collective-permute-start.5 = (f32[392,128]{1,0:T(8,128)}, f32[392,128]{1,0:T(8,128)S(1)}, u32[]{:S(2)}, u32[]{:S(2)}) collective-permute-start(f32[392,128]{1,0:T(8,128)} %get-tuple-element.26), channel_id=1, source_target_pairs={{0,3},{1,2},{2,1},{3,0},{4,7},{5,6},{6,5},{7,4},{8,11},{9,10},{10,... | collective-permute-start | bytes 602120 | tf_op jit(solution)/shard_map/ppermute | solution.py:95
  32.0 2.0 %prepare.1.refs_1_ = bf16[7,256,512]{2,1,0:T(8,128)(2,1)S(1)} custom-call(f32[392,256]{1,0:T(8,128)S(1)} %copy-done, f32[392,256]{1,0:T(8,128)} %collective-permute-done.refs_1_, f32[392,256]{1,0:T(8,128)} %collective-permute-done.1.refs_2_, f32[392,256]{1,0:T(8,128)} %collective-permute-done.2.refs_3_), custom_call_target="tpu_custom_call" | custom-call | tf_op jit(solution)/shard_map/prepare/pallas_call | solution.py:409
  34.1 1.6 %collective-permute-start.4 = (f32[392,128]{1,0:T(8,128)}, f32[392,128]{1,0:T(8,128)S(1)}, u32[]{:S(2)}, u32[]{:S(2)}) collective-permute-start(f32[392,128]{1,0:T(8,128)} %get-tuple-element.25.refs_2_), channel_id=1, source_target_pairs={{0,2},{1,3},{2,0},{3,1},{4,6},{5,7},{6,4},{7,5},{8,10},{9,11},{10,... | collective-permute-start | bytes 602120 | tf_op jit(solution)/shard_map/ppermute | solution.py:95
  36.9 4.2 %shard_map.38 = (f32[4,288,128]{2,1,0:T(8,128)S(1)}, f32[4,288,128]{2,1,0:T(8,128)S(1)}) custom-call(s32[3]{0:T(128)S(1)} %pad_add_fusion.1.refs_0_, bf16[7,256,512]{2,1,0:T(8,128)(2,1)S(1)} %prepare.1.refs_1_, f32[392,128]{1,0:T(8,128)S(1)} %copy-done.2, f32[392,128]{1,0:T(8,128)S(1)} %collective-permute-done.7.refs_3_, ...), custom_call_target="tpu_custom_call" | custom-call | flops 2774532096 | bytes 1179648 | tf_op jit(solution)/shard_map/pallas_call | solution.py:426
  41.2 3.0 %collective-permute-done.4.refs_4_ = f32[392,128]{1,0:T(8,128)S(1)} collective-permute-done((f32[392,128]{1,0:T(8,128)}, f32[392,128]{1,0:T(8,128)S(1)}, u32[]{:S(2)}, u32[]{:S(2)}) %collective-permute-start.4) | collective-permute-done | bytes 200736 | tf_op jit(solution)/shard_map/ppermute | solution.py:95
  44.2 4.2 %shard_map.37 = (f32[4,288,128]{2,1,0:T(8,128)S(1)}, f32[4,288,128]{2,1,0:T(8,128)S(1)}) custom-call(s32[3]{0:T(128)S(1)} %pad_add_fusion.1.refs_0_, bf16[7,256,512]{2,1,0:T(8,128)(2,1)S(1)} %prepare.1.refs_1_, f32[392,128]{1,0:T(8,128)S(1)} %copy-done.1, f32[392,128]{1,0:T(8,128)S(1)} %collective-permute-done.3.refs_3_, ...), custom_call_target="tpu_custom_call" | custom-call | flops 2774532096 | bytes 1179648 | tf_op jit(solution)/shard_map/pallas_call | solution.py:426
  48.7 1.8 %collective-permute-done.6.received_ref = f32[4,288,128]{2,1,0:T(8,128)S(1)} collective-permute-done((f32[4,288,128]{2,1,0:T(8,128)S(1)}, f32[4,288,128]{2,1,0:T(8,128)S(1)}, u32[]{:S(2)}, u32[]{:S(2)}) %collective-permute-start.6) | collective-permute-done | bytes 589856 | tf_op jit(solution)/shard_map/ppermute | solution.py:95
  53.6 1.7 %collective-permute-start.14 = (f32[8,128]{1,0:T(8,128)S(1)}, f32[8,128]{1,0:T(8,128)S(1)}, u32[]{:S(2)}, u32[]{:S(2)}) collective-permute-start(f32[8,128]{1,0:T(8,128)S(1)} %add.32.t0), channel_id=1, source_target_pairs={{0,3},{1,2},{2,1},{3,0},{4,7},{5,6},{6,5},{7,4},{8,11},{9,10},{10,... | collective-permute-start | bytes 12296 | tf_op jit(solution)/shard_map/ppermute | solution.py:95
  56.0 2.1 %collective-permute-done.14.t3 = f32[8,128]{1,0:T(8,128)S(1)} collective-permute-done((f32[8,128]{1,0:T(8,128)S(1)}, f32[8,128]{1,0:T(8,128)S(1)}, u32[]{:S(2)}, u32[]{:S(2)}) %collective-permute-start.14) | collective-permute-done | bytes 4128 | tf_op jit(solution)/shard_map/ppermute | solution.py:95
  59.0 2.2 %collective-permute-start.16 = (f32[288,128]{1,0:T(8,128)S(1)}, f32[288,128]{1,0:T(8,128)S(1)}, u32[]{:S(2)}, u32[]{:S(2)}) collective-permute-start(f32[288,128]{1,0:T(8,128)S(1)} %get-tuple-element.34), channel_id=1, source_target_pairs={{0,1},{1,5},{2,3},{3,7},{4,9},{5,13},{6,11},{7,15},{8,0},{9,4},{10... | collective-permute-start | bytes 442376 | tf_op jit(solution)/shard_map/ppermute | solution.py:95
  61.2 1.4 %collective-permute-start.17 = (f32[288,128]{1,0:T(8,128)S(1)}, f32[288,128]{1,0:T(8,128)S(1)}, u32[]{:S(2)}, u32[]{:S(2)}) collective-permute-start(f32[288,128]{1,0:T(8,128)S(1)} %get-tuple-element.35), channel_id=1, source_target_pairs={{0,2},{1,6},{2,0},{3,4},{4,10},{5,14},{6,8},{7,12},{8,3},{9,7},{10... | collective-permute-start | bytes 442376 | tf_op jit(solution)/shard_map/ppermute | solution.py:95
  62.6 2.4 %collective-permute-start.18 = (f32[288,128]{1,0:T(8,128)S(1)}, f32[288,128]{1,0:T(8,128)S(1)}, u32[]{:S(2)}, u32[]{:S(2)}) collective-permute-start(f32[288,128]{1,0:T(8,128)S(1)} %get-tuple-element.36), channel_id=1, source_target_pairs={{0,3},{1,7},{2,1},{3,5},{4,11},{5,15},{6,9},{7,13},{8,2},{9,6},{10... | collective-permute-start | bytes 442376 | tf_op jit(solution)/shard_map/ppermute | solution.py:95
  65.2 2.7 %collective-permute-start.19 = (f32[288,128]{1,0:T(8,128)S(1)}, f32[288,128]{1,0:T(8,128)S(1)}, u32[]{:S(2)}, u32[]{:S(2)}) collective-permute-start(f32[288,128]{1,0:T(8,128)S(1)} %get-tuple-element.37), channel_id=1, source_target_pairs={{0,16},{1,20},{2,18},{3,22},{4,24},{5,28},{6,26},{7,30},{8,17},{9,... | collective-permute-start | bytes 442376 | tf_op jit(solution)/shard_map/ppermute | solution.py:95
  67.9 1.5 %collective-permute-start.20 = (f32[288,128]{1,0:T(8,128)S(1)}, f32[288,128]{1,0:T(8,128)S(1)}, u32[]{:S(2)}, u32[]{:S(2)}) collective-permute-start(f32[288,128]{1,0:T(8,128)S(1)} %get-tuple-element.38), channel_id=1, source_target_pairs={{0,17},{1,21},{2,19},{3,23},{4,25},{5,29},{6,27},{7,31},{8,16},{9,... | collective-permute-start | bytes 442376 | tf_op jit(solution)/shard_map/ppermute | solution.py:95
  69.4 2.4 %collective-permute-start.21 = (f32[288,128]{1,0:T(8,128)S(1)}, f32[288,128]{1,0:T(8,128)S(1)}, u32[]{:S(2)}, u32[]{:S(2)}) collective-permute-start(f32[288,128]{1,0:T(8,128)S(1)} %get-tuple-element.39), channel_id=1, source_target_pairs={{0,18},{1,22},{2,16},{3,20},{4,26},{5,30},{6,24},{7,28},{8,19},{9,... | collective-permute-start | bytes 442376 | tf_op jit(solution)/shard_map/ppermute | solution.py:95
  71.9 3.0 %collective-permute-start.22 = (f32[288,128]{1,0:T(8,128)S(1)}, f32[288,128]{1,0:T(8,128)S(1)}, u32[]{:S(2)}, u32[]{:S(2)}) collective-permute-start(f32[288,128]{1,0:T(8,128)S(1)} %get-tuple-element.40), channel_id=1, source_target_pairs={{0,19},{1,23},{2,17},{3,21},{4,27},{5,31},{6,25},{7,29},{8,18},{9,... | collective-permute-start | bytes 442376 | tf_op jit(solution)/shard_map/ppermute | solution.py:95
  75.0 10.9 %collective-permute-done.19.refs_4_.refs_8_ = f32[288,128]{1,0:T(8,128)S(1)} collective-permute-done((f32[288,128]{1,0:T(8,128)S(1)}, f32[288,128]{1,0:T(8,128)S(1)}, u32[]{:S(2)}, u32[]{:S(2)}) %collective-permute-start.19) | collective-permute-done | bytes 147488 | tf_op jit(solution)/shard_map/ppermute | solution.py:95
  85.8 7.0 %collective-permute-done.21.refs_6_.refs_10_ = f32[288,128]{1,0:T(8,128)S(1)} collective-permute-done((f32[288,128]{1,0:T(8,128)S(1)}, f32[288,128]{1,0:T(8,128)S(1)}, u32[]{:S(2)}, u32[]{:S(2)}) %collective-permute-start.21) | collective-permute-done | bytes 147488 | tf_op jit(solution)/shard_map/ppermute | solution.py:95
  93.6 4.4 %collective-permute-start.24 = (f32[16,128]{1,0:T(8,128)S(1)}, f32[16,128]{1,0:T(8,128)S(1)}, u32[]{:S(2)}, u32[]{:S(2)}) collective-permute-start(f32[16,128]{1,0:T(8,128)S(1)} %gram.1), channel_id=1, source_target_pairs={{0,16},{1,17},{2,18},{3,19},{4,20},{5,21},{6,22},{7,23},{8,24},{9,... | collective-permute-start | bytes 24584 | tf_op jit(solution)/shard_map/ppermute | solution.py:95
  98.0 1.6 %collective-permute-start.25 = (f32[16,128]{1,0:T(8,128)S(1)}, f32[16,128]{1,0:T(8,128)S(1)}, u32[]{:S(2)}, u32[]{:S(2)}) collective-permute-start(f32[16,128]{1,0:T(8,128)S(1)} %gram.1), channel_id=1, source_target_pairs={{0,24},{1,25},{2,26},{3,27},{4,28},{5,29},{6,30},{7,31},{8,16},{9,... | collective-permute-start | bytes 24584 | tf_op jit(solution)/shard_map/ppermute | solution.py:95
  100.1 3.3 %collective-permute-done.25 = f32[16,128]{1,0:T(8,128)S(1)} collective-permute-done((f32[16,128]{1,0:T(8,128)S(1)}, f32[16,128]{1,0:T(8,128)S(1)}, u32[]{:S(2)}, u32[]{:S(2)}) %collective-permute-start.25) | collective-permute-done | bytes 8224 | tf_op jit(solution)/shard_map/ppermute | solution.py:95
  105.5 2.6 %collective-permute-start.29 = (f32[16,128]{1,0:T(8,128)S(1)}, f32[16,128]{1,0:T(8,128)S(1)}, u32[]{:S(2)}, u32[]{:S(2)}) collective-permute-start(f32[16,128]{1,0:T(8,128)S(1)} %add.36.refs_0_), channel_id=1, source_target_pairs={{0,3},{1,2},{2,1},{3,0},{4,7},{5,6},{6,5},{7,4},{8,11},{9,10},{10,... | collective-permute-start | bytes 24584 | tf_op jit(solution)/shard_map/ppermute | solution.py:95
  108.3 1.7 %collective-permute-done.29.refs_3_ = f32[16,128]{1,0:T(8,128)S(1)} collective-permute-done((f32[16,128]{1,0:T(8,128)S(1)}, f32[16,128]{1,0:T(8,128)S(1)}, u32[]{:S(2)}, u32[]{:S(2)}) %collective-permute-start.29) | collective-permute-done | bytes 8224 | tf_op jit(solution)/shard_map/ppermute | solution.py:95
  110.1 1.8 %place.1 = f32[64,1152]{1,0:T(8,128)} custom-call(s32[3]{0:T(128)S(1)} %pad_add_fusion.s_ref, f32[16,128]{1,0:T(8,128)S(1)} %add.36.refs_0_, f32[16,128]{1,0:T(8,128)S(1)} %collective-permute-done.27.refs_1_, f32[16,128]{1,0:T(8,128)S(1)} %collective-permute-done.28.refs_2_, f32[16,128]{1,0:T(8,128)S(1)} %collective-permute-done.29.refs_3_, ...), custom_call_target="tpu_custom_call" | custom-call | tf_op jit(solution)/shard_map/place/pallas_call | solution.py:486
  (51 shorter events, 12.5 us)
Async XLA Ops:
  2.5 26.6 %collective-permute-start.1 = (f32[392,256]{1,0:T(8,128)}, f32[392,256]{1,0:T(8,128)}, u32[]{:S(2)}, u32[]{:S(2)}) collective-permute-start(f32[392,256]{1,0:T(8,128)} %get-tuple-element.24), channel_id=1, source_target_pairs={{0,2},{1,3},{2,0},{3,1},{4,6},{5,7},{6,4},{7,5},{8,10},{9,11},{10,... | collective-permute-start | bytes 1204232 | tf_op jit(solution)/shard_map/ppermute | solution.py:95
  5.5 24.1 %collective-permute-start.2 = (f32[392,256]{1,0:T(8,128)}, f32[392,256]{1,0:T(8,128)}, u32[]{:S(2)}, u32[]{:S(2)}) collective-permute-start(f32[392,256]{1,0:T(8,128)} %get-tuple-element.24), channel_id=1, source_target_pairs={{0,3},{1,2},{2,1},{3,0},{4,7},{5,6},{6,5},{7,4},{8,11},{9,10},{10,... | collective-permute-start | bytes 1204232 | tf_op jit(solution)/shard_map/ppermute | solution.py:95
  7.0 19.2 %collective-permute-start = (f32[392,256]{1,0:T(8,128)}, f32[392,256]{1,0:T(8,128)}, u32[]{:S(2)}, u32[]{:S(2)}) collective-permute-start(f32[392,256]{1,0:T(8,128)} %get-tuple-element.23.refs_0_), channel_id=1, source_target_pairs={{0,1},{1,0},{2,3},{3,2},{4,5},{5,4},{6,7},{7,6},{8,9},{9,8},{10,11... | collective-permute-start | bytes 1204232 | tf_op jit(solution)/shard_map/ppermute | solution.py:95
  18.5 15.6 %collective-permute-start.7 = (f32[392,128]{1,0:T(8,128)}, f32[392,128]{1,0:T(8,128)S(1)}, u32[]{:S(2)}, u32[]{:S(2)}) collective-permute-start(f32[392,128]{1,0:T(8,128)} %get-tuple-element.30), channel_id=1, source_target_pairs={{0,1},{1,0},{2,3},{3,2},{4,5},{5,4},{6,7},{7,6},{8,9},{9,8},{10,11... | collective-permute-start | bytes 602120 | tf_op jit(solution)/shard_map/ppermute | solution.py:95
  20.4 15.2 %collective-permute-start.8 = (f32[392,128]{1,0:T(8,128)}, f32[392,128]{1,0:T(8,128)S(1)}, u32[]{:S(2)}, u32[]{:S(2)}) collective-permute-start(f32[392,128]{1,0:T(8,128)} %get-tuple-element.29.refs_2_), channel_id=1, source_target_pairs={{0,2},{1,3},{2,0},{3,1},{4,6},{5,7},{6,4},{7,5},{8,10},{9,11},{10,... | collective-permute-start | bytes 602120 | tf_op jit(solution)/shard_map/ppermute | solution.py:95
  26.1 9.9 %collective-permute-start.9 = (f32[392,128]{1,0:T(8,128)}, f32[392,128]{1,0:T(8,128)S(1)}, u32[]{:S(2)}, u32[]{:S(2)}) collective-permute-start(f32[392,128]{1,0:T(8,128)} %get-tuple-element.30), channel_id=1, source_target_pairs={{0,3},{1,2},{2,1},{3,0},{4,7},{5,6},{6,5},{7,4},{8,11},{9,10},{10,... | collective-permute-start | bytes 602120 | tf_op jit(solution)/shard_map/ppermute | solution.py:95
  29.1 12.1 %collective-permute-start.3 = (f32[392,128]{1,0:T(8,128)}, f32[392,128]{1,0:T(8,128)S(1)}, u32[]{:S(2)}, u32[]{:S(2)}) collective-permute-start(f32[392,128]{1,0:T(8,128)} %get-tuple-element.26), channel_id=1, source_target_pairs={{0,1},{1,0},{2,3},{3,2},{4,5},{5,4},{6,7},{7,6},{8,9},{9,8},{10,11... | collective-permute-start | bytes 602120 | tf_op jit(solution)/shard_map/ppermute | solution.py:95
  29.6 14.6 %collective-permute-start.5 = (f32[392,128]{1,0:T(8,128)}, f32[392,128]{1,0:T(8,128)S(1)}, u32[]{:S(2)}, u32[]{:S(2)}) collective-permute-start(f32[392,128]{1,0:T(8,128)} %get-tuple-element.26), channel_id=1, source_target_pairs={{0,3},{1,2},{2,1},{3,0},{4,7},{5,6},{6,5},{7,4},{8,11},{9,10},{10,... | collective-permute-start | bytes 602120 | tf_op jit(solution)/shard_map/ppermute | solution.py:95
  31.0 1.0 copy-start
  32.0 12.1 %copy-start.1 = (f32[392,128]{1,0:T(8,128)S(1)}, f32[392,128]{1,0:T(8,128)}, u32[]{:S(2)}) copy-start(f32[392,128]{1,0:T(8,128)} %get-tuple-element.25.refs_2_) | copy-start | bytes 602116
  34.1 10.1 %collective-permute-start.4 = (f32[392,128]{1,0:T(8,128)}, f32[392,128]{1,0:T(8,128)S(1)}, u32[]{:S(2)}, u32[]{:S(2)}) collective-permute-start(f32[392,128]{1,0:T(8,128)} %get-tuple-element.25.refs_2_), channel_id=1, source_target_pairs={{0,2},{1,3},{2,0},{3,1},{4,6},{5,7},{6,4},{7,5},{8,10},{9,11},{10,... | collective-permute-start | bytes 602120 | tf_op jit(solution)/shard_map/ppermute | solution.py:95
  41.1 7.3 %collective-permute-start.10 = (f32[4,288,128]{2,1,0:T(8,128)S(1)}, f32[4,288,128]{2,1,0:T(8,128)S(1)}, u32[]{:S(2)}, u32[]{:S(2)}) collective-permute-start(f32[4,288,128]{2,1,0:T(8,128)S(1)} %get-tuple-element.32), channel_id=1, source_target_pairs={{0,4},{1,5},{2,6},{3,7},{4,0},{5,1},{6,2},{7,3},{8,12},{9,13},{10,... | collective-permute-start | bytes 1769480 | tf_op jit(solution)/shard_map/ppermute | solution.py:95
  48.4 2.1 %collective-permute-start.6 = (f32[4,288,128]{2,1,0:T(8,128)S(1)}, f32[4,288,128]{2,1,0:T(8,128)S(1)}, u32[]{:S(2)}, u32[]{:S(2)}) collective-permute-start(f32[4,288,128]{2,1,0:T(8,128)S(1)} %get-tuple-element.28), channel_id=1, source_target_pairs={{0,4},{1,5},{2,6},{3,7},{4,0},{5,1},{6,2},{7,3},{8,12},{9,13},{10,... | collective-permute-start | bytes 1769480 | tf_op jit(solution)/shard_map/ppermute | solution.py:95
  50.6 1.2 %collective-permute-start.11 = (f32[8,128]{1,0:T(8,128)S(1)}, f32[8,128]{1,0:T(8,128)S(1)}, u32[]{:S(2)}, u32[]{:S(2)}) collective-permute-start(f32[8,128]{1,0:T(8,128)S(1)} %shard_map.40), channel_id=1, source_target_pairs={{0,4},{1,5},{2,6},{3,7},{4,0},{5,1},{6,2},{7,3},{8,12},{9,13},{10,... | collective-permute-start | bytes 12296 | tf_op jit(solution)/shard_map/ppermute | solution.py:95
  51.9 3.6 %collective-permute-start.12 = (f32[8,128]{1,0:T(8,128)S(1)}, f32[8,128]{1,0:T(8,128)S(1)}, u32[]{:S(2)}, u32[]{:S(2)}) collective-permute-start(f32[8,128]{1,0:T(8,128)S(1)} %add.32.t0), channel_id=1, source_target_pairs={{0,1},{1,0},{2,3},{3,2},{4,5},{5,4},{6,7},{7,6},{8,9},{9,8},{10,11... | collective-permute-start | bytes 12296 | tf_op jit(solution)/shard_map/ppermute | solution.py:95
  52.4 3.6 %collective-permute-start.13 = (f32[8,128]{1,0:T(8,128)S(1)}, f32[8,128]{1,0:T(8,128)S(1)}, u32[]{:S(2)}, u32[]{:S(2)}) collective-permute-start(f32[8,128]{1,0:T(8,128)S(1)} %add.32.t0), channel_id=1, source_target_pairs={{0,2},{1,3},{2,0},{3,1},{4,6},{5,7},{6,4},{7,5},{8,10},{9,11},{10,... | collective-permute-start | bytes 12296 | tf_op jit(solution)/shard_map/ppermute | solution.py:95
  53.6 4.5 %collective-permute-start.14 = (f32[8,128]{1,0:T(8,128)S(1)}, f32[8,128]{1,0:T(8,128)S(1)}, u32[]{:S(2)}, u32[]{:S(2)}) collective-permute-start(f32[8,128]{1,0:T(8,128)S(1)} %add.32.t0), channel_id=1, source_target_pairs={{0,3},{1,2},{2,1},{3,0},{4,7},{5,6},{6,5},{7,4},{8,11},{9,10},{10,... | collective-permute-start | bytes 12296 | tf_op jit(solution)/shard_map/ppermute | solution.py:95
  58.4 9.5 %collective-permute-start.15 = (f32[288,128]{1,0:T(8,128)S(1)}, f32[288,128]{1,0:T(8,128)S(1)}, u32[]{:S(2)}, u32[]{:S(2)}) collective-permute-start(f32[288,128]{1,0:T(8,128)S(1)} %get-tuple-element.33), channel_id=1, source_target_pairs={{0,0},{1,4},{2,2},{3,6},{4,8},{5,12},{6,10},{7,14},{8,1},{9,5},{10... | collective-permute-start | bytes 442376 | tf_op jit(solution)/shard_map/ppermute | solution.py:95
  59.0 10.4 %collective-permute-start.16 = (f32[288,128]{1,0:T(8,128)S(1)}, f32[288,128]{1,0:T(8,128)S(1)}, u32[]{:S(2)}, u32[]{:S(2)}) collective-permute-start(f32[288,128]{1,0:T(8,128)S(1)} %get-tuple-element.34), channel_id=1, source_target_pairs={{0,1},{1,5},{2,3},{3,7},{4,9},{5,13},{6,11},{7,15},{8,0},{9,4},{10... | collective-permute-start | bytes 442376 | tf_op jit(solution)/shard_map/ppermute | solution.py:95
  61.2 10.6 %collective-permute-start.17 = (f32[288,128]{1,0:T(8,128)S(1)}, f32[288,128]{1,0:T(8,128)S(1)}, u32[]{:S(2)}, u32[]{:S(2)}) collective-permute-start(f32[288,128]{1,0:T(8,128)S(1)} %get-tuple-element.35), channel_id=1, source_target_pairs={{0,2},{1,6},{2,0},{3,4},{4,10},{5,14},{6,8},{7,12},{8,3},{9,7},{10... | collective-permute-start | bytes 442376 | tf_op jit(solution)/shard_map/ppermute | solution.py:95
  62.6 12.3 %collective-permute-start.18 = (f32[288,128]{1,0:T(8,128)S(1)}, f32[288,128]{1,0:T(8,128)S(1)}, u32[]{:S(2)}, u32[]{:S(2)}) collective-permute-start(f32[288,128]{1,0:T(8,128)S(1)} %get-tuple-element.36), channel_id=1, source_target_pairs={{0,3},{1,7},{2,1},{3,5},{4,11},{5,15},{6,9},{7,13},{8,2},{9,6},{10... | collective-permute-start | bytes 442376 | tf_op jit(solution)/shard_map/ppermute | solution.py:95
  65.2 20.6 %collective-permute-start.19 = (f32[288,128]{1,0:T(8,128)S(1)}, f32[288,128]{1,0:T(8,128)S(1)}, u32[]{:S(2)}, u32[]{:S(2)}) collective-permute-start(f32[288,128]{1,0:T(8,128)S(1)} %get-tuple-element.37), channel_id=1, source_target_pairs={{0,16},{1,20},{2,18},{3,22},{4,24},{5,28},{6,26},{7,30},{8,17},{9,... | collective-permute-start | bytes 442376 | tf_op jit(solution)/shard_map/ppermute | solution.py:95
  67.9 18.0 %collective-permute-start.20 = (f32[288,128]{1,0:T(8,128)S(1)}, f32[288,128]{1,0:T(8,128)S(1)}, u32[]{:S(2)}, u32[]{:S(2)}) collective-permute-start(f32[288,128]{1,0:T(8,128)S(1)} %get-tuple-element.38), channel_id=1, source_target_pairs={{0,17},{1,21},{2,19},{3,23},{4,25},{5,29},{6,27},{7,31},{8,16},{9,... | collective-permute-start | bytes 442376 | tf_op jit(solution)/shard_map/ppermute | solution.py:95
  69.4 23.4 %collective-permute-start.21 = (f32[288,128]{1,0:T(8,128)S(1)}, f32[288,128]{1,0:T(8,128)S(1)}, u32[]{:S(2)}, u32[]{:S(2)}) collective-permute-start(f32[288,128]{1,0:T(8,128)S(1)} %get-tuple-element.39), channel_id=1, source_target_pairs={{0,18},{1,22},{2,16},{3,20},{4,26},{5,30},{6,24},{7,28},{8,19},{9,... | collective-permute-start | bytes 442376 | tf_op jit(solution)/shard_map/ppermute | solution.py:95
  71.9 20.9 %collective-permute-start.22 = (f32[288,128]{1,0:T(8,128)S(1)}, f32[288,128]{1,0:T(8,128)S(1)}, u32[]{:S(2)}, u32[]{:S(2)}) collective-permute-start(f32[288,128]{1,0:T(8,128)S(1)} %get-tuple-element.40), channel_id=1, source_target_pairs={{0,19},{1,23},{2,17},{3,21},{4,27},{5,31},{6,25},{7,29},{8,18},{9,... | collective-permute-start | bytes 442376 | tf_op jit(solution)/shard_map/ppermute | solution.py:95
  93.6 6.5 %collective-permute-start.24 = (f32[16,128]{1,0:T(8,128)S(1)}, f32[16,128]{1,0:T(8,128)S(1)}, u32[]{:S(2)}, u32[]{:S(2)}) collective-permute-start(f32[16,128]{1,0:T(8,128)S(1)} %gram.1), channel_id=1, source_target_pairs={{0,16},{1,17},{2,18},{3,19},{4,20},{5,21},{6,22},{7,23},{8,24},{9,... | collective-permute-start | bytes 24584 | tf_op jit(solution)/shard_map/ppermute | solution.py:95
  98.0 5.4 %collective-permute-start.25 = (f32[16,128]{1,0:T(8,128)S(1)}, f32[16,128]{1,0:T(8,128)S(1)}, u32[]{:S(2)}, u32[]{:S(2)}) collective-permute-start(f32[16,128]{1,0:T(8,128)S(1)} %gram.1), channel_id=1, source_target_pairs={{0,24},{1,25},{2,26},{3,27},{4,28},{5,29},{6,30},{7,31},{8,16},{9,... | collective-permute-start | bytes 24584 | tf_op jit(solution)/shard_map/ppermute | solution.py:95
  99.6 3.8 %collective-permute-start.23 = (f32[16,128]{1,0:T(8,128)S(1)}, f32[16,128]{1,0:T(8,128)S(1)}, u32[]{:S(2)}, u32[]{:S(2)}) collective-permute-start(f32[16,128]{1,0:T(8,128)S(1)} %gram.1), channel_id=1, source_target_pairs={{0,8},{1,9},{2,10},{3,11},{4,12},{5,13},{6,14},{7,15},{8,0},{9,1},... | collective-permute-start | bytes 24584 | tf_op jit(solution)/shard_map/ppermute | solution.py:95
  103.4 1.2 %collective-permute-start.26 = (f32[16,128]{1,0:T(8,128)S(1)}, f32[16,128]{1,0:T(8,128)S(1)}, u32[]{:S(2)}, u32[]{:S(2)}) collective-permute-start(f32[16,128]{1,0:T(8,128)S(1)} %add_add_fusion), channel_id=1, source_target_pairs={{0,4},{1,5},{2,6},{3,7},{4,0},{5,1},{6,2},{7,3},{8,12},{9,13},{10,... | collective-permute-start | bytes 24584 | tf_op jit(solution)/shard_map/ppermute | solution.py:95
  104.7 3.7 %collective-permute-start.27 = (f32[16,128]{1,0:T(8,128)S(1)}, f32[16,128]{1,0:T(8,128)S(1)}, u32[]{:S(2)}, u32[]{:S(2)}) collective-permute-start(f32[16,128]{1,0:T(8,128)S(1)} %add.36.refs_0_), channel_id=1, source_target_pairs={{0,1},{1,0},{2,3},{3,2},{4,5},{5,4},{6,7},{7,6},{8,9},{9,8},{10,11... | collective-permute-start | bytes 24584 | tf_op jit(solution)/shard_map/ppermute | solution.py:95
  104.7 3.7 %collective-permute-start.28 = (f32[16,128]{1,0:T(8,128)S(1)}, f32[16,128]{1,0:T(8,128)S(1)}, u32[]{:S(2)}, u32[]{:S(2)}) collective-permute-start(f32[16,128]{1,0:T(8,128)S(1)} %add.36.refs_0_), channel_id=1, source_target_pairs={{0,2},{1,3},{2,0},{3,1},{4,6},{5,7},{6,4},{7,5},{8,10},{9,11},{10,... | collective-permute-start | bytes 24584 | tf_op jit(solution)/shard_map/ppermute | solution.py:95
  105.5 4.5 %collective-permute-start.29 = (f32[16,128]{1,0:T(8,128)S(1)}, f32[16,128]{1,0:T(8,128)S(1)}, u32[]{:S(2)}, u32[]{:S(2)}) collective-permute-start(f32[16,128]{1,0:T(8,128)S(1)} %add.36.refs_0_), channel_id=1, source_target_pairs={{0,3},{1,2},{2,1},{3,0},{4,7},{5,6},{6,5},{7,4},{8,11},{9,10},{10,... | collective-permute-start | bytes 24584 | tf_op jit(solution)/shard_map/ppermute | solution.py:95
  (1 other events, 0.9 us)

commit v4 on v3

--- a/solution.py
+++ b/solution.py
@@ -204,7 +204,8 @@
 
 
 def gradient_kernel(scale, side, s_ref, xt_ref, *refs):
-    sources, (keep_ref, send_ref, rh, rl, g_ref) = refs[:4], refs[4:]
+    sources, outs, (rh, rl, g_ref) = refs[:4], refs[4:-3], refs[-3:]
+    keep_ref, send_ref = outs[:2]
     xt = xt_ref
     width = sources[0].shape[1]
     span = xt.shape[2] // 2
@@ -240,6 +241,8 @@
             first, second = pair_pack(g_ref[2 * per * quarter + m], g_ref[2 * per * quarter + per + m])
             keep_ref[slot, m * BLK : (m + 1) * BLK, :] = jnp.where(odd, second, first)
             send_ref[slot, m * BLK : (m + 1) * BLK, :] = jnp.where(odd, first, second)
+    for early, ref in zip(outs[2:], outs[:2]):
+        early[...] = ref[ref.shape[0] - 1]
 
 
 def column_sums(a, b):
@@ -280,19 +283,25 @@
     return (refs[0][...] + refs[1][...]) + (refs[2][...] + refs[3][...])
 
 
-def pair_mix_kernel(s_ref, t0, t1, t2, t3, keep_ref, received_ref, *out_refs):
+def pair_mix_kernel(pieces, s_ref, t0, t1, t2, t3, keep_ref, received_ref, *out_refs):
     core = s_ref[0]
     totals = jnp.sum(sum_four((t0, t1, t2, t3)), axis=1, keepdims=True)
     left, right = pair_coefs(totals[0:1], totals[1:2], totals[2:3])
     keep_coef = jnp.where(core == 0, left, right)
     received_coef = jnp.where(core == 0, right, left)
-    for d, out in enumerate(out_refs):
+    for d, out in enumerate(out_refs[:pieces]):
         out[...] = keep_coef * keep_ref[d] + received_coef * received_ref[d]
+    for out in out_refs[pieces:]:
+        out[...] = jnp.zeros(out.shape, jnp.float32)
+        out[0:1] = jnp.broadcast_to(keep_coef, (1, out.shape[1]))
+        out[1:2] = jnp.broadcast_to(received_coef, (1, out.shape[1]))
 
 
 def gram_kernel(s_ref, *refs):
     upper, x = s_ref[0], s_ref[1]
-    blocks, gram_ref = refs[:8], refs[8]
+    coefs, own, other, gram_ref, late_ref = refs[7:]
+    late_ref[...] = coefs[0:1] * own[...] + coefs[1:2] * other[...]
+    blocks = refs[:7] + (late_ref,)
     node = [2 * jnp.bitwise_xor(upper, d // 2) + jnp.bitwise_xor(x, d % 2) for d in range(4)]
     for e in range(4):
         for d in range(e + 1):
@@ -422,12 +431,12 @@
     half = count // 2
     place = scalars(z // 2, x, y)
 
-    def gradient(pieces):
+    def gradient(pieces, early):
         return pl.pallas_call(
             lambda *refs: gradient_kernel(1.0 / rows, side, *refs),
-            out_shape=(f32(half, part, 128), f32(half, part, 128)),
+            out_shape=(f32(half, part, 128),) * 2 + (f32(part, 128),) * early,
             in_specs=[SM] + [VM] * 5,
-            out_specs=(VM, VM),
+            out_specs=(VM,) * (2 + early),
             scratch_shapes=[
                 pltpu.VMEM((side, side + 3, 4 * imgs, 128), jnp.bfloat16),
                 pltpu.VMEM((side, side + 3, 4 * imgs, 128), jnp.bfloat16),
@@ -449,38 +458,37 @@
         )(scalars(c), keep, received, *before)
 
     across = lambda z, c, y, x: (z, 1 - c, y, x)
-    keep_far, send_far = gradient(far)
+    keep_far, send_far, early_keep, early_send = gradient(far, 2)
     received_far = hop(send_far, across)
-    keep_near, send_near = gradient(near)
+    last = half - 1
+    early_own = hop(early_keep, mover(count - 1))
+    early_other = hop(early_send, lambda z, c, y, x: mover(count - 1)(z, 1 - c, y, x))
+    keep_near, send_near = gradient(near, 0)
     received_near = hop(send_near, across)
     totals = dots(keep_far, received_far, ())
     totals = plane_sum(dots(keep_near, received_near, (totals,)))
 
-    def mix(keep, received):
+    def mix(keep, received, pieces):
         return pl.pallas_call(
-            pair_mix_kernel,
-            out_shape=(f32(part, 128),) * half,
+            lambda *refs: pair_mix_kernel(pieces, *refs),
+            out_shape=(f32(part, 128),) * pieces + (f32(8, 128),) * (half - pieces),
             in_specs=[SM] + [VM] * 6,
             out_specs=(VM,) * half,
             compiler_params=pltpu.CompilerParams(vmem_limit_bytes=SHARED),
         )(scalars(c), *totals, keep, received)
 
-    mixed_far = mix(keep_far, received_far)
-    blocks = tuple(mix(keep_near, received_near)) + tuple(mixed_far)
-
-    moved = []
-    for index in range(count):
-        e, dy, dx = index // 4, index // 2 % 2, index % 2
-        mapping = lambda z, c, y, x, e=e, dy=dy, dx=dx: (2 * (z // 2 ^ e) + c, x, y ^ dy, z % 2 ^ dx)
-        moved.append(hop(blocks[index], mapping))
-    gram = pl.pallas_call(
+    mixed_far = mix(keep_far, received_far, last)
+    blocks = tuple(mix(keep_near, received_near, half)) + tuple(mixed_far)
+
+    moved = [hop(blocks[index], mover(index)) for index in range(count)]
+    gram, moved[-1] = pl.pallas_call(
         gram_kernel,
-        out_shape=f32(16, 128),
-        in_specs=[SM] + [VM] * count,
-        out_specs=VM,
+        out_shape=(f32(16, 128), f32(part, 128)),
+        in_specs=[SM] + [VM] * (count + 2),
+        out_specs=(VM, VM),
         compiler_params=pltpu.CompilerParams(vmem_limit_bytes=SHARED),
         name="gram",
-    )(place, *moved)
+    )(place, *moved, early_own, early_other)
     along = [hop(gram, lambda z, c, y, x, d=d: (z ^ d, c, y, x)) for d in range(1, z_count)]
     gram = plane_sum((gram + along[0]) + (along[1] + along[2]))
     out = pl.pallas_call(
@@ -493,6 +501,11 @@
         name="place",
     )(place, *gram, *moved)
     return out.T
+
+
+def mover(index):
+    e, dy, dx = index // 4, index // 2 % 2, index % 2
+    return lambda z, c, y, x: (2 * (z // 2 ^ e) + c, x, y ^ dy, z % 2 ^ dx)
 
 
 def exchange(own, other):

time: 112 us -> 114 us (1.018)
  starting transfers between devices: 44.7 us -> 48.8 us
  waiting for transfers between devices: 37.4 us -> 35.5 us
    ppermute x30 -> x32, starting transfers between devices: 44.7 us -> 48.8 us  [hop(): return lax.ppermute(value, ('node', 'local'), pairs)]
    ppermute x30 -> x32, waiting for transfers between devices: 37.4 us -> 35.5 us  [hop(): return lax.ppermute(value, ('node', 'local'), pairs)]
  transfers between devices with their start and end apart: 30 -> 32, of which waited for: 14 -> 14; matrix products, arithmetic and copies ran while one was open for 1% -> 1% of each run, Pallas kernels for 19% -> 19%
where the time goes in v4:
time: 114 us
  starting transfers between devices  48.8 us (43%)
  waiting for transfers between devices  35.5 us (31%)
  Pallas kernels  26.8 us (24%)
  local copies, waits for them, and re-layouts  1.93 us (2%)
    ppermute x32, starting transfers between devices, hop(): return lax.ppermute(value, ('node', 'local'), pairs)  48.8 us
    ppermute x32, waiting for transfers between devices, hop(): return lax.ppermute(value, ('node', 'local'), pairs)  35.5 us
    pallas_call x1, Pallas kernels, tiles(): pl.pallas_call(residual_kernel, out_shape=(f32(rows, 128),) * 4, in_specs...  10.8 us
    pallas_call x2, Pallas kernels, gradient(): pl.pallas_call(lambda *refs: gradient_kernel(1.0 / rows, side, *refs), ou...  8.19 us
    pallas_call x1, Pallas kernels, tiles(): pl.pallas_call(split_kernel, out_shape=(f32(rows, width), f32(rows, width...  2.42 us
  transfers between devices with their start and end apart: 32, of which 14 were waited for; matrix products, arithmetic and copies ran while one was open for 1% of the time, Pallas kernels for 19%

profile of v4, /device:TPU:0, one launch (start us, length us, event | category | flops | bytes accessed | tf_op | source)
XLA Modules:
  0.0 114.1 jit_solution(8847454386765115211)
XLA Ops:
  0.0 2.4 %split_images.1 = (f32[392,256]{1,0:T(8,128)}, f32[392,256]{1,0:T(8,128)}) custom-call(s32[1]{0:T(128)} %bitcast.2.s_ref, f32[392,512]{1,0:T(8,128)} %bitcast.13), custom_call_target="tpu_custom_call" | custom-call | tf_op jit(solution)/shard_map/split_images/pallas_call | solution.py:373
  2.4 3.1 %collective-permute-start.1 = (f32[392,256]{1,0:T(8,128)}, f32[392,256]{1,0:T(8,128)}, u32[]{:S(2)}, u32[]{:S(2)}) collective-permute-start(f32[392,256]{1,0:T(8,128)} %get-tuple-element.28), channel_id=1, source_target_pairs={{0,2},{1,3},{2,0},{3,1},{4,6},{5,7},{6,4},{7,5},{8,10},{9,11},{10,... | collective-permute-start | bytes 1204232 | tf_op jit(solution)/shard_map/ppermute | solution.py:95
  5.5 1.4 %collective-permute-start.2 = (f32[392,256]{1,0:T(8,128)}, f32[392,256]{1,0:T(8,128)}, u32[]{:S(2)}, u32[]{:S(2)}) collective-permute-start(f32[392,256]{1,0:T(8,128)} %get-tuple-element.28), channel_id=1, source_target_pairs={{0,3},{1,2},{2,1},{3,0},{4,7},{5,6},{6,5},{7,4},{8,11},{9,10},{10,... | collective-permute-start | bytes 1204232 | tf_op jit(solution)/shard_map/ppermute | solution.py:95
  7.7 10.8 %residual.1 = (f32[392,128]{1,0:T(8,128)}, f32[392,128]{1,0:T(8,128)}, f32[392,128]{1,0:T(8,128)}, f32[392,128]{1,0:T(8,128)}) custom-call(s32[2]{0:T(128)} %pad_add_fusion.2.s_ref, f32[392,512]{1,0:T(8,128)} %bitcast.14, f32[392,512]{1,0:T(8,128)} %bitcast.16, f32[9,512,512]{2,1,0:T(8,128)} %bitcast.15), custom_call_target="tpu_custom_call" | custom-call | flops 5549064192 | bytes 9437184 | tf_op jit(solution)/shard_map/residual/pallas_call | solution.py:393
  18.5 2.0 %collective-permute-start.7 = (f32[392,128]{1,0:T(8,128)}, f32[392,128]{1,0:T(8,128)S(1)}, u32[]{:S(2)}, u32[]{:S(2)}) collective-permute-start(f32[392,128]{1,0:T(8,128)} %get-tuple-element.34), channel_id=1, source_target_pairs={{0,1},{1,0},{2,3},{3,2},{4,5},{5,4},{6,7},{7,6},{8,9},{9,8},{10,11... | collective-permute-start | bytes 602120 | tf_op jit(solution)/shard_map/ppermute | solution.py:95
  20.5 1.5 %collective-permute-start.8 = (f32[392,128]{1,0:T(8,128)}, f32[392,128]{1,0:T(8,128)S(1)}, u32[]{:S(2)}, u32[]{:S(2)}) collective-permute-start(f32[392,128]{1,0:T(8,128)} %get-tuple-element.33.refs_2_), channel_id=1, source_target_pairs={{0,2},{1,3},{2,0},{3,1},{4,6},{5,7},{6,4},{7,5},{8,10},{9,11},{10,... | collective-permute-start | bytes 602120 | tf_op jit(solution)/shard_map/ppermute | solution.py:95
  22.0 4.1 %collective-permute-done.refs_1_ = f32[392,256]{1,0:T(8,128)} collective-permute-done((f32[392,256]{1,0:T(8,128)}, f32[392,256]{1,0:T(8,128)}, u32[]{:S(2)}, u32[]{:S(2)}) %collective-permute-start) | collective-permute-done | bytes 401440 | tf_op jit(solution)/shard_map/ppermute | solution.py:95
  26.1 2.9 %collective-permute-start.9 = (f32[392,128]{1,0:T(8,128)}, f32[392,128]{1,0:T(8,128)S(1)}, u32[]{:S(2)}, u32[]{:S(2)}) collective-permute-start(f32[392,128]{1,0:T(8,128)} %get-tuple-element.34), channel_id=1, source_target_pairs={{0,3},{1,2},{2,1},{3,0},{4,7},{5,6},{6,5},{7,4},{8,11},{9,10},{10,... | collective-permute-start | bytes 602120 | tf_op jit(solution)/shard_map/ppermute | solution.py:95
  29.6 1.4 %collective-permute-start.5 = (f32[392,128]{1,0:T(8,128)}, f32[392,128]{1,0:T(8,128)S(1)}, u32[]{:S(2)}, u32[]{:S(2)}) collective-permute-start(f32[392,128]{1,0:T(8,128)} %get-tuple-element.30), channel_id=1, source_target_pairs={{0,3},{1,2},{2,1},{3,0},{4,7},{5,6},{6,5},{7,4},{8,11},{9,10},{10,... | collective-permute-start | bytes 602120 | tf_op jit(solution)/shard_map/ppermute | solution.py:95
  32.0 2.0 %prepare.1.refs_1_ = bf16[7,256,512]{2,1,0:T(8,128)(2,1)S(1)} custom-call(f32[392,256]{1,0:T(8,128)S(1)} %copy-done, f32[392,256]{1,0:T(8,128)} %collective-permute-done.refs_1_, f32[392,256]{1,0:T(8,128)} %collective-permute-done.1.refs_2_, f32[392,256]{1,0:T(8,128)} %collective-permute-done.2.refs_3_), custom_call_target="tpu_custom_call" | custom-call | tf_op jit(solution)/shard_map/prepare/pallas_call | solution.py:418
  34.1 1.6 %collective-permute-start.4 = (f32[392,128]{1,0:T(8,128)}, f32[392,128]{1,0:T(8,128)S(1)}, u32[]{:S(2)}, u32[]{:S(2)}) collective-permute-start(f32[392,128]{1,0:T(8,128)} %get-tuple-element.29.refs_2_), channel_id=1, source_target_pairs={{0,2},{1,3},{2,0},{3,1},{4,6},{5,7},{6,4},{7,5},{8,10},{9,11},{10,... | collective-permute-start | bytes 602120 | tf_op jit(solution)/shard_map/ppermute | solution.py:95
  36.9 4.1 %shard_map.38 = (f32[4,288,128]{2,1,0:T(8,128)S(1)}, f32[4,288,128]{2,1,0:T(8,128)S(1)}, f32[288,128]{1,0:T(8,128)S(1)}, f32[288,128]{1,0:T(8,128)S(1)}) custom-call(s32[3]{0:T(128)S(1)} %pad_add_fusion.1.refs_0_, bf16[7,256,512]{2,1,0:T(8,128)(2,1)S(1)} %prepare.1.refs_1_, f32[392,128]{1,0:T(8,128)S(1)} %copy-done.2, ...), custom_call_target="tpu_custom_call" | custom-call | flops 2774532096 | bytes 1179648 | tf_op jit(solution)/shard_map/pallas_call | solution.py:435
  41.1 3.1 %collective-permute-done.4.refs_4_ = f32[392,128]{1,0:T(8,128)S(1)} collective-permute-done((f32[392,128]{1,0:T(8,128)}, f32[392,128]{1,0:T(8,128)S(1)}, u32[]{:S(2)}, u32[]{:S(2)}) %collective-permute-start.4) | collective-permute-done | bytes 200736 | tf_op jit(solution)/shard_map/ppermute | solution.py:95
  44.2 4.1 %shard_map.37 = (f32[4,288,128]{2,1,0:T(8,128)S(1)}, f32[4,288,128]{2,1,0:T(8,128)S(1)}) custom-call(s32[3]{0:T(128)S(1)} %pad_add_fusion.1.refs_0_, bf16[7,256,512]{2,1,0:T(8,128)(2,1)S(1)} %prepare.1.refs_1_, f32[392,128]{1,0:T(8,128)S(1)} %copy-done.1, f32[392,128]{1,0:T(8,128)S(1)} %collective-permute-done.3.refs_3_, ...), custom_call_target="tpu_custom_call" | custom-call | flops 2774532096 | bytes 1179648 | tf_op jit(solution)/shard_map/pallas_call | solution.py:435
  48.5 1.8 %collective-permute-done.6.received_ref.refs_6_ = f32[4,288,128]{2,1,0:T(8,128)S(1)} collective-permute-done((f32[4,288,128]{2,1,0:T(8,128)S(1)}, f32[4,288,128]{2,1,0:T(8,128)S(1)}, u32[]{:S(2)}, u32[]{:S(2)}) %collective-permute-start.6) | collective-permute-done | bytes 589856 | tf_op jit(solution)/shard_map/ppermute | solution.py:95
  52.3 1.2 %collective-permute-start.13 = (f32[8,128]{1,0:T(8,128)S(1)}, f32[8,128]{1,0:T(8,128)S(1)}, u32[]{:S(2)}, u32[]{:S(2)}) collective-permute-start(f32[8,128]{1,0:T(8,128)S(1)} %add.32.refs_1_), channel_id=1, source_target_pairs={{0,2},{1,3},{2,0},{3,1},{4,6},{5,7},{6,4},{7,5},{8,10},{9,11},{10,... | collective-permute-start | bytes 12296 | tf_op jit(solution)/shard_map/ppermute | solution.py:95
  53.5 1.7 %collective-permute-start.14 = (f32[8,128]{1,0:T(8,128)S(1)}, f32[8,128]{1,0:T(8,128)S(1)}, u32[]{:S(2)}, u32[]{:S(2)}) collective-permute-start(f32[8,128]{1,0:T(8,128)S(1)} %add.32.refs_1_), channel_id=1, source_target_pairs={{0,3},{1,2},{2,1},{3,0},{4,7},{5,6},{6,5},{7,4},{8,11},{9,10},{10,... | collective-permute-start | bytes 12296 | tf_op jit(solution)/shard_map/ppermute | solution.py:95
  55.2 3.2 %collective-permute-start.23 = (f32[288,128]{1,0:T(8,128)S(1)}, f32[288,128]{1,0:T(8,128)S(1)}, u32[]{:S(2)}, u32[]{:S(2)}) collective-permute-start(f32[288,128]{1,0:T(8,128)S(1)} %get-tuple-element.45), channel_id=1, source_target_pairs={{0,19},{1,23},{2,17},{3,21},{4,27},{5,31},{6,25},{7,29},{8,18},{9,... | collective-permute-start | bytes 442376 | tf_op jit(solution)/shard_map/ppermute | solution.py:95
  58.5 1.3 %collective-permute-start.24 = (f32[288,128]{1,0:T(8,128)S(1)}, f32[288,128]{1,0:T(8,128)S(1)}, u32[]{:S(2)}, u32[]{:S(2)}) collective-permute-start(f32[288,128]{1,0:T(8,128)S(1)} %get-tuple-element.46), channel_id=1, source_target_pairs={{0,27},{1,31},{2,25},{3,29},{4,19},{5,23},{6,17},{7,21},{8,26},{9,... | collective-permute-start | bytes 442376 | tf_op jit(solution)/shard_map/ppermute | solution.py:95
  60.7 2.7 %collective-permute-start.16 = (f32[288,128]{1,0:T(8,128)S(1)}, f32[288,128]{1,0:T(8,128)S(1)}, u32[]{:S(2)}, u32[]{:S(2)}) collective-permute-start(f32[288,128]{1,0:T(8,128)S(1)} %get-tuple-element.38), channel_id=1, source_target_pairs={{0,1},{1,5},{2,3},{3,7},{4,9},{5,13},{6,11},{7,15},{8,0},{9,4},{10... | collective-permute-start | bytes 442376 | tf_op jit(solution)/shard_map/ppermute | solution.py:95
  63.7 3.3 %collective-permute-start.22 = (f32[8,128]{1,0:T(8,128)S(1)}, f32[8,128]{1,0:T(8,128)S(1)}, u32[]{:S(2)}, u32[]{:S(2)}) collective-permute-start(f32[8,128]{1,0:T(8,128)S(1)} %get-tuple-element.44), channel_id=1, source_target_pairs={{0,19},{1,23},{2,17},{3,21},{4,27},{5,31},{6,25},{7,29},{8,18},{9,... | collective-permute-start | bytes 12296 | tf_op jit(solution)/shard_map/ppermute | solution.py:95
  68.0 6.6 %collective-permute-start.18 = (f32[288,128]{1,0:T(8,128)S(1)}, f32[288,128]{1,0:T(8,128)S(1)}, u32[]{:S(2)}, u32[]{:S(2)}) collective-permute-start(f32[288,128]{1,0:T(8,128)S(1)} %get-tuple-element.40), channel_id=1, source_target_pairs={{0,3},{1,7},{2,1},{3,5},{4,11},{5,15},{6,9},{7,13},{8,2},{9,6},{10... | collective-permute-start | bytes 442376 | tf_op jit(solution)/shard_map/ppermute | solution.py:95
  74.5 1.1 collective-permute-start.19
  75.6 3.0 %collective-permute-start.20 = (f32[288,128]{1,0:T(8,128)S(1)}, f32[288,128]{1,0:T(8,128)S(1)}, u32[]{:S(2)}, u32[]{:S(2)}) collective-permute-start(f32[288,128]{1,0:T(8,128)S(1)} %get-tuple-element.42), channel_id=1, source_target_pairs={{0,17},{1,21},{2,19},{3,23},{4,25},{5,29},{6,27},{7,31},{8,16},{9,... | collective-permute-start | bytes 442376 | tf_op jit(solution)/shard_map/ppermute | solution.py:95
  79.7 11.0 %collective-permute-done.19.refs_4_.refs_8_ = f32[288,128]{1,0:T(8,128)S(1)} collective-permute-done((f32[288,128]{1,0:T(8,128)S(1)}, f32[288,128]{1,0:T(8,128)S(1)}, u32[]{:S(2)}, u32[]{:S(2)}) %collective-permute-start.19) | collective-permute-done | bytes 147488 | tf_op jit(solution)/shard_map/ppermute | solution.py:95
  90.7 6.2 %collective-permute-done.21.refs_6_.refs_10_ = f32[288,128]{1,0:T(8,128)S(1)} collective-permute-done((f32[288,128]{1,0:T(8,128)S(1)}, f32[288,128]{1,0:T(8,128)S(1)}, u32[]{:S(2)}, u32[]{:S(2)}) %collective-permute-start.21) | collective-permute-done | bytes 147488 | tf_op jit(solution)/shard_map/ppermute | solution.py:95
  98.4 2.8 %collective-permute-start.25 = (f32[16,128]{1,0:T(8,128)S(1)}, f32[16,128]{1,0:T(8,128)S(1)}, u32[]{:S(2)}, u32[]{:S(2)}) collective-permute-start(f32[16,128]{1,0:T(8,128)S(1)} %get-tuple-element.47), channel_id=1, source_target_pairs={{0,8},{1,9},{2,10},{3,11},{4,12},{5,13},{6,14},{7,15},{8,0},{9,1},... | collective-permute-start | bytes 24584 | tf_op jit(solution)/shard_map/ppermute | solution.py:95
  103.5 1.2 %collective-permute-done.28 = f32[16,128]{1,0:T(8,128)S(1)} collective-permute-done((f32[16,128]{1,0:T(8,128)S(1)}, f32[16,128]{1,0:T(8,128)S(1)}, u32[]{:S(2)}, u32[]{:S(2)}) %collective-permute-start.28) | collective-permute-done | bytes 8224 | tf_op jit(solution)/shard_map/ppermute | solution.py:95
  104.6 2.2 %collective-permute-start.29 = (f32[16,128]{1,0:T(8,128)S(1)}, f32[16,128]{1,0:T(8,128)S(1)}, u32[]{:S(2)}, u32[]{:S(2)}) collective-permute-start(f32[16,128]{1,0:T(8,128)S(1)} %add.36.refs_0_), channel_id=1, source_target_pairs={{0,1},{1,0},{2,3},{3,2},{4,5},{5,4},{6,7},{7,6},{8,9},{9,8},{10,11... | collective-permute-start | bytes 24584 | tf_op jit(solution)/shard_map/ppermute | solution.py:95
  108.4 2.0 %collective-permute-done.30.refs_2_ = f32[16,128]{1,0:T(8,128)S(1)} collective-permute-done((f32[16,128]{1,0:T(8,128)S(1)}, f32[16,128]{1,0:T(8,128)S(1)}, u32[]{:S(2)}, u32[]{:S(2)}) %collective-permute-start.30) | collective-permute-done | bytes 8224 | tf_op jit(solution)/shard_map/ppermute | solution.py:95
  110.5 1.8 %collective-permute-done.31.refs_3_ = f32[16,128]{1,0:T(8,128)S(1)} collective-permute-done((f32[16,128]{1,0:T(8,128)S(1)}, f32[16,128]{1,0:T(8,128)S(1)}, u32[]{:S(2)}, u32[]{:S(2)}) %collective-permute-start.31) | collective-permute-done | bytes 8224 | tf_op jit(solution)/shard_map/ppermute | solution.py:95
  112.3 1.8 %place.1 = f32[64,1152]{1,0:T(8,128)} custom-call(s32[3]{0:T(128)S(1)} %pad_add_fusion.s_ref, f32[16,128]{1,0:T(8,128)S(1)} %add.36.refs_0_, f32[16,128]{1,0:T(8,128)S(1)} %collective-permute-done.29.refs_1_, f32[16,128]{1,0:T(8,128)S(1)} %collective-permute-done.30.refs_2_, f32[16,128]{1,0:T(8,128)S(1)} %collective-permute-done.31.refs_3_, ...), custom_call_target="tpu_custom_call" | custom-call | tf_op jit(solution)/shard_map/place/pallas_call | solution.py:494
  (55 shorter events, 14.5 us)
Async XLA Ops:
  2.4 26.6 %collective-permute-start.1 = (f32[392,256]{1,0:T(8,128)}, f32[392,256]{1,0:T(8,128)}, u32[]{:S(2)}, u32[]{:S(2)}) collective-permute-start(f32[392,256]{1,0:T(8,128)} %get-tuple-element.28), channel_id=1, source_target_pairs={{0,2},{1,3},{2,0},{3,1},{4,6},{5,7},{6,4},{7,5},{8,10},{9,11},{10,... | collective-permute-start | bytes 1204232 | tf_op jit(solution)/shard_map/ppermute | solution.py:95
  5.5 24.1 %collective-permute-start.2 = (f32[392,256]{1,0:T(8,128)}, f32[392,256]{1,0:T(8,128)}, u32[]{:S(2)}, u32[]{:S(2)}) collective-permute-start(f32[392,256]{1,0:T(8,128)} %get-tuple-element.28), channel_id=1, source_target_pairs={{0,3},{1,2},{2,1},{3,0},{4,7},{5,6},{6,5},{7,4},{8,11},{9,10},{10,... | collective-permute-start | bytes 1204232 | tf_op jit(solution)/shard_map/ppermute | solution.py:95
  6.9 19.2 %collective-permute-start = (f32[392,256]{1,0:T(8,128)}, f32[392,256]{1,0:T(8,128)}, u32[]{:S(2)}, u32[]{:S(2)}) collective-permute-start(f32[392,256]{1,0:T(8,128)} %get-tuple-element.27.refs_0_), channel_id=1, source_target_pairs={{0,1},{1,0},{2,3},{3,2},{4,5},{5,4},{6,7},{7,6},{8,9},{9,8},{10,11... | collective-permute-start | bytes 1204232 | tf_op jit(solution)/shard_map/ppermute | solution.py:95
  18.5 15.5 %collective-permute-start.7 = (f32[392,128]{1,0:T(8,128)}, f32[392,128]{1,0:T(8,128)S(1)}, u32[]{:S(2)}, u32[]{:S(2)}) collective-permute-start(f32[392,128]{1,0:T(8,128)} %get-tuple-element.34), channel_id=1, source_target_pairs={{0,1},{1,0},{2,3},{3,2},{4,5},{5,4},{6,7},{7,6},{8,9},{9,8},{10,11... | collective-permute-start | bytes 602120 | tf_op jit(solution)/shard_map/ppermute | solution.py:95
  20.5 15.2 %collective-permute-start.8 = (f32[392,128]{1,0:T(8,128)}, f32[392,128]{1,0:T(8,128)S(1)}, u32[]{:S(2)}, u32[]{:S(2)}) collective-permute-start(f32[392,128]{1,0:T(8,128)} %get-tuple-element.33.refs_2_), channel_id=1, source_target_pairs={{0,2},{1,3},{2,0},{3,1},{4,6},{5,7},{6,4},{7,5},{8,10},{9,11},{10,... | collective-permute-start | bytes 602120 | tf_op jit(solution)/shard_map/ppermute | solution.py:95
  26.1 9.9 %collective-permute-start.9 = (f32[392,128]{1,0:T(8,128)}, f32[392,128]{1,0:T(8,128)S(1)}, u32[]{:S(2)}, u32[]{:S(2)}) collective-permute-start(f32[392,128]{1,0:T(8,128)} %get-tuple-element.34), channel_id=1, source_target_pairs={{0,3},{1,2},{2,1},{3,0},{4,7},{5,6},{6,5},{7,4},{8,11},{9,10},{10,... | collective-permute-start | bytes 602120 | tf_op jit(solution)/shard_map/ppermute | solution.py:95
  29.0 12.1 %collective-permute-start.3 = (f32[392,128]{1,0:T(8,128)}, f32[392,128]{1,0:T(8,128)S(1)}, u32[]{:S(2)}, u32[]{:S(2)}) collective-permute-start(f32[392,128]{1,0:T(8,128)} %get-tuple-element.30), channel_id=1, source_target_pairs={{0,1},{1,0},{2,3},{3,2},{4,5},{5,4},{6,7},{7,6},{8,9},{9,8},{10,11... | collective-permute-start | bytes 602120 | tf_op jit(solution)/shard_map/ppermute | solution.py:95
  29.6 14.6 %collective-permute-start.5 = (f32[392,128]{1,0:T(8,128)}, f32[392,128]{1,0:T(8,128)S(1)}, u32[]{:S(2)}, u32[]{:S(2)}) collective-permute-start(f32[392,128]{1,0:T(8,128)} %get-tuple-element.30), channel_id=1, source_target_pairs={{0,3},{1,2},{2,1},{3,0},{4,7},{5,6},{6,5},{7,4},{8,11},{9,10},{10,... | collective-permute-start | bytes 602120 | tf_op jit(solution)/shard_map/ppermute | solution.py:95
  34.1 10.1 %collective-permute-start.4 = (f32[392,128]{1,0:T(8,128)}, f32[392,128]{1,0:T(8,128)S(1)}, u32[]{:S(2)}, u32[]{:S(2)}) collective-permute-start(f32[392,128]{1,0:T(8,128)} %get-tuple-element.29.refs_2_), channel_id=1, source_target_pairs={{0,2},{1,3},{2,0},{3,1},{4,6},{5,7},{6,4},{7,5},{8,10},{9,11},{10,... | collective-permute-start | bytes 602120 | tf_op jit(solution)/shard_map/ppermute | solution.py:95
  41.0 7.3 %collective-permute-start.10 = (f32[4,288,128]{2,1,0:T(8,128)S(1)}, f32[4,288,128]{2,1,0:T(8,128)S(1)}, u32[]{:S(2)}, u32[]{:S(2)}) collective-permute-start(f32[4,288,128]{2,1,0:T(8,128)S(1)} %get-tuple-element.36), channel_id=1, source_target_pairs={{0,4},{1,5},{2,6},{3,7},{4,0},{5,1},{6,2},{7,3},{8,12},{9,13},{10,... | collective-permute-start | bytes 1769480 | tf_op jit(solution)/shard_map/ppermute | solution.py:95
  48.3 2.1 %collective-permute-start.6 = (f32[4,288,128]{2,1,0:T(8,128)S(1)}, f32[4,288,128]{2,1,0:T(8,128)S(1)}, u32[]{:S(2)}, u32[]{:S(2)}) collective-permute-start(f32[4,288,128]{2,1,0:T(8,128)S(1)} %get-tuple-element.32), channel_id=1, source_target_pairs={{0,4},{1,5},{2,6},{3,7},{4,0},{5,1},{6,2},{7,3},{8,12},{9,13},{10,... | collective-permute-start | bytes 1769480 | tf_op jit(solution)/shard_map/ppermute | solution.py:95
  50.5 1.2 %collective-permute-start.11 = (f32[8,128]{1,0:T(8,128)S(1)}, f32[8,128]{1,0:T(8,128)S(1)}, u32[]{:S(2)}, u32[]{:S(2)}) collective-permute-start(f32[8,128]{1,0:T(8,128)S(1)} %shard_map.40), channel_id=1, source_target_pairs={{0,4},{1,5},{2,6},{3,7},{4,0},{5,1},{6,2},{7,3},{8,12},{9,13},{10,... | collective-permute-start | bytes 12296 | tf_op jit(solution)/shard_map/ppermute | solution.py:95
  51.8 8.0 %collective-permute-start.12 = (f32[8,128]{1,0:T(8,128)S(1)}, f32[8,128]{1,0:T(8,128)S(1)}, u32[]{:S(2)}, u32[]{:S(2)}) collective-permute-start(f32[8,128]{1,0:T(8,128)S(1)} %add.32.refs_1_), channel_id=1, source_target_pairs={{0,1},{1,0},{2,3},{3,2},{4,5},{5,4},{6,7},{7,6},{8,9},{9,8},{10,11... | collective-permute-start | bytes 12296 | tf_op jit(solution)/shard_map/ppermute | solution.py:95
  52.3 7.5 %collective-permute-start.13 = (f32[8,128]{1,0:T(8,128)S(1)}, f32[8,128]{1,0:T(8,128)S(1)}, u32[]{:S(2)}, u32[]{:S(2)}) collective-permute-start(f32[8,128]{1,0:T(8,128)S(1)} %add.32.refs_1_), channel_id=1, source_target_pairs={{0,2},{1,3},{2,0},{3,1},{4,6},{5,7},{6,4},{7,5},{8,10},{9,11},{10,... | collective-permute-start | bytes 12296 | tf_op jit(solution)/shard_map/ppermute | solution.py:95
  53.5 6.3 %collective-permute-start.14 = (f32[8,128]{1,0:T(8,128)S(1)}, f32[8,128]{1,0:T(8,128)S(1)}, u32[]{:S(2)}, u32[]{:S(2)}) collective-permute-start(f32[8,128]{1,0:T(8,128)S(1)} %add.32.refs_1_), channel_id=1, source_target_pairs={{0,3},{1,2},{2,1},{3,0},{4,7},{5,6},{6,5},{7,4},{8,11},{9,10},{10,... | collective-permute-start | bytes 12296 | tf_op jit(solution)/shard_map/ppermute | solution.py:95
  55.2 11.7 %collective-permute-start.23 = (f32[288,128]{1,0:T(8,128)S(1)}, f32[288,128]{1,0:T(8,128)S(1)}, u32[]{:S(2)}, u32[]{:S(2)}) collective-permute-start(f32[288,128]{1,0:T(8,128)S(1)} %get-tuple-element.45), channel_id=1, source_target_pairs={{0,19},{1,23},{2,17},{3,21},{4,27},{5,31},{6,25},{7,29},{8,18},{9,... | collective-permute-start | bytes 442376 | tf_op jit(solution)/shard_map/ppermute | solution.py:95
  58.5 9.5 %collective-permute-start.24 = (f32[288,128]{1,0:T(8,128)S(1)}, f32[288,128]{1,0:T(8,128)S(1)}, u32[]{:S(2)}, u32[]{:S(2)}) collective-permute-start(f32[288,128]{1,0:T(8,128)S(1)} %get-tuple-element.46), channel_id=1, source_target_pairs={{0,27},{1,31},{2,25},{3,29},{4,19},{5,23},{6,17},{7,21},{8,26},{9,... | collective-permute-start | bytes 442376 | tf_op jit(solution)/shard_map/ppermute | solution.py:95
  60.0 15.6 %collective-permute-start.15 = (f32[288,128]{1,0:T(8,128)S(1)}, f32[288,128]{1,0:T(8,128)S(1)}, u32[]{:S(2)}, u32[]{:S(2)}) collective-permute-start(f32[288,128]{1,0:T(8,128)S(1)} %get-tuple-element.37), channel_id=1, source_target_pairs={{0,0},{1,4},{2,2},{3,6},{4,8},{5,12},{6,10},{7,14},{8,1},{9,5},{10... | collective-permute-start | bytes 442376 | tf_op jit(solution)/shard_map/ppermute | solution.py:95
  60.7 17.9 %collective-permute-start.16 = (f32[288,128]{1,0:T(8,128)S(1)}, f32[288,128]{1,0:T(8,128)S(1)}, u32[]{:S(2)}, u32[]{:S(2)}) collective-permute-start(f32[288,128]{1,0:T(8,128)S(1)} %get-tuple-element.38), channel_id=1, source_target_pairs={{0,1},{1,5},{2,3},{3,7},{4,9},{5,13},{6,11},{7,15},{8,0},{9,4},{10... | collective-permute-start | bytes 442376 | tf_op jit(solution)/shard_map/ppermute | solution.py:95
  63.7 10.9 %collective-permute-start.22 = (f32[8,128]{1,0:T(8,128)S(1)}, f32[8,128]{1,0:T(8,128)S(1)}, u32[]{:S(2)}, u32[]{:S(2)}) collective-permute-start(f32[8,128]{1,0:T(8,128)S(1)} %get-tuple-element.44), channel_id=1, source_target_pairs={{0,19},{1,23},{2,17},{3,21},{4,27},{5,31},{6,25},{7,29},{8,18},{9,... | collective-permute-start | bytes 12296 | tf_op jit(solution)/shard_map/ppermute | solution.py:95
  67.0 12.0 %collective-permute-start.17 = (f32[288,128]{1,0:T(8,128)S(1)}, f32[288,128]{1,0:T(8,128)S(1)}, u32[]{:S(2)}, u32[]{:S(2)}) collective-permute-start(f32[288,128]{1,0:T(8,128)S(1)} %get-tuple-element.39), channel_id=1, source_target_pairs={{0,2},{1,6},{2,0},{3,4},{4,10},{5,14},{6,8},{7,12},{8,3},{9,7},{10... | collective-permute-start | bytes 442376 | tf_op jit(solution)/shard_map/ppermute | solution.py:95
  68.0 11.7 %collective-permute-start.18 = (f32[288,128]{1,0:T(8,128)S(1)}, f32[288,128]{1,0:T(8,128)S(1)}, u32[]{:S(2)}, u32[]{:S(2)}) collective-permute-start(f32[288,128]{1,0:T(8,128)S(1)} %get-tuple-element.40), channel_id=1, source_target_pairs={{0,3},{1,7},{2,1},{3,5},{4,11},{5,15},{6,9},{7,13},{8,2},{9,6},{10... | collective-permute-start | bytes 442376 | tf_op jit(solution)/shard_map/ppermute | solution.py:95
  74.5 16.2 %collective-permute-start.19 = (f32[288,128]{1,0:T(8,128)S(1)}, f32[288,128]{1,0:T(8,128)S(1)}, u32[]{:S(2)}, u32[]{:S(2)}) collective-permute-start(f32[288,128]{1,0:T(8,128)S(1)} %get-tuple-element.41), channel_id=1, source_target_pairs={{0,16},{1,20},{2,18},{3,22},{4,24},{5,28},{6,26},{7,30},{8,17},{9,... | collective-permute-start | bytes 442376 | tf_op jit(solution)/shard_map/ppermute | solution.py:95
  75.6 15.1 %collective-permute-start.20 = (f32[288,128]{1,0:T(8,128)S(1)}, f32[288,128]{1,0:T(8,128)S(1)}, u32[]{:S(2)}, u32[]{:S(2)}) collective-permute-start(f32[288,128]{1,0:T(8,128)S(1)} %get-tuple-element.42), channel_id=1, source_target_pairs={{0,17},{1,21},{2,19},{3,23},{4,25},{5,29},{6,27},{7,31},{8,16},{9,... | collective-permute-start | bytes 442376 | tf_op jit(solution)/shard_map/ppermute | solution.py:95
  78.6 18.3 %collective-permute-start.21 = (f32[288,128]{1,0:T(8,128)S(1)}, f32[288,128]{1,0:T(8,128)S(1)}, u32[]{:S(2)}, u32[]{:S(2)}) collective-permute-start(f32[288,128]{1,0:T(8,128)S(1)} %get-tuple-element.43), channel_id=1, source_target_pairs={{0,18},{1,22},{2,16},{3,20},{4,26},{5,30},{6,24},{7,28},{8,19},{9,... | collective-permute-start | bytes 442376 | tf_op jit(solution)/shard_map/ppermute | solution.py:95
  97.7 4.6 %collective-permute-start.26 = (f32[16,128]{1,0:T(8,128)S(1)}, f32[16,128]{1,0:T(8,128)S(1)}, u32[]{:S(2)}, u32[]{:S(2)}) collective-permute-start(f32[16,128]{1,0:T(8,128)S(1)} %get-tuple-element.47), channel_id=1, source_target_pairs={{0,16},{1,17},{2,18},{3,19},{4,20},{5,21},{6,22},{7,23},{8,24},{9,... | collective-permute-start | bytes 24584 | tf_op jit(solution)/shard_map/ppermute | solution.py:95
  97.8 5.6 %collective-permute-start.27 = (f32[16,128]{1,0:T(8,128)S(1)}, f32[16,128]{1,0:T(8,128)S(1)}, u32[]{:S(2)}, u32[]{:S(2)}) collective-permute-start(f32[16,128]{1,0:T(8,128)S(1)} %get-tuple-element.47), channel_id=1, source_target_pairs={{0,24},{1,25},{2,26},{3,27},{4,28},{5,29},{6,30},{7,31},{8,16},{9,... | collective-permute-start | bytes 24584 | tf_op jit(solution)/shard_map/ppermute | solution.py:95
  98.4 4.9 %collective-permute-start.25 = (f32[16,128]{1,0:T(8,128)S(1)}, f32[16,128]{1,0:T(8,128)S(1)}, u32[]{:S(2)}, u32[]{:S(2)}) collective-permute-start(f32[16,128]{1,0:T(8,128)S(1)} %get-tuple-element.47), channel_id=1, source_target_pairs={{0,8},{1,9},{2,10},{3,11},{4,12},{5,13},{6,14},{7,15},{8,0},{9,1},... | collective-permute-start | bytes 24584 | tf_op jit(solution)/shard_map/ppermute | solution.py:95
  103.4 1.2 %collective-permute-start.28 = (f32[16,128]{1,0:T(8,128)S(1)}, f32[16,128]{1,0:T(8,128)S(1)}, u32[]{:S(2)}, u32[]{:S(2)}) collective-permute-start(f32[16,128]{1,0:T(8,128)S(1)} %add_add_fusion), channel_id=1, source_target_pairs={{0,4},{1,5},{2,6},{3,7},{4,0},{5,1},{6,2},{7,3},{8,12},{9,13},{10,... | collective-permute-start | bytes 24584 | tf_op jit(solution)/shard_map/ppermute | solution.py:95
  104.6 3.8 %collective-permute-start.29 = (f32[16,128]{1,0:T(8,128)S(1)}, f32[16,128]{1,0:T(8,128)S(1)}, u32[]{:S(2)}, u32[]{:S(2)}) collective-permute-start(f32[16,128]{1,0:T(8,128)S(1)} %add.36.refs_0_), channel_id=1, source_target_pairs={{0,1},{1,0},{2,3},{3,2},{4,5},{5,4},{6,7},{7,6},{8,9},{9,8},{10,11... | collective-permute-start | bytes 24584 | tf_op jit(solution)/shard_map/ppermute | solution.py:95
  106.8 3.7 %collective-permute-start.30 = (f32[16,128]{1,0:T(8,128)S(1)}, f32[16,128]{1,0:T(8,128)S(1)}, u32[]{:S(2)}, u32[]{:S(2)}) collective-permute-start(f32[16,128]{1,0:T(8,128)S(1)} %add.36.refs_0_), channel_id=1, source_target_pairs={{0,2},{1,3},{2,0},{3,1},{4,6},{5,7},{6,4},{7,5},{8,10},{9,11},{10,... | collective-permute-start | bytes 24584 | tf_op jit(solution)/shard_map/ppermute | solution.py:95
  107.7 4.5 %collective-permute-start.31 = (f32[16,128]{1,0:T(8,128)S(1)}, f32[16,128]{1,0:T(8,128)S(1)}, u32[]{:S(2)}, u32[]{:S(2)}) collective-permute-start(f32[16,128]{1,0:T(8,128)S(1)} %add.36.refs_0_), channel_id=1, source_target_pairs={{0,3},{1,2},{2,1},{3,0},{4,7},{5,6},{6,5},{7,4},{8,11},{9,10},{10,... | collective-permute-start | bytes 24584 | tf_op jit(solution)/shard_map/ppermute | solution.py:95
  (3 other events, 14.1 us)

commit v5 on v4

--- a/solution.py
+++ b/solution.py
@@ -11,7 +11,7 @@
 BLK = 32
 AHEAD = 2
 SHARED = 24 * 2**20
-ALONE = 65 * 2**20
+ALONE = 58 * 2**20
 
 
 def partner(value, axis, distance):
@@ -124,22 +124,16 @@
     return jnp.concatenate(evens, axis=1), jnp.concatenate(odds, axis=1)
 
 
-def split_kernel(s_ref, x_ref, own_ref, other_ref, buf, halves, in_sems, out_sems):
+def split_kernel(s_ref, x_ref, own_ref, other_ref, buf, sems):
     strips, strip, _ = buf.shape
     spans = [pl.ds(r * strip, strip) for r in range(strips)]
-    copies = fetch([x_ref.at[span] for span in spans], [buf.at[r] for r in range(strips)], in_sems)
+    copies = fetch([x_ref.at[span] for span in spans], [buf.at[r] for r in range(strips)], sems)
     up = s_ref[0] == 1
-    stores = []
     for r in range(strips):
         copies[r].wait()
         even, odd = lane_halves(buf[r])
-        halves[2 * r] = jnp.where(up, odd, even)
-        halves[2 * r + 1] = jnp.where(up, even, odd)
-        for k, ref in enumerate((own_ref, other_ref)):
-            stores.append(pltpu.make_async_copy(halves.at[2 * r + k], ref.at[spans[r]], out_sems.at[2 * r + k]))
-            stores[-1].start()
-    for store in stores:
-        store.wait()
+        own_ref[spans[r]] = jnp.where(up, odd, even)
+        other_ref[spans[r]] = jnp.where(up, even, odd)
 
 
 def residual_kernel(s_ref, x_ref, t_ref, w_ref, own_far, other_far, own_near, other_near, *scratch):
@@ -182,14 +176,13 @@
 
 
 def prepare_kernel(side, *refs):
-    sources, (out_ref, buf, sems) = refs[:4], refs[4:]
-    copies = fetch(sources, [buf.at[i] for i in range(4)], sems)
-    _, _, width = buf.shape
+    sources, (far_ref, near_ref, out_ref, far_out, near_out) = refs[:4], refs[4:]
+    far_out[...] = far_ref[...]
+    near_out[...] = near_ref[...]
+    width = sources[0].shape[1]
     span = out_ref.shape[2] // 2
-    for copy in copies:
-        copy.wait()
     for r in range(side):
-        strip = gather([buf.at[i] for i in range(4)], r, side)
+        strip = gather(sources, r, side)
         strip = strip.reshape(-1, width)
         strip = jnp.concatenate([strip, jnp.zeros((span - strip.shape[0], width), jnp.float32)], axis=0)
         xh, xl = split2(strip.T)
@@ -311,7 +304,8 @@
 
 
 def slot_of(d, dy):
-    return 4 * (d // 2) + 2 * dy + d % 2
+    index = 2 * dy + d % 2
+    return 7 - index if d // 2 else index
 
 
 def place_kernel(s_ref, *refs):
@@ -374,12 +368,10 @@
         split_kernel,
         out_shape=(f32(rows, width), f32(rows, width)),
         in_specs=[SM, HB],
-        out_specs=(HB, HB),
+        out_specs=(VM, VM),
         scratch_shapes=[
             pltpu.VMEM((side, rows // side, channels), jnp.float32),
-            pltpu.VMEM((2 * side, rows // side, width), jnp.float32),
             pltpu.SemaphoreType.DMA((side,)),
-            pltpu.SemaphoreType.DMA((2 * side,)),
         ],
         compiler_params=pltpu.CompilerParams(vmem_limit_bytes=ALONE),
         name="split_images",
@@ -415,15 +407,15 @@
 
     span = (side + 1) * 4 * imgs
     xt_shape = (side, width, 2 * span)
-    images_t = pl.pallas_call(
+    images_t, *own_pieces = pl.pallas_call(
         lambda *refs: prepare_kernel(side, *refs),
-        out_shape=jax.ShapeDtypeStruct(xt_shape, jnp.bfloat16),
-        in_specs=[HB] * 4,
-        out_specs=VM,
-        scratch_shapes=[pltpu.VMEM((4, rows, width), jnp.float32), pltpu.SemaphoreType.DMA((4,))],
+        out_shape=(jax.ShapeDtypeStruct(xt_shape, jnp.bfloat16),) + (f32(rows, 128),) * 2,
+        in_specs=[VM] * 6,
+        out_specs=(VM,) * 3,
         compiler_params=pltpu.CompilerParams(vmem_limit_bytes=SHARED),
         name="prepare",
-    )(x_own, x_x, x_y, x_d)
+    )(x_own, x_x, x_y, x_d, own_far, own_near)
+    far, near = (own_pieces[0], *far[1:]), (own_pieces[1], *near[1:])
 
     z_count = lax.axis_size("node") // 2
     part = taps * width // 8
@@ -431,7 +423,7 @@
     half = count // 2
     place = scalars(z // 2, x, y)
 
-    def gradient(pieces, early):
+    def gradient(pieces, early, flip):
         return pl.pallas_call(
             lambda *refs: gradient_kernel(1.0 / rows, side, *refs),
             out_shape=(f32(half, part, 128),) * 2 + (f32(part, 128),) * early,
@@ -446,7 +438,7 @@
                 flops=24 * rows * taps * width * 128, bytes_accessed=4 * taps * width * 128, transcendentals=0
             ),
             compiler_params=pltpu.CompilerParams(vmem_limit_bytes=SHARED),
-        )(scalars(c, y, z % 2), images_t, *pieces)
+        )(scalars(c, y ^ flip, z % 2 ^ flip), images_t, *pieces)
 
     def dots(keep, received, before):
         return pl.pallas_call(
@@ -458,12 +450,12 @@
         )(scalars(c), keep, received, *before)
 
     across = lambda z, c, y, x: (z, 1 - c, y, x)
-    keep_far, send_far, early_keep, early_send = gradient(far, 2)
+    keep_far, send_far, early_keep, early_send = gradient(far, 2, 1)
     received_far = hop(send_far, across)
     last = half - 1
     early_own = hop(early_keep, mover(count - 1))
     early_other = hop(early_send, lambda z, c, y, x: mover(count - 1)(z, 1 - c, y, x))
-    keep_near, send_near = gradient(near, 0)
+    keep_near, send_near = gradient(near, 0, 0)
     received_near = hop(send_near, across)
     totals = dots(keep_far, received_far, ())
     totals = plane_sum(dots(keep_near, received_near, (totals,)))
@@ -504,7 +496,9 @@
 
 
 def mover(index):
-    e, dy, dx = index // 4, index // 2 % 2, index % 2
+    e = index // 4
+    index = 7 - index if e else index
+    dy, dx = index // 2, index % 2
     return lambda z, c, y, x: (2 * (z // 2 ^ e) + c, x, y ^ dy, z % 2 ^ dx)
 
 

time: 114 us -> 115 us (level)
  waiting for transfers between devices: 35.5 us -> 40.9 us
  starting transfers between devices: 48.8 us -> 45 us
    ppermute x32, waiting for transfers between devices: 35.5 us -> 40.9 us  [hop(): return lax.ppermute(value, ('node', 'local'), pairs)]
    ppermute x32, starting transfers between devices: 48.8 us -> 45 us  [hop(): return lax.ppermute(value, ('node', 'local'), pairs)]
    pallas_call x1, Pallas kernels: 2.01 us -> 0.55 us  [tiles(): pl.pallas_call(lambda *refs: prepare_kernel(side, *refs), out_shape=(jax....]
  transfers between devices with their start and end apart: 32 -> 32, of which waited for: 14 -> 16; matrix products, arithmetic and copies ran while one was open for 1% -> 1% of each run, Pallas kernels for 19% -> 18%
where the time goes in v5:
time: 115 us
  starting transfers between devices  45 us (39%)
  waiting for transfers between devices  40.9 us (36%)
  Pallas kernels  25.7 us (22%)
  local copies, waits for them, and re-layouts  1.89 us (2%)
    ppermute x32, starting transfers between devices, hop(): return lax.ppermute(value, ('node', 'local'), pairs)  45 us
    ppermute x32, waiting for transfers between devices, hop(): return lax.ppermute(value, ('node', 'local'), pairs)  40.9 us
    pallas_call x1, Pallas kernels, tiles(): pl.pallas_call(residual_kernel, out_shape=(f32(rows, 128),) * 4, in_specs...  10.9 us
    pallas_call x2, Pallas kernels, gradient(): pl.pallas_call(lambda *refs: gradient_kernel(1.0 / rows, side, *refs), ou...  8.2 us
    pallas_call x1, Pallas kernels, tiles(): pl.pallas_call(split_kernel, out_shape=(f32(rows, width), f32(rows, width...  2.56 us
  transfers between devices with their start and end apart: 32, of which 16 were waited for; matrix products, arithmetic and copies ran while one was open for 1% of the time, Pallas kernels for 18%

profile of v5, /device:TPU:0, one launch (start us, length us, event | category | flops | bytes accessed | tf_op | source)
XLA Modules:
  0.0 114.5 jit_solution(13757000152871199412)
XLA Ops:
  0.0 2.6 %split_images.1 = (f32[392,256]{1,0:T(8,128)}, f32[392,256]{1,0:T(8,128)}) custom-call(s32[1]{0:T(128)} %bitcast.2.s_ref, f32[392,512]{1,0:T(8,128)} %bitcast.15), custom_call_target="tpu_custom_call" | custom-call | tf_op jit(solution)/shard_map/split_images/pallas_call | solution.py:367
  2.6 3.1 %collective-permute-start.1 = (f32[392,256]{1,0:T(8,128)}, f32[392,256]{1,0:T(8,128)S(1)}, u32[]{:S(2)}, u32[]{:S(2)}) collective-permute-start(f32[392,256]{1,0:T(8,128)} %get-tuple-element.31), channel_id=1, source_target_pairs={{0,2},{1,3},{2,0},{3,1},{4,6},{5,7},{6,4},{7,5},{8,10},{9,11},{10,... | collective-permute-start | bytes 1204232 | tf_op jit(solution)/shard_map/ppermute | solution.py:95
  5.6 1.4 %collective-permute-start.2 = (f32[392,256]{1,0:T(8,128)}, f32[392,256]{1,0:T(8,128)S(1)}, u32[]{:S(2)}, u32[]{:S(2)}) collective-permute-start(f32[392,256]{1,0:T(8,128)} %get-tuple-element.31), channel_id=1, source_target_pairs={{0,3},{1,2},{2,1},{3,0},{4,7},{5,6},{6,5},{7,4},{8,11},{9,10},{10,... | collective-permute-start | bytes 1204232 | tf_op jit(solution)/shard_map/ppermute | solution.py:95
  7.8 10.9 %residual.1 = (f32[392,128]{1,0:T(8,128)}, f32[392,128]{1,0:T(8,128)}, f32[392,128]{1,0:T(8,128)}, f32[392,128]{1,0:T(8,128)}) custom-call(s32[2]{0:T(128)} %pad_add_fusion.2.s_ref, f32[392,512]{1,0:T(8,128)} %bitcast.16, f32[392,512]{1,0:T(8,128)} %bitcast.18, f32[9,512,512]{2,1,0:T(8,128)} %bitcast.17), custom_call_target="tpu_custom_call" | custom-call | flops 5549064192 | bytes 9437184 | tf_op jit(solution)/shard_map/residual/pallas_call | solution.py:385
  18.7 2.0 %collective-permute-start.7 = (f32[392,128]{1,0:T(8,128)}, f32[392,128]{1,0:T(8,128)S(1)}, u32[]{:S(2)}, u32[]{:S(2)}) collective-permute-start(f32[392,128]{1,0:T(8,128)} %get-tuple-element.40), channel_id=1, source_target_pairs={{0,1},{1,0},{2,3},{3,2},{4,5},{5,4},{6,7},{7,6},{8,9},{9,8},{10,11... | collective-permute-start | bytes 602120 | tf_op jit(solution)/shard_map/ppermute | solution.py:95
  20.7 1.5 %collective-permute-start.9 = (f32[392,128]{1,0:T(8,128)}, f32[392,128]{1,0:T(8,128)S(1)}, u32[]{:S(2)}, u32[]{:S(2)}) collective-permute-start(f32[392,128]{1,0:T(8,128)} %get-tuple-element.40), channel_id=1, source_target_pairs={{0,3},{1,2},{2,1},{3,0},{4,7},{5,6},{6,5},{7,4},{8,11},{9,10},{10,... | collective-permute-start | bytes 602120 | tf_op jit(solution)/shard_map/ppermute | solution.py:95
  22.2 3.9 %collective-permute-done.refs_1_ = f32[392,256]{1,0:T(8,128)S(1)} collective-permute-done((f32[392,256]{1,0:T(8,128)}, f32[392,256]{1,0:T(8,128)S(1)}, u32[]{:S(2)}, u32[]{:S(2)}) %collective-permute-start) | collective-permute-done | bytes 401440 | tf_op jit(solution)/shard_map/ppermute | solution.py:95
  26.1 1.9 %collective-permute-start.8 = (f32[392,128]{1,0:T(8,128)}, f32[392,128]{1,0:T(8,128)S(1)}, u32[]{:S(2)}, u32[]{:S(2)}) collective-permute-start(f32[392,128]{1,0:T(8,128)} %get-tuple-element.32.refs_4_), channel_id=1, source_target_pairs={{0,2},{1,3},{2,0},{3,1},{4,6},{5,7},{6,4},{7,5},{8,10},{9,11},{10,... | collective-permute-start | bytes 602120 | tf_op jit(solution)/shard_map/ppermute | solution.py:95
  28.2 1.5 %collective-permute-start.3 = (f32[392,128]{1,0:T(8,128)}, f32[392,128]{1,0:T(8,128)S(1)}, u32[]{:S(2)}, u32[]{:S(2)}) collective-permute-start(f32[392,128]{1,0:T(8,128)} %get-tuple-element.36), channel_id=1, source_target_pairs={{0,1},{1,0},{2,3},{3,2},{4,5},{5,4},{6,7},{7,6},{8,9},{9,8},{10,11... | collective-permute-start | bytes 602120 | tf_op jit(solution)/shard_map/ppermute | solution.py:95
  32.7 1.6 %collective-permute-start.5 = (f32[392,128]{1,0:T(8,128)}, f32[392,128]{1,0:T(8,128)S(1)}, u32[]{:S(2)}, u32[]{:S(2)}) collective-permute-start(f32[392,128]{1,0:T(8,128)} %get-tuple-element.36), channel_id=1, source_target_pairs={{0,3},{1,2},{2,1},{3,0},{4,7},{5,6},{6,5},{7,4},{8,11},{9,10},{10,... | collective-permute-start | bytes 602120 | tf_op jit(solution)/shard_map/ppermute | solution.py:95
  34.3 3.6 %collective-permute-done.8.refs_4_ = f32[392,128]{1,0:T(8,128)S(1)} collective-permute-done((f32[392,128]{1,0:T(8,128)}, f32[392,128]{1,0:T(8,128)S(1)}, u32[]{:S(2)}, u32[]{:S(2)}) %collective-permute-start.8) | collective-permute-done | bytes 200736 | tf_op jit(solution)/shard_map/ppermute | solution.py:95
  37.9 4.1 %shard_map.38 = (f32[4,288,128]{2,1,0:T(8,128)S(1)}, f32[4,288,128]{2,1,0:T(8,128)S(1)}, f32[288,128]{1,0:T(8,128)S(1)}, f32[288,128]{1,0:T(8,128)S(1)}) custom-call(s32[3]{0:T(128)S(1)} %pad_add_fusion.3.refs_0_, bf16[7,256,512]{2,1,0:T(8,128)(2,1)S(1)} %get-tuple-element.34.refs_1_, f32[392,128]{1,0:T(8,128)S(1)} %get-tuple-element.39.refs_2_, ...), custom_call_target="tpu_custom_call" | custom-call | flops 2774532096 | bytes 1179648 | tf_op jit(solution)/shard_map/pallas_call | solution.py:427
  42.1 2.2 %collective-permute-done.4.refs_4_ = f32[392,128]{1,0:T(8,128)S(1)} collective-permute-done((f32[392,128]{1,0:T(8,128)}, f32[392,128]{1,0:T(8,128)S(1)}, u32[]{:S(2)}, u32[]{:S(2)}) %collective-permute-start.4) | collective-permute-done | bytes 200736 | tf_op jit(solution)/shard_map/ppermute | solution.py:95
  44.3 4.1 %shard_map.37 = (f32[4,288,128]{2,1,0:T(8,128)S(1)}, f32[4,288,128]{2,1,0:T(8,128)S(1)}) custom-call(s32[3]{0:T(128)S(1)} %pad_add_fusion.1.refs_0_, bf16[7,256,512]{2,1,0:T(8,128)(2,1)S(1)} %get-tuple-element.34.refs_1_, f32[392,128]{1,0:T(8,128)S(1)} %get-tuple-element.35.refs_2_, f32[392,128]{1,0:T(8,128)S(1)} %collective-permute-done.3.refs_3_, ...), custom_call_target="tpu_custom_call" | custom-call | flops 2774532096 | bytes 1179648 | tf_op jit(solution)/shard_map/pallas_call | solution.py:427
  48.6 1.8 %collective-permute-done.6.received_ref.refs_6_ = f32[4,288,128]{2,1,0:T(8,128)S(1)} collective-permute-done((f32[4,288,128]{2,1,0:T(8,128)S(1)}, f32[4,288,128]{2,1,0:T(8,128)S(1)}, u32[]{:S(2)}, u32[]{:S(2)}) %collective-permute-start.6) | collective-permute-done | bytes 589856 | tf_op jit(solution)/shard_map/ppermute | solution.py:95
  53.0 1.5 %collective-permute-start.13 = (f32[8,128]{1,0:T(8,128)S(1)}, f32[8,128]{1,0:T(8,128)S(1)}, u32[]{:S(2)}, u32[]{:S(2)}) collective-permute-start(f32[8,128]{1,0:T(8,128)S(1)} %add.32.refs_1_), channel_id=1, source_target_pairs={{0,2},{1,3},{2,0},{3,1},{4,6},{5,7},{6,4},{7,5},{8,10},{9,11},{10,... | collective-permute-start | bytes 12296 | tf_op jit(solution)/shard_map/ppermute | solution.py:95
  55.4 2.6 %collective-permute-start.23 = (f32[288,128]{1,0:T(8,128)S(1)}, f32[288,128]{1,0:T(8,128)S(1)}, u32[]{:S(2)}, u32[]{:S(2)}) collective-permute-start(f32[288,128]{1,0:T(8,128)S(1)} %get-tuple-element.51), channel_id=1, source_target_pairs={{0,16},{1,20},{2,18},{3,22},{4,24},{5,28},{6,26},{7,30},{8,17},{9,... | collective-permute-start | bytes 442376 | tf_op jit(solution)/shard_map/ppermute | solution.py:95
  57.9 1.8 %collective-permute-start.24 = (f32[288,128]{1,0:T(8,128)S(1)}, f32[288,128]{1,0:T(8,128)S(1)}, u32[]{:S(2)}, u32[]{:S(2)}) collective-permute-start(f32[288,128]{1,0:T(8,128)S(1)} %get-tuple-element.52), channel_id=1, source_target_pairs={{0,24},{1,28},{2,26},{3,30},{4,16},{5,20},{6,18},{7,22},{8,25},{9,... | collective-permute-start | bytes 442376 | tf_op jit(solution)/shard_map/ppermute | solution.py:95
  60.7 2.6 %collective-permute-start.16 = (f32[288,128]{1,0:T(8,128)S(1)}, f32[288,128]{1,0:T(8,128)S(1)}, u32[]{:S(2)}, u32[]{:S(2)}) collective-permute-start(f32[288,128]{1,0:T(8,128)S(1)} %get-tuple-element.44), channel_id=1, source_target_pairs={{0,1},{1,5},{2,3},{3,7},{4,9},{5,13},{6,11},{7,15},{8,0},{9,4},{10... | collective-permute-start | bytes 442376 | tf_op jit(solution)/shard_map/ppermute | solution.py:95
  63.5 1.7 %collective-permute-start.22 = (f32[8,128]{1,0:T(8,128)S(1)}, f32[8,128]{1,0:T(8,128)S(1)}, u32[]{:S(2)}, u32[]{:S(2)}) collective-permute-start(f32[8,128]{1,0:T(8,128)S(1)} %get-tuple-element.50), channel_id=1, source_target_pairs={{0,16},{1,20},{2,18},{3,22},{4,24},{5,28},{6,26},{7,30},{8,17},{9,... | collective-permute-start | bytes 12296 | tf_op jit(solution)/shard_map/ppermute | solution.py:95
  65.3 4.1 %collective-permute-done.23.refs_8_ = f32[288,128]{1,0:T(8,128)S(1)} collective-permute-done((f32[288,128]{1,0:T(8,128)S(1)}, f32[288,128]{1,0:T(8,128)S(1)}, u32[]{:S(2)}, u32[]{:S(2)}) %collective-permute-start.23) | collective-permute-done | bytes 147488 | tf_op jit(solution)/shard_map/ppermute | solution.py:95
  69.4 1.2 %collective-permute-start.17 = (f32[288,128]{1,0:T(8,128)S(1)}, f32[288,128]{1,0:T(8,128)S(1)}, u32[]{:S(2)}, u32[]{:S(2)}) collective-permute-start(f32[288,128]{1,0:T(8,128)S(1)} %get-tuple-element.45), channel_id=1, source_target_pairs={{0,2},{1,6},{2,0},{3,4},{4,10},{5,14},{6,8},{7,12},{8,3},{9,7},{10... | collective-permute-start | bytes 442376 | tf_op jit(solution)/shard_map/ppermute | solution.py:95
  72.3 4.4 %collective-permute-start.19 = (f32[288,128]{1,0:T(8,128)S(1)}, f32[288,128]{1,0:T(8,128)S(1)}, u32[]{:S(2)}, u32[]{:S(2)}) collective-permute-start(f32[288,128]{1,0:T(8,128)S(1)} %get-tuple-element.47), channel_id=1, source_target_pairs={{0,19},{1,23},{2,17},{3,21},{4,27},{5,31},{6,25},{7,29},{8,18},{9,... | collective-permute-start | bytes 442376 | tf_op jit(solution)/shard_map/ppermute | solution.py:95
  77.3 3.9 %collective-permute-start.21 = (f32[288,128]{1,0:T(8,128)S(1)}, f32[288,128]{1,0:T(8,128)S(1)}, u32[]{:S(2)}, u32[]{:S(2)}) collective-permute-start(f32[288,128]{1,0:T(8,128)S(1)} %get-tuple-element.49), channel_id=1, source_target_pairs={{0,17},{1,21},{2,19},{3,23},{4,25},{5,29},{6,27},{7,31},{8,16},{9,... | collective-permute-start | bytes 442376 | tf_op jit(solution)/shard_map/ppermute | solution.py:95
  81.3 1.4 %collective-permute-done.19.refs_4_.refs_8_ = f32[288,128]{1,0:T(8,128)S(1)} collective-permute-done((f32[288,128]{1,0:T(8,128)S(1)}, f32[288,128]{1,0:T(8,128)S(1)}, u32[]{:S(2)}, u32[]{:S(2)}) %collective-permute-start.19) | collective-permute-done | bytes 147488 | tf_op jit(solution)/shard_map/ppermute | solution.py:95
  82.6 11.8 %collective-permute-done.20.refs_5_.refs_9_ = f32[288,128]{1,0:T(8,128)S(1)} collective-permute-done((f32[288,128]{1,0:T(8,128)S(1)}, f32[288,128]{1,0:T(8,128)S(1)}, u32[]{:S(2)}, u32[]{:S(2)}) %collective-permute-start.20) | collective-permute-done | bytes 147488 | tf_op jit(solution)/shard_map/ppermute | solution.py:95
  95.3 3.7 %collective-permute-start.26 = (f32[16,128]{1,0:T(8,128)S(1)}, f32[16,128]{1,0:T(8,128)S(1)}, u32[]{:S(2)}, u32[]{:S(2)}) collective-permute-start(f32[16,128]{1,0:T(8,128)S(1)} %get-tuple-element.53), channel_id=1, source_target_pairs={{0,16},{1,17},{2,18},{3,19},{4,20},{5,21},{6,22},{7,23},{8,24},{9,... | collective-permute-start | bytes 24584 | tf_op jit(solution)/shard_map/ppermute | solution.py:95
  100.6 3.8 %collective-permute-done.27 = f32[16,128]{1,0:T(8,128)S(1)} collective-permute-done((f32[16,128]{1,0:T(8,128)S(1)}, f32[16,128]{1,0:T(8,128)S(1)}, u32[]{:S(2)}, u32[]{:S(2)}) %collective-permute-start.27) | collective-permute-done | bytes 8224 | tf_op jit(solution)/shard_map/ppermute | solution.py:95
  105.7 1.8 %collective-permute-start.29 = (f32[16,128]{1,0:T(8,128)S(1)}, f32[16,128]{1,0:T(8,128)S(1)}, u32[]{:S(2)}, u32[]{:S(2)}) collective-permute-start(f32[16,128]{1,0:T(8,128)S(1)} %add.36.refs_0_), channel_id=1, source_target_pairs={{0,1},{1,0},{2,3},{3,2},{4,5},{5,4},{6,7},{7,6},{8,9},{9,8},{10,11... | collective-permute-start | bytes 24584 | tf_op jit(solution)/shard_map/ppermute | solution.py:95
  109.4 1.8 %collective-permute-done.30.refs_2_ = f32[16,128]{1,0:T(8,128)S(1)} collective-permute-done((f32[16,128]{1,0:T(8,128)S(1)}, f32[16,128]{1,0:T(8,128)S(1)}, u32[]{:S(2)}, u32[]{:S(2)}) %collective-permute-start.30) | collective-permute-done | bytes 8224 | tf_op jit(solution)/shard_map/ppermute | solution.py:95
  111.2 1.6 %collective-permute-done.31.refs_3_ = f32[16,128]{1,0:T(8,128)S(1)} collective-permute-done((f32[16,128]{1,0:T(8,128)S(1)}, f32[16,128]{1,0:T(8,128)S(1)}, u32[]{:S(2)}, u32[]{:S(2)}) %collective-permute-start.31) | collective-permute-done | bytes 8224 | tf_op jit(solution)/shard_map/ppermute | solution.py:95
  112.7 1.8 %place.1 = f32[64,1152]{1,0:T(8,128)} custom-call(s32[3]{0:T(128)S(1)} %pad_add_fusion.s_ref, f32[16,128]{1,0:T(8,128)S(1)} %add.36.refs_0_, f32[16,128]{1,0:T(8,128)S(1)} %collective-permute-done.29.refs_1_, f32[16,128]{1,0:T(8,128)S(1)} %collective-permute-done.30.refs_2_, f32[16,128]{1,0:T(8,128)S(1)} %collective-permute-done.31.refs_3_, ...), custom_call_target="tpu_custom_call" | custom-call | tf_op jit(solution)/shard_map/place/pallas_call | solution.py:486
  (56 shorter events, 16.7 us)
Async XLA Ops:
  2.6 25.7 %collective-permute-start.1 = (f32[392,256]{1,0:T(8,128)}, f32[392,256]{1,0:T(8,128)S(1)}, u32[]{:S(2)}, u32[]{:S(2)}) collective-permute-start(f32[392,256]{1,0:T(8,128)} %get-tuple-element.31), channel_id=1, source_target_pairs={{0,2},{1,3},{2,0},{3,1},{4,6},{5,7},{6,4},{7,5},{8,10},{9,11},{10,... | collective-permute-start | bytes 1204232 | tf_op jit(solution)/shard_map/ppermute | solution.py:95
  5.6 24.1 %collective-permute-start.2 = (f32[392,256]{1,0:T(8,128)}, f32[392,256]{1,0:T(8,128)S(1)}, u32[]{:S(2)}, u32[]{:S(2)}) collective-permute-start(f32[392,256]{1,0:T(8,128)} %get-tuple-element.31), channel_id=1, source_target_pairs={{0,3},{1,2},{2,1},{3,0},{4,7},{5,6},{6,5},{7,4},{8,11},{9,10},{10,... | collective-permute-start | bytes 1204232 | tf_op jit(solution)/shard_map/ppermute | solution.py:95
  7.1 19.1 %collective-permute-start = (f32[392,256]{1,0:T(8,128)}, f32[392,256]{1,0:T(8,128)S(1)}, u32[]{:S(2)}, u32[]{:S(2)}) collective-permute-start(f32[392,256]{1,0:T(8,128)} %get-tuple-element.30.refs_0_), channel_id=1, source_target_pairs={{0,1},{1,0},{2,3},{3,2},{4,5},{5,4},{6,7},{7,6},{8,9},{9,8},{10,11... | collective-permute-start | bytes 1204232 | tf_op jit(solution)/shard_map/ppermute | solution.py:95
  18.7 14.0 %collective-permute-start.7 = (f32[392,128]{1,0:T(8,128)}, f32[392,128]{1,0:T(8,128)S(1)}, u32[]{:S(2)}, u32[]{:S(2)}) collective-permute-start(f32[392,128]{1,0:T(8,128)} %get-tuple-element.40), channel_id=1, source_target_pairs={{0,1},{1,0},{2,3},{3,2},{4,5},{5,4},{6,7},{7,6},{8,9},{9,8},{10,11... | collective-permute-start | bytes 602120 | tf_op jit(solution)/shard_map/ppermute | solution.py:95
  20.7 17.2 %collective-permute-start.9 = (f32[392,128]{1,0:T(8,128)}, f32[392,128]{1,0:T(8,128)S(1)}, u32[]{:S(2)}, u32[]{:S(2)}) collective-permute-start(f32[392,128]{1,0:T(8,128)} %get-tuple-element.40), channel_id=1, source_target_pairs={{0,3},{1,2},{2,1},{3,0},{4,7},{5,6},{6,5},{7,4},{8,11},{9,10},{10,... | collective-permute-start | bytes 602120 | tf_op jit(solution)/shard_map/ppermute | solution.py:95
  26.1 11.8 %collective-permute-start.8 = (f32[392,128]{1,0:T(8,128)}, f32[392,128]{1,0:T(8,128)S(1)}, u32[]{:S(2)}, u32[]{:S(2)}) collective-permute-start(f32[392,128]{1,0:T(8,128)} %get-tuple-element.32.refs_4_), channel_id=1, source_target_pairs={{0,2},{1,3},{2,0},{3,1},{4,6},{5,7},{6,4},{7,5},{8,10},{9,11},{10,... | collective-permute-start | bytes 602120 | tf_op jit(solution)/shard_map/ppermute | solution.py:95
  28.2 13.9 %collective-permute-start.3 = (f32[392,128]{1,0:T(8,128)}, f32[392,128]{1,0:T(8,128)S(1)}, u32[]{:S(2)}, u32[]{:S(2)}) collective-permute-start(f32[392,128]{1,0:T(8,128)} %get-tuple-element.36), channel_id=1, source_target_pairs={{0,1},{1,0},{2,3},{3,2},{4,5},{5,4},{6,7},{7,6},{8,9},{9,8},{10,11... | collective-permute-start | bytes 602120 | tf_op jit(solution)/shard_map/ppermute | solution.py:95
  29.7 14.5 %collective-permute-start.4 = (f32[392,128]{1,0:T(8,128)}, f32[392,128]{1,0:T(8,128)S(1)}, u32[]{:S(2)}, u32[]{:S(2)}) collective-permute-start(f32[392,128]{1,0:T(8,128)} %get-tuple-element.33.refs_5_), channel_id=1, source_target_pairs={{0,2},{1,3},{2,0},{3,1},{4,6},{5,7},{6,4},{7,5},{8,10},{9,11},{10,... | collective-permute-start | bytes 602120 | tf_op jit(solution)/shard_map/ppermute | solution.py:95
  32.7 11.6 %collective-permute-start.5 = (f32[392,128]{1,0:T(8,128)}, f32[392,128]{1,0:T(8,128)S(1)}, u32[]{:S(2)}, u32[]{:S(2)}) collective-permute-start(f32[392,128]{1,0:T(8,128)} %get-tuple-element.36), channel_id=1, source_target_pairs={{0,3},{1,2},{2,1},{3,0},{4,7},{5,6},{6,5},{7,4},{8,11},{9,10},{10,... | collective-permute-start | bytes 602120 | tf_op jit(solution)/shard_map/ppermute | solution.py:95
  42.0 6.4 %collective-permute-start.10 = (f32[4,288,128]{2,1,0:T(8,128)S(1)}, f32[4,288,128]{2,1,0:T(8,128)S(1)}, u32[]{:S(2)}, u32[]{:S(2)}) collective-permute-start(f32[4,288,128]{2,1,0:T(8,128)S(1)} %get-tuple-element.42), channel_id=1, source_target_pairs={{0,4},{1,5},{2,6},{3,7},{4,0},{5,1},{6,2},{7,3},{8,12},{9,13},{10,... | collective-permute-start | bytes 1769480 | tf_op jit(solution)/shard_map/ppermute | solution.py:95
  48.4 2.1 %collective-permute-start.6 = (f32[4,288,128]{2,1,0:T(8,128)S(1)}, f32[4,288,128]{2,1,0:T(8,128)S(1)}, u32[]{:S(2)}, u32[]{:S(2)}) collective-permute-start(f32[4,288,128]{2,1,0:T(8,128)S(1)} %get-tuple-element.38), channel_id=1, source_target_pairs={{0,4},{1,5},{2,6},{3,7},{4,0},{5,1},{6,2},{7,3},{8,12},{9,13},{10,... | collective-permute-start | bytes 1769480 | tf_op jit(solution)/shard_map/ppermute | solution.py:95
  50.6 1.2 %collective-permute-start.11 = (f32[8,128]{1,0:T(8,128)S(1)}, f32[8,128]{1,0:T(8,128)S(1)}, u32[]{:S(2)}, u32[]{:S(2)}) collective-permute-start(f32[8,128]{1,0:T(8,128)S(1)} %shard_map.40), channel_id=1, source_target_pairs={{0,4},{1,5},{2,6},{3,7},{4,0},{5,1},{6,2},{7,3},{8,12},{9,13},{10,... | collective-permute-start | bytes 12296 | tf_op jit(solution)/shard_map/ppermute | solution.py:95
  51.9 7.9 %collective-permute-start.12 = (f32[8,128]{1,0:T(8,128)S(1)}, f32[8,128]{1,0:T(8,128)S(1)}, u32[]{:S(2)}, u32[]{:S(2)}) collective-permute-start(f32[8,128]{1,0:T(8,128)S(1)} %add.32.refs_1_), channel_id=1, source_target_pairs={{0,1},{1,0},{2,3},{3,2},{4,5},{5,4},{6,7},{7,6},{8,9},{9,8},{10,11... | collective-permute-start | bytes 12296 | tf_op jit(solution)/shard_map/ppermute | solution.py:95
  53.0 6.8 %collective-permute-start.13 = (f32[8,128]{1,0:T(8,128)S(1)}, f32[8,128]{1,0:T(8,128)S(1)}, u32[]{:S(2)}, u32[]{:S(2)}) collective-permute-start(f32[8,128]{1,0:T(8,128)S(1)} %add.32.refs_1_), channel_id=1, source_target_pairs={{0,2},{1,3},{2,0},{3,1},{4,6},{5,7},{6,4},{7,5},{8,10},{9,11},{10,... | collective-permute-start | bytes 12296 | tf_op jit(solution)/shard_map/ppermute | solution.py:95
  54.5 5.2 %collective-permute-start.14 = (f32[8,128]{1,0:T(8,128)S(1)}, f32[8,128]{1,0:T(8,128)S(1)}, u32[]{:S(2)}, u32[]{:S(2)}) collective-permute-start(f32[8,128]{1,0:T(8,128)S(1)} %add.32.refs_1_), channel_id=1, source_target_pairs={{0,3},{1,2},{2,1},{3,0},{4,7},{5,6},{6,5},{7,4},{8,11},{9,10},{10,... | collective-permute-start | bytes 12296 | tf_op jit(solution)/shard_map/ppermute | solution.py:95
  55.4 14.0 %collective-permute-start.23 = (f32[288,128]{1,0:T(8,128)S(1)}, f32[288,128]{1,0:T(8,128)S(1)}, u32[]{:S(2)}, u32[]{:S(2)}) collective-permute-start(f32[288,128]{1,0:T(8,128)S(1)} %get-tuple-element.51), channel_id=1, source_target_pairs={{0,16},{1,20},{2,18},{3,22},{4,24},{5,28},{6,26},{7,30},{8,17},{9,... | collective-permute-start | bytes 442376 | tf_op jit(solution)/shard_map/ppermute | solution.py:95
  57.9 13.7 %collective-permute-start.24 = (f32[288,128]{1,0:T(8,128)S(1)}, f32[288,128]{1,0:T(8,128)S(1)}, u32[]{:S(2)}, u32[]{:S(2)}) collective-permute-start(f32[288,128]{1,0:T(8,128)S(1)} %get-tuple-element.52), channel_id=1, source_target_pairs={{0,24},{1,28},{2,26},{3,30},{4,16},{5,20},{6,18},{7,22},{8,25},{9,... | collective-permute-start | bytes 442376 | tf_op jit(solution)/shard_map/ppermute | solution.py:95
  60.0 16.7 %collective-permute-start.15 = (f32[288,128]{1,0:T(8,128)S(1)}, f32[288,128]{1,0:T(8,128)S(1)}, u32[]{:S(2)}, u32[]{:S(2)}) collective-permute-start(f32[288,128]{1,0:T(8,128)S(1)} %get-tuple-element.43), channel_id=1, source_target_pairs={{0,0},{1,4},{2,2},{3,6},{4,8},{5,12},{6,10},{7,14},{8,1},{9,5},{10... | collective-permute-start | bytes 442376 | tf_op jit(solution)/shard_map/ppermute | solution.py:95
  60.7 16.6 %collective-permute-start.16 = (f32[288,128]{1,0:T(8,128)S(1)}, f32[288,128]{1,0:T(8,128)S(1)}, u32[]{:S(2)}, u32[]{:S(2)}) collective-permute-start(f32[288,128]{1,0:T(8,128)S(1)} %get-tuple-element.44), channel_id=1, source_target_pairs={{0,1},{1,5},{2,3},{3,7},{4,9},{5,13},{6,11},{7,15},{8,0},{9,4},{10... | collective-permute-start | bytes 442376 | tf_op jit(solution)/shard_map/ppermute | solution.py:95
  63.5 8.8 %collective-permute-start.22 = (f32[8,128]{1,0:T(8,128)S(1)}, f32[8,128]{1,0:T(8,128)S(1)}, u32[]{:S(2)}, u32[]{:S(2)}) collective-permute-start(f32[8,128]{1,0:T(8,128)S(1)} %get-tuple-element.50), channel_id=1, source_target_pairs={{0,16},{1,20},{2,18},{3,22},{4,24},{5,28},{6,26},{7,30},{8,17},{9,... | collective-permute-start | bytes 12296 | tf_op jit(solution)/shard_map/ppermute | solution.py:95
  69.4 11.9 %collective-permute-start.17 = (f32[288,128]{1,0:T(8,128)S(1)}, f32[288,128]{1,0:T(8,128)S(1)}, u32[]{:S(2)}, u32[]{:S(2)}) collective-permute-start(f32[288,128]{1,0:T(8,128)S(1)} %get-tuple-element.45), channel_id=1, source_target_pairs={{0,2},{1,6},{2,0},{3,4},{4,10},{5,14},{6,8},{7,12},{8,3},{9,7},{10... | collective-permute-start | bytes 442376 | tf_op jit(solution)/shard_map/ppermute | solution.py:95
  71.6 9.6 %collective-permute-start.18 = (f32[288,128]{1,0:T(8,128)S(1)}, f32[288,128]{1,0:T(8,128)S(1)}, u32[]{:S(2)}, u32[]{:S(2)}) collective-permute-start(f32[288,128]{1,0:T(8,128)S(1)} %get-tuple-element.46), channel_id=1, source_target_pairs={{0,3},{1,7},{2,1},{3,5},{4,11},{5,15},{6,9},{7,13},{8,2},{9,6},{10... | collective-permute-start | bytes 442376 | tf_op jit(solution)/shard_map/ppermute | solution.py:95
  72.3 10.4 %collective-permute-start.19 = (f32[288,128]{1,0:T(8,128)S(1)}, f32[288,128]{1,0:T(8,128)S(1)}, u32[]{:S(2)}, u32[]{:S(2)}) collective-permute-start(f32[288,128]{1,0:T(8,128)S(1)} %get-tuple-element.47), channel_id=1, source_target_pairs={{0,19},{1,23},{2,17},{3,21},{4,27},{5,31},{6,25},{7,29},{8,18},{9,... | collective-permute-start | bytes 442376 | tf_op jit(solution)/shard_map/ppermute | solution.py:95
  76.7 17.7 %collective-permute-start.20 = (f32[288,128]{1,0:T(8,128)S(1)}, f32[288,128]{1,0:T(8,128)S(1)}, u32[]{:S(2)}, u32[]{:S(2)}) collective-permute-start(f32[288,128]{1,0:T(8,128)S(1)} %get-tuple-element.48), channel_id=1, source_target_pairs={{0,18},{1,22},{2,16},{3,20},{4,26},{5,30},{6,24},{7,28},{8,19},{9,... | collective-permute-start | bytes 442376 | tf_op jit(solution)/shard_map/ppermute | solution.py:95
  77.3 17.1 %collective-permute-start.21 = (f32[288,128]{1,0:T(8,128)S(1)}, f32[288,128]{1,0:T(8,128)S(1)}, u32[]{:S(2)}, u32[]{:S(2)}) collective-permute-start(f32[288,128]{1,0:T(8,128)S(1)} %get-tuple-element.49), channel_id=1, source_target_pairs={{0,17},{1,21},{2,19},{3,23},{4,25},{5,29},{6,27},{7,31},{8,16},{9,... | collective-permute-start | bytes 442376 | tf_op jit(solution)/shard_map/ppermute | solution.py:95
  95.3 5.3 %collective-permute-start.26 = (f32[16,128]{1,0:T(8,128)S(1)}, f32[16,128]{1,0:T(8,128)S(1)}, u32[]{:S(2)}, u32[]{:S(2)}) collective-permute-start(f32[16,128]{1,0:T(8,128)S(1)} %get-tuple-element.53), channel_id=1, source_target_pairs={{0,16},{1,17},{2,18},{3,19},{4,20},{5,21},{6,22},{7,23},{8,24},{9,... | collective-permute-start | bytes 24584 | tf_op jit(solution)/shard_map/ppermute | solution.py:95
  99.0 5.4 %collective-permute-start.27 = (f32[16,128]{1,0:T(8,128)S(1)}, f32[16,128]{1,0:T(8,128)S(1)}, u32[]{:S(2)}, u32[]{:S(2)}) collective-permute-start(f32[16,128]{1,0:T(8,128)S(1)} %get-tuple-element.53), channel_id=1, source_target_pairs={{0,24},{1,25},{2,26},{3,27},{4,28},{5,29},{6,30},{7,31},{8,16},{9,... | collective-permute-start | bytes 24584 | tf_op jit(solution)/shard_map/ppermute | solution.py:95
  99.4 5.0 %collective-permute-start.25 = (f32[16,128]{1,0:T(8,128)S(1)}, f32[16,128]{1,0:T(8,128)S(1)}, u32[]{:S(2)}, u32[]{:S(2)}) collective-permute-start(f32[16,128]{1,0:T(8,128)S(1)} %get-tuple-element.53), channel_id=1, source_target_pairs={{0,8},{1,9},{2,10},{3,11},{4,12},{5,13},{6,14},{7,15},{8,0},{9,1},... | collective-permute-start | bytes 24584 | tf_op jit(solution)/shard_map/ppermute | solution.py:95
  104.5 1.2 %collective-permute-start.28 = (f32[16,128]{1,0:T(8,128)S(1)}, f32[16,128]{1,0:T(8,128)S(1)}, u32[]{:S(2)}, u32[]{:S(2)}) collective-permute-start(f32[16,128]{1,0:T(8,128)S(1)} %add_add_fusion), channel_id=1, source_target_pairs={{0,4},{1,5},{2,6},{3,7},{4,0},{5,1},{6,2},{7,3},{8,12},{9,13},{10,... | collective-permute-start | bytes 24584 | tf_op jit(solution)/shard_map/ppermute | solution.py:95
  105.7 3.7 %collective-permute-start.29 = (f32[16,128]{1,0:T(8,128)S(1)}, f32[16,128]{1,0:T(8,128)S(1)}, u32[]{:S(2)}, u32[]{:S(2)}) collective-permute-start(f32[16,128]{1,0:T(8,128)S(1)} %add.36.refs_0_), channel_id=1, source_target_pairs={{0,1},{1,0},{2,3},{3,2},{4,5},{5,4},{6,7},{7,6},{8,9},{9,8},{10,11... | collective-permute-start | bytes 24584 | tf_op jit(solution)/shard_map/ppermute | solution.py:95
  107.5 3.7 %collective-permute-start.30 = (f32[16,128]{1,0:T(8,128)S(1)}, f32[16,128]{1,0:T(8,128)S(1)}, u32[]{:S(2)}, u32[]{:S(2)}) collective-permute-start(f32[16,128]{1,0:T(8,128)S(1)} %add.36.refs_0_), channel_id=1, source_target_pairs={{0,2},{1,3},{2,0},{3,1},{4,6},{5,7},{6,4},{7,5},{8,10},{9,11},{10,... | collective-permute-start | bytes 24584 | tf_op jit(solution)/shard_map/ppermute | solution.py:95
  108.2 4.5 %collective-permute-start.31 = (f32[16,128]{1,0:T(8,128)S(1)}, f32[16,128]{1,0:T(8,128)S(1)}, u32[]{:S(2)}, u32[]{:S(2)}) collective-permute-start(f32[16,128]{1,0:T(8,128)S(1)} %add.36.refs_0_), channel_id=1, source_target_pairs={{0,3},{1,2},{2,1},{3,0},{4,7},{5,6},{6,5},{7,4},{8,11},{9,10},{10,... | collective-permute-start | bytes 24584 | tf_op jit(solution)/shard_map/ppermute | solution.py:95
  (3 other events, 24.3 us)
